TPU v7x, 512 devices: a whole 4x4x16 slice. The times are simulated.
512 devices in a mesh: obs: 16 (over y, x), space: 32 (over z, core).
Axes of the slice: x: 4, y: 4, z: 16, core: 2. Of those that a mesh axis runs over, the one named last changes fastest.
Arguments:
- probes: float32 [32, 4, 512, 256], P(None, None, 'space'), may hold values from -6 to 6
- wind: float32 [16, 2, 2, 4, 512, 256], P('obs', None, None, None, 'space'), may hold values from -0.6 to 0.6
- station_cell: int32 [16, 8192], P('obs', 'space'), may hold values from 0 to 16383
- obs_count: int32 [16, 32], P('obs', 'space'), may hold values from 1 to 256, as said below
- obs_weight: float32 [16, 8192], P('obs', 'space'), may hold values from 0.5 to 4
Outputs:
- basis: float32 [32, 4, 512, 256], P('obs', None, 'space')
- core: float32 [32, 32], replicated
Inputs may be any that keep to these rules, and one draw needn't show every extreme that they name: `obs_count`: the live slots of a tile in a window are its first ones; some tile of some window has all 256 live.
All inputs are finite; a program needn't handle non-finite values.
Results may differ from a plain program's by a relative error of at most 0.0003.
Values sent between devices are 32-bit elements; how exact they have to be, the bound alone decides.
No kernel may reach another device: no remote copies, remote signals or barrier semaphores. Data moves between devices by JAX's collectives and lax.ppermute only.
A program may use at most 64 MiB of HBM per device.

v0:
```python
import math

import jax
import jax.numpy as jnp
from jax import lax
from jax.sharding import Mesh
from jax.sharding import PartitionSpec as P

SPACE = ("space_0", "space_1")
OBS = ("obs_0", "obs_1")


def extended_2(block, sides, width):
    for axis, dim in sides:
        count = lax.axis_size(axis)
        forward = [(i, i + 1) for i in range(count - 1)]
        backward = [(target, source) for source, target in forward]
        low = lax.ppermute(
            lax.slice_in_dim(block, block.shape[dim] - width, None, axis=dim), axis, forward
        )
        high = lax.ppermute(lax.slice_in_dim(block, 0, width, axis=dim), axis, backward)
        block = jnp.concatenate([low, block, high], axis=dim)
    return block


def cut_along(shard, dim, peers):
    dims = shard.shape
    blocks = shard.reshape(*dims[:dim], peers, dims[dim] // peers, *dims[dim + 1 :])
    return jnp.moveaxis(blocks, dim, 0)


def sent_and_summed(shard, axis, dim):
    peers = lax.axis_size(axis)
    blocks = lax.all_to_all(cut_along(shard, dim, peers), axis, 0, 0, tiled=True)
    return jnp.sum(blocks, axis=0)


def copy_for_each(shard, axis):
    copies = jnp.broadcast_to(shard, (lax.axis_size(axis), *shard.shape))
    return lax.all_to_all(copies, axis, split_axis=0, concat_axis=0, tiled=True)


def over_copies(shard, axis):
    everything = copy_for_each(shard, axis)
    return jnp.sum(everything, axis=0)


def over_axes(shard, axes):
    far, near = axes
    return over_copies(over_copies(shard, near), far)


def together(arrays, axis):
    ends = [0]
    for a in arrays:
        ends.append(ends[-1] + a.size)
    subtotal = over_axes(jnp.concatenate([a.ravel() for a in arrays]), axis)
    return tuple((subtotal[b:e].reshape(a.shape) for a, b, e in zip(arrays, ends, ends[1:])))


def smooth_terms(centre, upper, lower):
    yplus = jnp.pad(centre, [(0, 0), (0, 0), (0, 0), (0, 1)])[:, :, :, 1:]
    yminus = jnp.pad(centre, [(0, 0), (0, 0), (0, 0), (1, 0)])[:, :, :, :-1]
    zplus = jnp.pad(centre, [(0, 0), (0, 1), (0, 0), (0, 0)])[:, 1:]
    zminus = jnp.pad(centre, [(0, 0), (1, 0), (0, 0), (0, 0)])[:, :-1]
    return (
        centre
        + 0.15 * (upper + lower + yplus + yminus - 4.0 * centre)
        + 0.1 * (zplus + zminus - 2.0 * centre),
        yplus,
        yminus,
    )


def forward_advance(extended, wind_x, wind_y):
    centre = extended[:, :, 1:-1]
    upper = extended[:, :, 2:]
    lower = extended[:, :, :-2]
    result, yplus, yminus = smooth_terms(centre, upper, lower)
    return result - 0.5 * (wind_x * (upper - lower) + wind_y * (yplus - yminus))


def adjoint_advance(extended, wind_x_ext, wind_y):
    centre = extended[:, :, 1:-1]
    upper = extended[:, :, 2:]
    lower = extended[:, :, :-2]
    result, yplus, yminus = smooth_terms(centre, upper, lower)
    carried = wind_x_ext * extended
    across = wind_y * centre
    aplus = jnp.pad(across, [(0, 0), (0, 0), (0, 0), (0, 1)])[:, :, :, 1:]
    aminus = jnp.pad(across, [(0, 0), (0, 0), (0, 0), (1, 0)])[:, :, :, :-1]
    return result + 0.5 * (carried[:, :, 2:] - carried[:, :, :-2] + (aplus - aminus))


def on_device(probes, wind, station_cell, obs_count, obs_weight):
    probe_count, levels, local_rows, columns = probes.shape
    steps = wind.shape[1]
    total_rows = local_rows * lax.axis_size(SPACE)
    winds = wind[0]
    depth = 1
    wind_ext = extended_2(winds, ((SPACE, 3),), depth)
    field = probes
    for step in range(steps):
        extended = extended_2(field, ((SPACE, 2),), 1)
        field = forward_advance(
            extended,
            wind_ext[step, 0, :, 1 : 1 + local_rows],
            wind_ext[step, 1, :, 1 : 1 + local_rows],
        )
    slots = station_cell.shape[1]
    cells = station_cell[0]
    live = (lax.iota(jnp.int32, slots) < obs_count[0, 0]).astype(jnp.float32)
    flat = field.reshape(probe_count, -1)
    sampled = flat[:, cells]
    weighted = sampled * (obs_weight[0] * live)[None, :]
    injected = jnp.zeros_like(flat).at[:, cells].add(weighted).reshape(probes.shape)
    adjoint_field = injected
    for step in reversed(range(steps)):
        extended = extended_2(adjoint_field, ((SPACE, 2),), 1)
        adjoint_field = adjoint_advance(
            extended,
            wind_ext[step, 0, :, 0 : local_rows + 2],
            wind_ext[step, 1, :, 1 : 1 + local_rows],
        )
    local_sketch = adjoint_field.reshape(probe_count, -1)
    omega = probes.reshape(probe_count, -1)
    divisor = lax.axis_size(OBS) * lax.axis_size(SPACE) * slots
    scale = math.sqrt(levels * total_rows * columns)
    rows_each = probe_count // lax.axis_size(OBS)
    share = sent_and_summed(local_sketch, OBS, 1)
    share_width = share.shape[1]
    omega_share = lax.dynamic_slice_in_dim(omega, lax.axis_index(OBS) * share_width, share_width, 1)
    gram_part = jnp.dot(share, share.T, precision=lax.Precision.HIGHEST)
    cross_part = jnp.dot(omega_share, share.T, precision=lax.Precision.HIGHEST)
    gram, cross = together((gram_part, cross_part), (("obs_0", "obs_1"), ("space_0", "space_1")))
    lower = jnp.linalg.cholesky(gram)
    basis_share = jax.scipy.linalg.solve_triangular(lower, share, lower=True) * scale
    basis = lax.all_to_all(basis_share, OBS, split_axis=0, concat_axis=1, tiled=True)
    core = cross / divisor
    return (basis.reshape(rows_each, levels, local_rows, columns), core)


def solution(mesh):
    split = Mesh(mesh.devices.reshape(4, 4, 16, 2), ("obs_0", "obs_1", "space_0", "space_1"))
    in_specs = (
        P(None, None, SPACE, None),
        P(OBS, None, None, None, SPACE, None),
        P(OBS, SPACE),
        P(OBS, SPACE),
        P(OBS, SPACE),
    )
    out_specs = (P(OBS, None, SPACE, None), P())
    return jax.shard_map(
        on_device, mesh=split, in_specs=in_specs, out_specs=out_specs, check_vma=False
    )
```

profile of v0, /device:TPU:2, one launch (start us, length us, event | category | flops | bytes accessed | tf_op | source)
XLA Modules:
  0.0 185.7 jit_solution(13124052681833476974)
XLA Ops:
  0.7 2.8 %copy.131 = f32[32,4,16,256]{3,0,2,1:T(8,128)S(1)} copy(f32[32,4,16,256]{3,2,1,0:T(8,128)} %param.5) | data formatting | bytes 4194304 | tf_op args[0]
  4.8 3.0 %collective-permute-start.1 = (f32[32,4,1,256]{3,0,2,1:T(8,128)S(1)}, f32[32,4,1,256]{3,0,2,1:T(8,128)S(1)}, u32[]{:S(2)}, u32[]{:S(2)}) collective-permute-start(f32[32,4,1,256]{3,0,2,1:T(8,128)S(1)} %get-tuple-element.10), channel_id=1, source_target_pairs={{0,1},{1,2},{2,3},{3,4},{4,5},{5,6},{6,7},{7,8},{8,9},{9,10},{10,1... | collective-permute-start | bytes 393224 | tf_op jit(solution)/shard_map/ppermute | solution.py:18
  7.9 3.4 %collective-permute-start.6 = (f32[2,2,4,1,256]{4,3,2,1,0:T(1,128)S(1)}, f32[2,2,4,1,256]{4,3,2,1,0:T(1,128)S(1)}, u32[]{:S(2)}, u32[]{:S(2)}) collective-permute-start(f32[2,2,4,1,256]{4,3,2,1,0:T(1,128)S(1)} %get-tuple-element.14), channel_id=1, source_target_pairs={{0,1},{1,2},{2,3},{3,4},{4,5},{5,6},{6,7},{7,8},{8,9},{9,10},{10,1... | collective-permute-start | bytes 49160 | tf_op jit(solution)/shard_map/ppermute | solution.py:18
  13.4 2.5 %fusion.6 = f32[32,4,16,256]{3,0,2,1:T(8,128)S(1)} fusion(f32[32,4,16,256]{3,0,2,1:T(8,128)S(1)} %copy.131, f32[32,4,1,256]{3,0,2,1:T(8,128)S(1)} %collective-permute-done, f32[32,4,1,256]{3,0,2,1:T(8,128)S(1)} %collective-permute-done.1, f32[4,16,256]{2,1,0:T(8,128)S(1)} %get-tuple-element.18, f32[4,16,256]{2,1,0:T(8,128)S(1)} %get-tuple-element.19), kind=kLoop, calls=%fused_computation.30 | loop fusion | flops 11010048 | bytes 4587520 | tf_op jit(solution)/shard_map/sub | solution.py:80
  17.2 3.7 %collective-permute-start.3 = (f32[32,4,1,256]{3,0,2,1:T(8,128)S(1)}, f32[32,4,1,256]{3,0,2,1:T(8,128)S(1)}, u32[]{:S(2)}, u32[]{:S(2)}) collective-permute-start(f32[32,4,1,256]{3,0,2,1:T(8,128)S(1)} %get-tuple-element.8), channel_id=1, source_target_pairs={{0,1},{1,2},{2,3},{3,4},{4,5},{5,6},{6,7},{7,8},{8,9},{9,10},{10,1... | collective-permute-start | bytes 393224 | tf_op jit(solution)/shard_map/ppermute | solution.py:18
  21.9 2.5 %fusion.11 = f32[32,4,16,256]{3,0,2,1:T(8,128)S(1)} fusion(f32[32,4,16,256]{3,0,2,1:T(8,128)S(1)} %fusion.6, f32[32,4,1,256]{3,0,2,1:T(8,128)S(1)} %collective-permute-done.2, f32[32,4,1,256]{3,0,2,1:T(8,128)S(1)} %collective-permute-done.3, f32[4,16,256]{2,1,0:T(8,128)S(1)} %get-tuple-element.17, f32[4,16,256]{2,1,0:T(8,128)S(1)} %get-tuple-element.16), kind=kLoop, calls=%fused_computation.35 | loop fusion | flops 11010048 | bytes 4587520 | tf_op jit(solution)/shard_map/sub | solution.py:80
  24.3 4.7 %copy.135 = f32[32,4,16,256]{0,3,2,1:T(8,128)} copy(f32[32,4,16,256]{3,0,2,1:T(8,128)S(1)} %fusion.11) | data formatting | bytes 4194304 | tf_op jit(solution)/shard_map/sub | solution.py:80
  29.0 7.0 %scatter_custom_fusion = f32[32,16384]{0,1:T(8,128)} fusion(s32[256]{0:T(256)S(1)} %bitcast.52, f32[]{:T(128)} %constant.64.clone.1, f32[256]{0:T(256)S(1)} %bitcast.50, f32[32,16384]{0,1:T(8,128)} %bitcast.41, s32[1024]{0:T(1024)S(1)} %pad_clamp_fusion), kind=kCustom, calls=%fused_computation.2 | custom fusion | flops 16384 | bytes 4199428 | tf_op jit(solution)/shard_map/scatter-add | solution.py:116
  36.0 5.1 %copy.143 = f32[32,4,16,256]{3,0,2,1:T(8,128)S(1)} copy(f32[32,4,16,256]{0,3,2,1:T(8,128)} %bitcast.42) | data formatting | bytes 4194304 | tf_op jit(solution)/shard_map/reshape | solution.py:116
  42.5 5.2 %collective-permute-start.5 = (f32[32,4,1,256]{3,0,2,1:T(8,128)S(1)}, f32[32,4,1,256]{3,0,2,1:T(8,128)S(1)}, u32[]{:S(2)}, u32[]{:S(2)}) collective-permute-start(f32[32,4,1,256]{3,0,2,1:T(8,128)S(1)} %get-tuple-element.6), channel_id=1, source_target_pairs={{0,1},{1,2},{2,3},{3,4},{4,5},{5,6},{6,7},{7,8},{8,9},{9,10},{10,1... | collective-permute-start | bytes 393224 | tf_op jit(solution)/shard_map/ppermute | solution.py:18
  49.0 3.0 %broadcast_multiply_fusion.1 = (f32[32,4,16,256]{3,0,2,1:T(8,128)S(1)}, f32[32,4,16,256]{3,0,2,1:T(8,128)S(1)}) fusion(f32[4,16,256]{2,1,0:T(8,128)S(1)} %get-tuple-element.18, f32[32,4,16,256]{3,0,2,1:T(8,128)S(1)} %broadcast_multiply_fusion, f32[32,4,18,256]{3,0,2,1:T(8,128)S(1)} %maximum_multiply_fusion, f32[32,4,16,256]{3,0,2,1:T(8,128)S(1)} %copy.143, ...), kind=kLoop, calls=%fused_computation.76 | loop fusion | flops 10485760 | bytes 12910592 | tf_op jit(solution)/shard_map/mul | solution.py:89
  53.3 6.1 %collective-permute-start.9 = (f32[32,4,1,256]{3,0,2,1:T(8,128)S(1)}, f32[32,4,1,256]{3,0,2,1:T(8,128)S(1)}, u32[]{:S(2)}, u32[]{:S(2)}) collective-permute-start(f32[32,4,1,256]{3,0,2,1:T(8,128)S(1)} %get-tuple-element.4), channel_id=1, source_target_pairs={{0,1},{1,2},{2,3},{3,4},{4,5},{5,6},{6,7},{7,8},{8,9},{9,10},{10,1... | collective-permute-start | bytes 393224 | tf_op jit(solution)/shard_map/ppermute | solution.py:18
  60.6 3.0 %fusion.21 = f32[32,4,16,256]{3,0,2,1:T(8,128)S(1)} fusion(f32[32,4,16,256]{3,0,2,1:T(8,128)S(1)} %get-tuple-element.3, f32[32,4,16,256]{3,0,2,1:T(8,128)S(1)} %get-tuple-element.2, f32[32,4,18,256]{3,0,2,1:T(8,128)S(1)} %maximum_multiply_fusion.1, f32[32,4,1,256]{3,0,2,1:T(8,128)S(1)} %collective-permute-done.9, f32[32,4,1,256]{3,0,2,1:T(8,128)S(1)} %collective-permute-done.8), kind=kLoop, calls=%fused_computation.45 | loop fusion | flops 9961472 | bytes 10747904 | tf_op jit(solution)/shard_map/add | solution.py:92
  66.4 4.1 %copy.150 = f32[16,32,1024]{2,1,0:T(8,128)} copy(f32[16,32,1024]{2,0,1:T(8,128)} %bitcast.44) | data formatting | bytes 4194304 | tf_op jit(solution)/shard_map/transpose | solution.py:29
  70.6 8.6 %all-to-all-start = ((f32[16,32,1024]{2,1,0:T(8,128)}), f32[16,32,1024]{2,1,0:T(8,128)}, u32[]{:S(2)}, u32[]{:S(2)}) async-start(f32[16,32,1024]{2,1,0:T(8,128)} %copy.150), calls=%async_computation | async-start | bytes 4194304 | tf_op jit(solution)/shard_map/all_to_all | solution.py:34
  79.2 2.5 %copy.159 = f32[4,8,64,256]{3,1,2,0:T(8,128)} copy(f32[4,8,64,256]{3,2,1,0:T(8,128)S(1)} %bitcast.43) | data formatting | bytes 4194304
  81.8 25.0 %all-to-all-done = f32[16,32,1024]{2,1,0:T(8,128)} async-done(((f32[16,32,1024]{2,1,0:T(8,128)}), f32[16,32,1024]{2,1,0:T(8,128)}, u32[]{:S(2)}, u32[]{:S(2)}) %all-to-all-start) | async-done | bytes 2097184 | tf_op jit(solution)/shard_map/all_to_all | solution.py:34
  106.7 1.7 reduce_sum.27
  110.2 43.0 %all_to_all.33 = f32[32,1,2048]{2,1,0:T(1,128)S(1)} all-to-all(f32[32,1,2048]{2,1,0:T(1,128)S(1)} %broadcast_in_dim.15), channel_id=1, replica_groups=mesh['obs_0'=4,'obs_1'=4,'space_0'=16,'space_1'=2] {'space_0','space_1'}, dimensions={0} | all-to-all | bytes 524288 | tf_op jit(solution)/shard_map/all_to_all | solution.py:40
  153.4 12.0 %all_to_all.34 = f32[16,1,2048]{2,1,0:T(1,128)S(1)} all-to-all(f32[16,1,2048]{2,1,0:T(1,128)S(1)} %broadcast_in_dim.16), channel_id=1, replica_groups=mesh['obs_0'=4,'obs_1'=4,'space_0'=16,'space_1'=2] {'obs_0','obs_1'}, dimensions={0} | all-to-all | bytes 262144 | tf_op jit(solution)/shard_map/all_to_all | solution.py:40
  165.7 2.9 %cholesky.16 = f32[32,32]{1,0:T(8,128)S(1)} custom-call(f32[32,32]{1,0:T(8,128)S(1)} %fusion.47), custom_call_target="Cholesky" | custom-call | tf_op jit(solution)/shard_map/jit(cholesky)/cholesky | solution.py:136
  169.9 2.4 %custom-call.7 = f32[1,32,32]{1,2,0:T(8,128)S(1)} custom-call(f32[1,32,32]{2,1,0:T(8,128)S(1)} %fusion.45), custom_call_target="InvertDiagBlocksLowerTriangular" | custom-call | tf_op jit(solution)/shard_map/jit(_solve_triangular)/triangular_solve | solution.py:137
  173.4 4.8 %all-to-all-start.3 = ((f32[16,2,1024]{2,1,0:T(2,128)}), f32[16,2,1024]{2,1,0:T(2,128)S(1)}, u32[]{:S(2)}, u32[]{:S(2)}) async-start(f32[16,2,1024]{2,1,0:T(2,128)} %all_to_all.26), calls=%async_computation.3 | async-start | bytes 262144 | tf_op jit(solution)/shard_map/all_to_all | solution.py:138
  178.9 6.0 %all-to-all-done.3 = f32[16,2,1024]{2,1,0:T(2,128)S(1)} async-done(((f32[16,2,1024]{2,1,0:T(2,128)}), f32[16,2,1024]{2,1,0:T(2,128)S(1)}, u32[]{:S(2)}, u32[]{:S(2)}) %all-to-all-start.3) | async-done | bytes 131104 | tf_op jit(solution)/shard_map/all_to_all | solution.py:138
  (59 shorter events, 18.7 us)
Async XLA Ops:
  0.6 7.3 %copy-start.1 = (f32[1,2,2,4,16,256]{5,4,3,2,1,0:T(8,128)S(1)}, f32[1,2,2,4,16,256]{5,4,3,2,1,0:T(8,128)}, u32[]{:S(2)}) copy-start(f32[1,2,2,4,16,256]{5,4,3,2,1,0:T(8,128)} %param.6) | copy-start | bytes 786436
  0.6 12.1 %copy-start.2 = (s32[1,256]{1,0:T(1,128)S(1)}, s32[1,256]{1,0:T(1,128)}, u32[]{:S(2)}) copy-start(s32[1,256]{1,0:T(1,128)} %param.7) | copy-start | bytes 3076
  0.7 12.7 %copy-start.3 = (f32[1,256]{1,0:T(1,128)S(1)}, f32[1,256]{1,0:T(1,128)}, u32[]{:S(2)}) copy-start(f32[1,256]{1,0:T(1,128)} %param.9) | copy-start | bytes 3076
  3.5 9.9 %collective-permute-start = (f32[32,4,1,256]{3,0,2,1:T(8,128)S(1)}, f32[32,4,1,256]{3,0,2,1:T(8,128)S(1)}, u32[]{:S(2)}, u32[]{:S(2)}) collective-permute-start(f32[32,4,1,256]{3,0,2,1:T(8,128)S(1)} %get-tuple-element.11), channel_id=1, source_target_pairs={{1,0},{2,1},{3,2},{4,3},{5,4},{6,5},{7,6},{8,7},{9,8},{10,9},{11,1... | collective-permute-start | bytes 393224 | tf_op jit(solution)/shard_map/ppermute | solution.py:21
  4.8 8.6 %collective-permute-start.1 = (f32[32,4,1,256]{3,0,2,1:T(8,128)S(1)}, f32[32,4,1,256]{3,0,2,1:T(8,128)S(1)}, u32[]{:S(2)}, u32[]{:S(2)}) collective-permute-start(f32[32,4,1,256]{3,0,2,1:T(8,128)S(1)} %get-tuple-element.10), channel_id=1, source_target_pairs={{0,1},{1,2},{2,3},{3,4},{4,5},{5,6},{6,7},{7,8},{8,9},{9,10},{10,1... | collective-permute-start | bytes 393224 | tf_op jit(solution)/shard_map/ppermute | solution.py:18
  7.9 13.0 %collective-permute-start.6 = (f32[2,2,4,1,256]{4,3,2,1,0:T(1,128)S(1)}, f32[2,2,4,1,256]{4,3,2,1,0:T(1,128)S(1)}, u32[]{:S(2)}, u32[]{:S(2)}) collective-permute-start(f32[2,2,4,1,256]{4,3,2,1,0:T(1,128)S(1)} %get-tuple-element.14), channel_id=1, source_target_pairs={{0,1},{1,2},{2,3},{3,4},{4,5},{5,6},{6,7},{7,8},{8,9},{9,10},{10,1... | collective-permute-start | bytes 49160 | tf_op jit(solution)/shard_map/ppermute | solution.py:18
  11.4 9.6 %collective-permute-start.7 = (f32[2,2,4,1,256]{4,3,2,1,0:T(1,128)S(1)}, f32[2,2,4,1,256]{4,3,2,1,0:T(1,128)S(1)}, u32[]{:S(2)}, u32[]{:S(2)}) collective-permute-start(f32[2,2,4,1,256]{4,3,2,1,0:T(1,128)S(1)} %get-tuple-element.15), channel_id=1, source_target_pairs={{1,0},{2,1},{3,2},{4,3},{5,4},{6,5},{7,6},{8,7},{9,8},{10,9},{11,1... | collective-permute-start | bytes 49160 | tf_op jit(solution)/shard_map/ppermute | solution.py:21
  15.9 5.1 %collective-permute-start.2 = (f32[32,4,1,256]{3,0,2,1:T(8,128)S(1)}, f32[32,4,1,256]{3,0,2,1:T(8,128)S(1)}, u32[]{:S(2)}, u32[]{:S(2)}) collective-permute-start(f32[32,4,1,256]{3,0,2,1:T(8,128)S(1)} %get-tuple-element.9), channel_id=1, source_target_pairs={{1,0},{2,1},{3,2},{4,3},{5,4},{6,5},{7,6},{8,7},{9,8},{10,9},{11,1... | collective-permute-start | bytes 393224 | tf_op jit(solution)/shard_map/ppermute | solution.py:21
  17.2 4.6 %collective-permute-start.3 = (f32[32,4,1,256]{3,0,2,1:T(8,128)S(1)}, f32[32,4,1,256]{3,0,2,1:T(8,128)S(1)}, u32[]{:S(2)}, u32[]{:S(2)}) collective-permute-start(f32[32,4,1,256]{3,0,2,1:T(8,128)S(1)} %get-tuple-element.8), channel_id=1, source_target_pairs={{0,1},{1,2},{2,3},{3,4},{4,5},{5,6},{6,7},{7,8},{8,9},{9,10},{10,1... | collective-permute-start | bytes 393224 | tf_op jit(solution)/shard_map/ppermute | solution.py:18
  41.2 6.8 %collective-permute-start.4 = (f32[32,4,1,256]{3,0,2,1:T(8,128)S(1)}, f32[32,4,1,256]{3,0,2,1:T(8,128)S(1)}, u32[]{:S(2)}, u32[]{:S(2)}) collective-permute-start(f32[32,4,1,256]{3,0,2,1:T(8,128)S(1)} %get-tuple-element.7), channel_id=1, source_target_pairs={{1,0},{2,1},{3,2},{4,3},{5,4},{6,5},{7,6},{8,7},{9,8},{10,9},{11,1... | collective-permute-start | bytes 393224 | tf_op jit(solution)/shard_map/ppermute | solution.py:21
  42.5 6.2 %collective-permute-start.5 = (f32[32,4,1,256]{3,0,2,1:T(8,128)S(1)}, f32[32,4,1,256]{3,0,2,1:T(8,128)S(1)}, u32[]{:S(2)}, u32[]{:S(2)}) collective-permute-start(f32[32,4,1,256]{3,0,2,1:T(8,128)S(1)} %get-tuple-element.6), channel_id=1, source_target_pairs={{0,1},{1,2},{2,3},{3,4},{4,5},{5,6},{6,7},{7,8},{8,9},{9,10},{10,1... | collective-permute-start | bytes 393224 | tf_op jit(solution)/shard_map/ppermute | solution.py:18
  52.0 7.4 %collective-permute-start.8 = (f32[32,4,1,256]{3,0,2,1:T(8,128)S(1)}, f32[32,4,1,256]{3,0,2,1:T(8,128)S(1)}, u32[]{:S(2)}, u32[]{:S(2)}) collective-permute-start(f32[32,4,1,256]{3,0,2,1:T(8,128)S(1)} %get-tuple-element.5), channel_id=1, source_target_pairs={{1,0},{2,1},{3,2},{4,3},{5,4},{6,5},{7,6},{8,7},{9,8},{10,9},{11,1... | collective-permute-start | bytes 393224 | tf_op jit(solution)/shard_map/ppermute | solution.py:21
  53.3 6.9 %collective-permute-start.9 = (f32[32,4,1,256]{3,0,2,1:T(8,128)S(1)}, f32[32,4,1,256]{3,0,2,1:T(8,128)S(1)}, u32[]{:S(2)}, u32[]{:S(2)}) collective-permute-start(f32[32,4,1,256]{3,0,2,1:T(8,128)S(1)} %get-tuple-element.4), channel_id=1, source_target_pairs={{0,1},{1,2},{2,3},{3,4},{4,5},{5,6},{6,7},{7,8},{8,9},{9,10},{10,1... | collective-permute-start | bytes 393224 | tf_op jit(solution)/shard_map/ppermute | solution.py:18
  70.6 8.6 %copy-start = (f32[32,4,16,256]{3,2,1,0:T(8,128)S(1)}, f32[32,4,16,256]{3,2,1,0:T(8,128)}, u32[]{:S(2)}) copy-start(f32[32,4,16,256]{3,2,1,0:T(8,128)} %param.5) | copy-start | bytes 6291460
  70.6 36.1 %all-to-all-start = ((f32[16,32,1024]{2,1,0:T(8,128)}), f32[16,32,1024]{2,1,0:T(8,128)}, u32[]{:S(2)}, u32[]{:S(2)}) async-start(f32[16,32,1024]{2,1,0:T(8,128)} %copy.150), calls=%async_computation | async-start | bytes 4194304 | tf_op jit(solution)/shard_map/all_to_all | solution.py:34
  173.4 11.5 %all-to-all-start.3 = ((f32[16,2,1024]{2,1,0:T(2,128)}), f32[16,2,1024]{2,1,0:T(2,128)S(1)}, u32[]{:S(2)}, u32[]{:S(2)}) async-start(f32[16,2,1024]{2,1,0:T(2,128)} %all_to_all.26), calls=%async_computation.3 | async-start | bytes 262144 | tf_op jit(solution)/shard_map/all_to_all | solution.py:138
where the time goes:
time: 186 us
  blocking collectives  55 us (30%)
  starting transfers between devices  41.4 us (22%)
  waiting for transfers between devices  33.3 us (18%)
  other arithmetic  27.6 us (15%)
  local copies, waits for them, and re-layouts  24.9 us (13%)
    all_to_all x2, blocking collectives, copy_for_each(): return lax.all_to_all(copies, axis, split_axis=0, concat_axis=0, tiled=True)  55 us
    all_to_all x1, waiting for transfers between devices, sent_and_summed(): lax.all_to_all(cut_along(shard, dim, peers), axis, 0, 0, tiled=True)  25 us
    ppermute x5, starting transfers between devices, extended_2(): lax.ppermute(lax.slice_in_dim(block, block.shape[dim] - width, None, axis...  21.5 us
    all_to_all x1, starting transfers between devices, sent_and_summed(): lax.all_to_all(cut_along(shard, dim, peers), axis, 0, 0, tiled=True)  8.63 us
    scatter-add x1, other arithmetic, on_device(): jnp.zeros_like(flat).at[:, cells].add(weighted).reshape(probes.shape)  7.02 us
    ppermute x5, starting transfers between devices, extended_2(): lax.ppermute(lax.slice_in_dim(block, 0, width, axis=dim), axis, backward)  6.46 us
    all_to_all x1, waiting for transfers between devices, on_device(): lax.all_to_all(basis_share, OBS, split_axis=0, concat_axis=1, tiled=True)  6.04 us
    unnamed x10, local copies, waits for them, and re-layouts  5.4 us
  transfers between devices with their start and end apart: 12, of which 5 were waited for; matrix products, arithmetic and copies ran while one was open for 3% of the time, Pallas kernels for 0%

commit v1 on v0

v1 whole, which is shorter than its diff:
```python
import math

import jax
import jax.numpy as jnp
from jax import lax
from jax.experimental import pallas as pl
from jax.experimental.pallas import tpu as pltpu
from jax.sharding import PartitionSpec as P

F32 = jnp.float32
HIGH = lax.Precision.HIGHEST
VM = pl.BlockSpec(memory_space=pltpu.VMEM)
SM = pl.BlockSpec(memory_space=pltpu.SMEM)
NT = (((1,), (1,)), ((), ()))

NP, LV, RX, NY = 32, 4, 16, 256
HALO = 4
ROWS = RX + 2 * HALO
LANES = 128
BLK = LV * NP
LINE = 2 * BLK
STRIDE = LV * RX * 2
AUX = HALO * LINE
SIDE = 56
MSG = AUX + 2 * SIDE


def iota(shape, dim):
    return lax.broadcasted_iota(jnp.int32, shape, dim)


def live_weights(weight_ref, count_ref):
    w = weight_ref[...]
    return jnp.where(iota(w.shape, 1) < count_ref[0, 0], w, 0.0)


def arrived(probes, x, h, l):
    first = ((l * 2 + x // 8) * 2 + h) * 8 + x % 8
    return probes[pl.ds(first, NP, stride=STRIDE), :]


def pack_kernel(probes, wind, cells, weight, count, up, down):
    cell_row = cells[...].astype(F32)
    live = live_weights(weight, count)
    for out, first in ((up, RX - HALO), (down, 0)):
        for xh in range(HALO):
            for h in range(2):
                for l in range(LV):
                    out[pl.ds(((xh * 2 + h) * LV + l) * NP, NP), :] = arrived(
                        probes, first + xh, h, l
                    )
        wfirst = RX - 3 if first else 0
        for h in range(2):
            at, cols = AUX + h * SIDE, pl.ds(h * LANES, LANES)
            for i in range(16):
                out[pl.ds(at + 3 * i, 3), :] = wind[pl.ds(i * RX + wfirst, 3), cols]
            out[pl.ds(at + 48, 1), :] = cell_row[:, h * LANES : (h + 1) * LANES]
            out[pl.ds(at + 49, 1), :] = live[:, h * LANES : (h + 1) * LANES]
            out[pl.ds(at + 50, 6), :] = jnp.zeros((6, LANES), F32)


def weight_map(cell_row, live):
    cell = cell_row.astype(jnp.int32)
    row, col = cell // NY, cell % NY
    nslot = cell.shape[1]
    on_col = (iota((NY, nslot), 0) == col).astype(jnp.bfloat16)
    on_row = iota((LV * RX, nslot), 0) == row
    total = jnp.zeros((LV * RX, NY), F32)
    rest = live
    for _ in range(3):
        part = rest.astype(jnp.bfloat16).astype(F32)
        rest = rest - part
        lhs = jnp.where(on_row, part, 0.0).astype(jnp.bfloat16)
        total += lax.dot_general(lhs, on_col, NT, preferred_element_type=F32)
    return total


def at(x, h, l):
    return pl.ds(pl.multiple_of(x * LINE + (h * LV + l) * NP, NP), NP)


def level_sum(c, l):
    if l == 0:
        return c[1]
    if l == LV - 1:
        return c[l - 1]
    return c[l - 1] + c[l + 1]


def slot_row(msg, r):
    return jnp.concatenate([msg[pl.ds(AUX + h * SIDE + r, 1), :] for h in range(2)], axis=1)


def tile_kernel(probes, wind, cells, weight, count, place, low, high, out, u, v, coef, wmap, ext):
    t, last = place[0, 0], place[0, 1] - 1
    lane = iota((NP, LANES), 1)
    first_lane, last_lane = lane == 0, lane == LANES - 1
    col = iota((ROWS, LANES), 1)
    for h in range(2):
        cols = pl.ds(h * LANES, LANES)
        for i in range(16):
            ext[i, pl.ds(HALO, RX), :] = wind[pl.ds(i * RX, RX), cols]
            ext[i, pl.ds(1, 3), :] = low[pl.ds(AUX + h * SIDE + 3 * i, 3), :]
            ext[i, pl.ds(HALO + RX, 3), :] = high[pl.ds(AUX + h * SIDE + 3 * i, 3), :]
        for k in range(2):
            for l in range(LV):
                a = 0.5 * ext[(k * 2 + 0) * LV + l]
                b = 0.5 * ext[(k * 2 + 1) * LV + l]
                plus, minus = 0.15 - b, 0.15 + b
                if h:
                    plus = jnp.where(col < LANES - 1, plus, 0.0)
                else:
                    minus = jnp.where(col > 0, minus, 0.0)
                for j, value in enumerate((0.15 - a, 0.15 + a, plus, minus)):
                    coef[(k * 4 + j) * LV + l, h] = value
    own = weight_map(cells[...].astype(F32), live_weights(weight, count))
    wlow = weight_map(slot_row(low, 48), slot_row(low, 49))
    whigh = weight_map(slot_row(high, 48), slot_row(high, 49))
    for h in range(2):
        cols = slice(h * LANES, (h + 1) * LANES)
        for l in range(LV):
            wmap[l, h, pl.ds(HALO, RX), :] = own[l * RX : (l + 1) * RX, cols]
            wmap[l, h, pl.ds(2, 2), :] = wlow[l * RX + RX - 2 : l * RX + RX, cols]
            wmap[l, h, pl.ds(HALO + RX, 2), :] = whigh[l * RX : l * RX + 2, cols]
    half = HALO * LINE
    u[pl.ds(0, half), :] = low[pl.ds(0, half), :]
    u[pl.ds(half + RX * LINE, half), :] = high[pl.ds(0, half), :]

    for x in range(RX):
        for h in range(2):
            for l in range(LV):
                u[at(x + HALO, h, l), :] = arrived(probes, x, h, l)

    def cf(k, j, l, h, x):
        return coef[(k * 4 + j) * LV + l, h, pl.ds(x, 1), :]

    def next_column(lo, hi, wrap):
        lo, hi = pltpu.roll(lo, LANES - 1, 1), pltpu.roll(hi, LANES - 1, 1)
        return jnp.where(last_lane, hi, lo), jnp.where(last_lane, lo, hi) if wrap else hi

    def previous_column(lo, hi, wrap):
        lo, hi = pltpu.roll(lo, 1, 1), pltpu.roll(hi, 1, 1)
        return jnp.where(first_lane, hi, lo) if wrap else lo, jnp.where(first_lane, lo, hi)

    def forward(src, k, x, put):
        c = [[src[at(x, h, l), :] for l in range(LV)] for h in range(2)]
        for l in range(LV):
            plus = next_column(c[0][l], c[1][l], False)
            minus = previous_column(c[0][l], c[1][l], False)
            for h in range(2):
                r = 0.2 * c[h][l] + 0.1 * level_sum(c[h], l)
                r += cf(k, 0, l, h, x) * src[at(x + 1, h, l), :]
                r += cf(k, 1, l, h, x) * src[at(x - 1, h, l), :]
                r += cf(k, 2, l, h, x) * plus[h]
                r += cf(k, 3, l, h, x) * minus[h]
                put(x, h, l, r)

    def adjoint(src, k, x, put):
        c = [[src[at(x, h, l), :] for l in range(LV)] for h in range(2)]
        for l in range(LV):
            plus = next_column(*(cf(k, 3, l, h, x) * c[h][l] for h in range(2)), True)
            minus = previous_column(*(cf(k, 2, l, h, x) * c[h][l] for h in range(2)), True)
            for h in range(2):
                r = 0.2 * c[h][l] + 0.1 * level_sum(c[h], l)
                r += cf(k, 1, l, h, x + 1) * src[at(x + 1, h, l), :]
                r += cf(k, 0, l, h, x - 1) * src[at(x - 1, h, l), :]
                put(x, h, l, r + plus[h] + minus[h])

    def sweep(lo, hi, op, src, k, put):
        def step(x, _):
            op(src, k, x, put)
            return 0

        lax.fori_loop(lo, hi, step, 0)

    def clear(dst, lo, hi):
        n = (hi - lo) * LINE
        dst[pl.ds(lo * LINE, n), :] = jnp.zeros((n, LANES), F32)

    def put_v(x, h, l, r):
        v[at(x, h, l), :] = r

    def put_weighted(x, h, l, r):
        u[at(x, h, l), :] = wmap[l, h, pl.ds(x, 1), :] * r

    def put_out(x, h, l, r):
        out[at(x - HALO, h, l), :] = r

    sweep(1, ROWS - 1, forward, u, 0, put_v)

    @pl.when(t == 0)
    def _():
        clear(v, 1, HALO)

    @pl.when(t == last)
    def _():
        clear(v, HALO + RX, ROWS - 1)

    sweep(2, ROWS - 2, forward, v, 1, put_weighted)
    sweep(3, ROWS - 3, adjoint, u, 1, put_v)

    @pl.when(t == 0)
    def _():
        clear(v, HALO - 1, HALO)

    @pl.when(t == last)
    def _():
        clear(v, HALO + RX, HALO + RX + 1)

    sweep(HALO, HALO + RX, adjoint, v, 0, put_out)


def all_blocks(t):
    return t + pltpu.roll(t, 32, 1) + pltpu.roll(t, 64, 1) + pltpu.roll(t, 96, 1)


def folded(prod):
    lane = iota((NP, 128), 1) // NP
    t = jnp.zeros((NP, 128), F32)
    for l in range(LV):
        t += jnp.where(lane == l, prod[l * NP : (l + 1) * NP], 0.0)
    return all_blocks(t)


def product(a, b, dims):
    return lax.dot_general(a, b, (dims, ((), ())), precision=HIGH, preferred_element_type=F32)


def gram_kernel(parts, probes, place, share, msg):
    o = place[0, 0]
    gram = jnp.zeros((BLK, BLK), F32)
    cross = jnp.zeros((BLK, BLK), F32)
    for h in range(2):
        s = parts[pl.ds(h * BLK, BLK), :]
        for g in range(1, 16):
            s = s + parts[pl.ds(g * LINE + h * BLK, BLK), :]
        share[pl.ds(h * BLK, BLK), :] = s
        omega = jnp.concatenate([arrived(probes, o, h, l) for l in range(LV)], axis=0)
        gram += product(s, s, ((1,), (1,)))
        cross += product(omega, s, ((1,), (1,)))
    gram, cross = folded(gram), folded(cross)
    shifted = pltpu.roll(cross, 16, 1)
    lane = iota((8, 128), 1)
    packed = jnp.zeros((8, 128), F32)
    for b in range(4):
        packed = jnp.where(lane // 32 == b, gram[8 * b : 8 * b + 8], packed)
    spare = (lane < 64) & (lane % 32 >= 16)
    for kind in range(4):
        rb, src = kind // 2, (cross if kind % 2 else shifted)
        piece = jnp.where(lane < 32, src[16 * rb : 16 * rb + 8], src[16 * rb + 8 : 16 * rb + 16])
        value = jnp.where(spare, piece, packed)
        for i in range(4):
            msg[pl.ds((4 * i + kind) * 8, 8), :] = value


def sum_kernel(parts, msg):
    n = parts.shape[0] // 8
    s = parts[pl.ds(0, 8), :]
    for g in range(1, n):
        s = s + parts[pl.ds(8 * g, 8), :]
    for d in range(msg.shape[0] // 8):
        msg[pl.ds(8 * d, 8), :] = s


def basis_kernel(parts, share, msg, *, scale):
    n = parts.shape[0] // 8
    s = parts[pl.ds(0, 8), :]
    for g in range(1, n):
        s = s + parts[pl.ds(8 * g, 8), :]
    lane8 = iota((8, 128), 1) // 32
    rows = [all_blocks(jnp.where(lane8 == b, s, 0.0)) for b in range(4)]
    gram = jnp.concatenate(rows, axis=0)
    square = jnp.concatenate([gram] * 4, axis=0)
    flipped = square.T[:NP]
    row, lane = iota((NP, 128), 0), iota((NP, 128), 1)
    a = jnp.where((row < 16) & (lane % 32 >= 16), flipped, gram)
    a = jnp.where(lane < NP, a, jnp.where(lane - NP == row, 1.0, 0.0))
    for j in range(NP - 1):
        pivot = a[j : j + 1, :]
        scaled = pivot / a[j : j + 1, j : j + 1]
        factor = jnp.where(row > j, a[:, j : j + 1], 0.0)
        a = a - factor * scaled
    diag = jnp.sum(jnp.where(lane == row, a, 0.0), axis=1, keepdims=True)
    inverse = jnp.where(lane // 32 == 1, a * (scale / jnp.sqrt(diag)), 0.0)
    inverse = all_blocks(inverse)
    r = iota((128, NP), 0)
    pick = (iota((128, NP), 1) == 2 * (r // 8) + r % 2).astype(F32)
    wide = product(pick, inverse, ((1,), (0,)))
    r = iota((128, 128), 0)
    wide = jnp.where(iota((128, 128), 1) // 32 == (r // 2) % 4, wide, 0.0)
    for h in range(2):
        rows = product(wide, share[pl.ds(h * BLK, BLK), :], ((1,), (0,)))
        for d in range(16):
            msg[pl.ds((3 * d + h) * 8, 8), :] = rows[8 * d : 8 * d + 8]
    for d in range(16):
        msg[pl.ds((3 * d + 2) * 8, 8), :] = s


def finish_kernel(got, basis, core, *, factor):
    for l in range(LV):
        for j in range(2):
            for h in range(2):
                basis[pl.ds((j * LV + l) * RX, RX), pl.ds(h * LANES, LANES)] = got[
                    pl.ds(h * 8 + 2 * l + j, RX, stride=24), :
                ]
    lane = iota((8, 128), 1)
    rows = []
    for rb in range(2):
        for half in range(2):
            first = 16 + 32 * half
            row = jnp.zeros((8, 128), F32)
            for cb in range(2):
                tile = got[pl.ds((3 * (2 * rb + cb) + 2) * 8, 8), :]
                moved = pltpu.roll(tile, (16 * cb - first) % 128, 1)
                row = jnp.where(lane // 16 == cb, moved, row)
            rows.append(row)
    core[...] = jnp.concatenate(rows, axis=0)[:, :NP] * factor


def shape(*dims):
    return jax.ShapeDtypeStruct(dims, F32)


def call(kernel, specs, outs, scratch=()):
    many = isinstance(outs, tuple)
    return pl.pallas_call(
        kernel,
        out_shape=outs,
        in_specs=specs,
        out_specs=(VM,) * len(outs) if many else VM,
        scratch_shapes=list(scratch),
    )


def on_device(probes, wind, station_cell, obs_count, obs_weight):
    tiles, groups = lax.axis_size("space"), lax.axis_size("obs")
    t, o = lax.axis_index("space"), lax.axis_index("obs")
    flat = probes.reshape(NP, LV, 2, 8, 2, LANES).transpose(0, 1, 2, 4, 3, 5).reshape(-1, LANES)
    winds = wind.reshape(16 * RX, NY)
    up, down = call(pack_kernel, [VM] * 4 + [SM], (shape(MSG, LANES), shape(MSG, LANES)))(
        flat, winds, station_cell, obs_weight, obs_count
    )
    low = lax.ppermute(up, "space", [(i, i + 1) for i in range(tiles - 1)])
    high = lax.ppermute(down, "space", [(i + 1, i) for i in range(tiles - 1)])
    place = jnp.stack([t, jnp.int32(tiles)]).reshape(1, 2).astype(jnp.int32)
    local = call(
        tile_kernel,
        [VM] * 4 + [SM, SM] + [VM] * 2,
        shape(RX * LINE, LANES),
        (
            pltpu.VMEM((ROWS * LINE, LANES), F32),
            pltpu.VMEM((ROWS * LINE, LANES), F32),
            pltpu.VMEM((32, 2, ROWS, LANES), F32),
            pltpu.VMEM((LV, 2, ROWS, LANES), F32),
            pltpu.VMEM((16, ROWS, LANES), F32),
        ),
    )(flat, winds, station_cell, obs_weight, obs_count, place, low, high)
    parts = lax.all_to_all(local.reshape(groups, LINE, LANES), "obs", 0, 0, tiled=True)
    share, msg = call(gram_kernel, [VM, VM, SM], (shape(LINE, LANES), shape(groups * 8, 128)))(
        parts.reshape(groups * LINE, LANES), flat, o.reshape(1, 1).astype(jnp.int32)
    )
    got = lax.all_to_all(msg.reshape(groups, 8, 128), "obs", 0, 0, tiled=True)
    msg = call(sum_kernel, [VM], shape(tiles * 8, 128))(got.reshape(groups * 8, 128))
    got = lax.all_to_all(msg.reshape(tiles, 8, 128), "space", 0, 0, tiled=True)
    scale = math.sqrt(LV * RX * tiles * NY)
    msg = call(
        lambda *refs: basis_kernel(*refs, scale=scale), [VM] * 2, shape(groups * 24, LANES)
    )(got.reshape(tiles * 8, 128), share)
    got = lax.all_to_all(msg.reshape(groups, 24, LANES), "obs", 0, 0, tiled=True)
    factor = 1.0 / (groups * tiles * station_cell.shape[1])
    basis, core = call(
        lambda *refs: finish_kernel(*refs, factor=factor),
        [VM],
        (shape(2 * LV * RX, NY), shape(NP, NP)),
    )(got.reshape(groups * 24, LANES))
    return basis.reshape(2, LV, RX, NY), core


def solution(mesh):
    in_specs = (
        P(None, None, "space", None),
        P("obs", None, None, None, "space", None),
        P("obs", "space"),
        P("obs", "space"),
        P("obs", "space"),
    )
    out_specs = (P("obs", None, "space", None), P())
    return jax.shard_map(
        on_device, mesh=mesh, in_specs=in_specs, out_specs=out_specs, check_vma=False
    )
```

time: 186 us -> 147 us (0.79)
  Pallas kernels: 0 us -> 31.3 us
  starting transfers between devices: 41.4 us -> 10.5 us
  other arithmetic: 27.6 us -> 0.59 us
  local copies, waits for them, and re-layouts: 24.9 us -> 2.17 us
  blocking collectives: 55 us -> 72.3 us
  waiting for transfers between devices: 33.3 us -> 27.9 us
    pallas_call x0 -> x6, Pallas kernels: none -> 31.3 us  [the longest x1 16.2 us: on_device(): call(tile_kernel, [VM] * 4 + [SM, SM] + [VM] * 2, shape(RX * LINE, LANES)...]
    ppermute x10 -> x2, starting transfers between devices: 28 us -> 3.05 us  [the longest x1 1.76 us: on_device(): low = lax.ppermute(up, 'space', [(i, i + 1) for i in range(tiles - 1)])]
    all_to_all x2 -> x3, blocking collectives: 55 us -> 72.3 us  [the longest x1 47.2 us: on_device(): got = lax.all_to_all(msg.reshape(tiles, 8, 128), 'space', 0, 0, tiled=True)]
    scatter-add x1 -> x0, other arithmetic: 7.02 us -> none  [on_device(): jnp.zeros_like(flat).at[:, cells].add(weighted).reshape(probes.shape)]
    all_to_all x2 -> x1, waiting for transfers between devices: 31 us -> 24.1 us  [on_device(): lax.all_to_all(local.reshape(groups, LINE, LANES), 'obs', 0, 0, tiled=True)]
    another operation x5 -> x0, other arithmetic: 6.68 us -> none  [the longest x3 3.6 us: on_device(): lower = jnp.linalg.cholesky(gram)]
    reshape x6 -> x0, local copies, waits for them, and re-layouts: 6.1 us -> none  [the longest x1 5.12 us: on_device(): jnp.zeros_like(flat).at[:, cells].add(weighted).reshape(probes.shape)]
    all_to_all x2 -> x1, starting transfers between devices: 13.4 us -> 7.48 us  [on_device(): lax.all_to_all(local.reshape(groups, LINE, LANES), 'obs', 0, 0, tiled=True)]
  transfers between devices with their start and end apart: 12 -> 3, of which waited for: 5 -> 2; matrix products, arithmetic and copies ran while one was open for 3% -> 0% of each run, Pallas kernels for 0% -> 0%
where the time goes in v1:
time: 147 us; the launch traced here: 146 us
  blocking collectives  72.3 us (49%)
  Pallas kernels  31.3 us (21%)
  waiting for transfers between devices  27.9 us (19%)
  starting transfers between devices  10.5 us (7%)
  local copies, waits for them, and re-layouts  2.17 us (1%)
    all_to_all x1, blocking collectives, on_device(): got = lax.all_to_all(msg.reshape(tiles, 8, 128), 'space', 0, 0, tiled=True)  47.2 us
    all_to_all x1, waiting for transfers between devices, on_device(): lax.all_to_all(local.reshape(groups, LINE, LANES), 'obs', 0, 0, tiled=True)  24.1 us
    pallas_call x1, Pallas kernels, on_device(): call(tile_kernel, [VM] * 4 + [SM, SM] + [VM] * 2, shape(RX * LINE, LANES)...  16.2 us
    all_to_all x1, blocking collectives, on_device(): got = lax.all_to_all(msg.reshape(groups, 8, 128), 'obs', 0, 0, tiled=True)  12.6 us
    all_to_all x1, blocking collectives, on_device(): lax.all_to_all(msg.reshape(groups, 24, LANES), 'obs', 0, 0, tiled=True)  12.5 us
    all_to_all x1, starting transfers between devices, on_device(): lax.all_to_all(local.reshape(groups, LINE, LANES), 'obs', 0, 0, tiled=True)  7.48 us
    pallas_call x1, Pallas kernels, on_device(): call(lambda *refs: basis_kernel(*refs, scale=scale), [VM] * 2, shape(grou...  4.93 us
    ppermute x1, waiting for transfers between devices, on_device(): high = lax.ppermute(down, 'space', [(i + 1, i) for i in range(tiles - 1)])  3.87 us
  transfers between devices with their start and end apart: 3, of which 2 were waited for; matrix products, arithmetic and copies ran while one was open for 0% of the time, Pallas kernels for 0%

profile of v1, /device:TPU:2, one launch (start us, length us, event | category | flops | bytes accessed | tf_op | source)
XLA Modules:
  0.0 146.0 jit_solution(11596340333035580557)
XLA Ops:
  1.3 3.4 %shard_map.68 = (f32[1136,128]{1,0:T(8,128)}, f32[1136,128]{1,0:T(8,128)}) custom-call(f32[4096,128]{1,0:T(8,128)} %bitcast.19, f32[256,256]{1,0:T(8,128)} %bitcast.24, s32[1,256]{1,0:T(1,128)} %cells.3, f32[1,256]{1,0:T(1,128)} %weight.3, s32[1,1]{1,0:T(1,128)S(6)} %copy.7.count), custom_call_target="tpu_custom_call" | custom-call | tf_op jit(solution)/shard_map/pallas_call | solution.py:340
  4.7 1.8 %collective-permute-start = (f32[1136,128]{1,0:T(8,128)}, f32[1136,128]{1,0:T(8,128)S(1)}, u32[]{:S(2)}, u32[]{:S(2)}) collective-permute-start(f32[1136,128]{1,0:T(8,128)} %get-tuple-element.8), channel_id=1, source_target_pairs={{0,1},{1,2},{2,3},{3,4},{4,5},{5,6},{6,7},{7,8},{8,9},{9,10},{10,1... | collective-permute-start | bytes 1744904 | tf_op jit(solution)/shard_map/ppermute | solution.py:343
  6.4 1.3 collective-permute-start.1
  7.7 0.6 add_bitcast_fusion.place
  8.3 0.0 collective-permute-done.low
  8.3 0.0 copy-start.1
  8.3 3.9 %collective-permute-done.1.high = f32[1136,128]{1,0:T(8,128)S(1)} collective-permute-done((f32[1136,128]{1,0:T(8,128)}, f32[1136,128]{1,0:T(8,128)S(1)}, u32[]{:S(2)}, u32[]{:S(2)}) %collective-permute-start.1) | collective-permute-done | bytes 581664 | tf_op jit(solution)/shard_map/ppermute | solution.py:344
  12.2 0.0 copy-done.1
  12.2 0.0 copy-start.2
  12.2 0.8 copy-done.2
  13.0 16.2 %shard_map.69 = f32[4096,128]{1,0:T(8,128)} custom-call(f32[4096,128]{1,0:T(8,128)} %bitcast.20, f32[256,256]{1,0:T(8,128)} %bitcast.25, s32[1,256]{1,0:T(1,128)} %cells.3, f32[1,256]{1,0:T(1,128)} %weight.3, s32[1,1]{1,0:T(1,128)S(6)} %copy.7.count, s32[1,2]{1,0:T(1,128)} %add_bitcast_fusion.place, f32[1136,128]{1,0:T(8,128)} %copy-done.1, ...), custom_call_target="tpu_custom_call" | custom-call | tf_op jit(solution)/shard_map/pallas_call | solution.py:346
  29.2 7.5 %all-to-all-start = ((f32[16,256,128]{2,1,0:T(8,128)}), f32[16,256,128]{2,1,0:T(8,128)S(1)}, u32[]{:S(2)}, u32[]{:S(2)}) async-start(f32[16,256,128]{2,1,0:T(8,128)} %bitcast.23), calls=%async_computation | async-start | bytes 4194304 | tf_op jit(solution)/shard_map/all_to_all | solution.py:358
  36.7 24.1 %all-to-all-done = f32[16,256,128]{2,1,0:T(8,128)S(1)} async-done(((f32[16,256,128]{2,1,0:T(8,128)}), f32[16,256,128]{2,1,0:T(8,128)S(1)}, u32[]{:S(2)}, u32[]{:S(2)}) %all-to-all-start) | async-done | bytes 2097184 | tf_op jit(solution)/shard_map/all_to_all | solution.py:358
  60.7 0.0 copy-start
  60.7 1.3 copy-done
  62.1 3.6 %shard_map.70 = (f32[256,128]{1,0:T(8,128)}, f32[128,128]{1,0:T(8,128)}) custom-call(f32[4096,128]{1,0:T(8,128)} %bitcast.22, f32[4096,128]{1,0:T(8,128)} %bitcast.21, s32[1,1]{1,0:T(1,128)} %bitcast.10.place), custom_call_target="tpu_custom_call" | custom-call | tf_op jit(solution)/shard_map/pallas_call | solution.py:359
  65.7 12.6 %all_to_all.20 = f32[16,8,128]{2,1,0:T(8,128)} all-to-all(f32[16,8,128]{2,1,0:T(8,128)} %bitcast.31), channel_id=1, replica_groups=mesh['obs'=16,'space'=32] {'obs'}, dimensions={0} | all-to-all | bytes 131072 | tf_op jit(solution)/shard_map/all_to_all | solution.py:362
  78.3 1.5 %shard_map.71 = f32[256,128]{1,0:T(8,128)} custom-call(f32[128,128]{1,0:T(8,128)} %bitcast.30), custom_call_target="tpu_custom_call" | custom-call | tf_op jit(solution)/shard_map/pallas_call | solution.py:363
  79.8 47.2 %all_to_all.21 = f32[32,8,128]{2,1,0:T(8,128)} all-to-all(f32[32,8,128]{2,1,0:T(8,128)} %bitcast.29), channel_id=1, replica_groups=mesh['obs'=16,'space'=32] {'space'}, dimensions={0} | all-to-all | bytes 262144 | tf_op jit(solution)/shard_map/all_to_all | solution.py:364
  127.0 4.9 %shard_map.72 = f32[384,128]{1,0:T(8,128)} custom-call(f32[256,128]{1,0:T(8,128)} %bitcast.28, f32[256,128]{1,0:T(8,128)} %get-tuple-element.11.refs_1_), custom_call_target="tpu_custom_call" | custom-call | tf_op jit(solution)/shard_map/pallas_call | solution.py:366
  131.9 12.5 %all_to_all.22 = f32[16,24,128]{2,1,0:T(8,128)} all-to-all(f32[16,24,128]{2,1,0:T(8,128)} %bitcast.26), channel_id=1, replica_groups=mesh['obs'=16,'space'=32] {'obs'}, dimensions={0} | all-to-all | bytes 393216 | tf_op jit(solution)/shard_map/all_to_all | solution.py:369
  144.4 1.6 %shard_map.73 = (f32[128,256]{1,0:T(8,128)}, f32[32,32]{1,0:T(8,128)}) custom-call(f32[384,128]{1,0:T(8,128)} %bitcast.27), custom_call_target="tpu_custom_call" | custom-call | tf_op jit(solution)/shard_map/pallas_call | solution.py:371
Async XLA Ops:
  4.7 3.7 %collective-permute-start = (f32[1136,128]{1,0:T(8,128)}, f32[1136,128]{1,0:T(8,128)S(1)}, u32[]{:S(2)}, u32[]{:S(2)}) collective-permute-start(f32[1136,128]{1,0:T(8,128)} %get-tuple-element.8), channel_id=1, source_target_pairs={{0,1},{1,2},{2,3},{3,4},{4,5},{5,6},{6,7},{7,8},{8,9},{9,10},{10,1... | collective-permute-start | bytes 1744904 | tf_op jit(solution)/shard_map/ppermute | solution.py:343
  6.4 5.8 %collective-permute-start.1 = (f32[1136,128]{1,0:T(8,128)}, f32[1136,128]{1,0:T(8,128)S(1)}, u32[]{:S(2)}, u32[]{:S(2)}) collective-permute-start(f32[1136,128]{1,0:T(8,128)} %get-tuple-element.9), channel_id=1, source_target_pairs={{1,0},{2,1},{3,2},{4,3},{5,4},{6,5},{7,6},{8,7},{9,8},{10,9},{11,1... | collective-permute-start | bytes 1744904 | tf_op jit(solution)/shard_map/ppermute | solution.py:344
  8.3 3.9 %copy-start.1 = (f32[1136,128]{1,0:T(8,128)}, f32[1136,128]{1,0:T(8,128)S(1)}, u32[]{:S(2)}) copy-start(f32[1136,128]{1,0:T(8,128)S(1)} %collective-permute-done.low) | copy-start | bytes 1744900
  12.2 0.8 copy-start.2
  29.2 31.5 %all-to-all-start = ((f32[16,256,128]{2,1,0:T(8,128)}), f32[16,256,128]{2,1,0:T(8,128)S(1)}, u32[]{:S(2)}, u32[]{:S(2)}) async-start(f32[16,256,128]{2,1,0:T(8,128)} %bitcast.23), calls=%async_computation | async-start | bytes 4194304 | tf_op jit(solution)/shard_map/all_to_all | solution.py:358
  60.7 1.3 copy-start

commit v2 on v1

v2 whole, which is shorter than its diff:
```python
import math

import jax
import jax.numpy as jnp
from jax import lax
from jax.experimental import pallas as pl
from jax.experimental.pallas import tpu as pltpu
from jax.sharding import PartitionSpec as P

F32 = jnp.float32
HIGH = lax.Precision.HIGHEST
VM = pl.BlockSpec(memory_space=pltpu.VMEM)
SM = pl.BlockSpec(memory_space=pltpu.SMEM)
NT = (((1,), (1,)), ((), ()))

NP, LV, RX, NY = 32, 4, 16, 256
OWN = 16
WIN = 32
MARGIN = 8
HALO = 4
ROWS = RX + 2 * HALO
LANES = 128
PAD = 8
UNROLL = 4
KINDS = 5
SIDE = KINDS * LV * HALO
MSG = 2 * SIDE + NP * HALO


def iota(shape, dim):
    return lax.broadcasted_iota(jnp.int32, shape, dim)


def live_weights(weight_ref, count_ref):
    w = weight_ref[...]
    return jnp.where(iota(w.shape, 1) < count_ref[0, 0], w, 0.0)


def weight_map(cell_row, live):
    cell = cell_row.astype(jnp.int32)
    row, col = cell // NY, cell % NY
    nslot = cell.shape[1]
    on_col = (iota((NY, nslot), 0) == col).astype(jnp.bfloat16)
    on_row = iota((LV * RX, nslot), 0) == row
    total = jnp.zeros((LV * RX, NY), F32)
    rest = live
    for _ in range(3):
        part = rest.astype(jnp.bfloat16).astype(F32)
        rest = rest - part
        lhs = jnp.where(on_row, part, 0.0).astype(jnp.bfloat16)
        total += lax.dot_general(lhs, on_col, NT, preferred_element_type=F32)
    return total


def window(tiles, first):
    shape = tiles[0][0].shape
    lane = iota(shape, 1)
    col = first + lane % WIN
    halves = []
    for h in range(2):
        start = first - h * LANES
        if isinstance(first, int) and not (-WIN < start < LANES):
            halves.append(None)
            continue
        acc = jnp.zeros(shape, F32)
        for l in range(LV):
            shift = l * WIN - start
            shift = shift % LANES if isinstance(first, int) else (shift + 2 * LANES) % LANES
            acc = jnp.where(lane // WIN == l, pltpu.roll(tiles[l][h], shift, 1), acc)
        halves.append(acc)
    if halves[0] is None:
        value = halves[1]
    elif halves[1] is None:
        value = halves[0]
    else:
        value = jnp.where(col < LANES, halves[0], halves[1])
    return jnp.where((col >= 0) & (col < NY), value, 0.0)


def prepare_kernel(probes, wind, cells, weight, count, place, raw, patch, up, down):
    first = place[0, 2] * OWN - MARGIN
    for i in range(4 * LV):
        raw[pl.ds(i * RX, RX), :] = 0.5 * wind[pl.ds(i * RX, RX), :]
    raw[pl.ds(4 * LV * RX, LV * RX), :] = weight_map(
        cells[...].astype(F32), live_weights(weight, count)
    )

    def one(p, _):
        for xt in range(2):
            tiles = [
                [
                    probes[
                        pl.ds(pl.multiple_of((p * LV + l) * RX + 8 * xt, 8), 8),
                        pl.ds(h * LANES, LANES),
                    ]
                    for h in range(2)
                ]
                for l in range(LV)
            ]
            patch[pl.ds(pl.multiple_of(p * RX + 8 * xt, 8), 8), :] = window(tiles, first)
        return 0

    lax.fori_loop(0, NP, one, 0, unroll=2)
    for out, start in ((up, RX - HALO), (down, 0)):
        for h in range(2):
            for i in range(KINDS * LV):
                out[pl.ds(h * SIDE + i * HALO, HALO), :] = raw[
                    pl.ds(i * RX + start, HALO), pl.ds(h * LANES, LANES)
                ]
        for p in range(NP):
            out[pl.ds(2 * SIDE + p * HALO, HALO), :] = patch[pl.ds(p * RX + start, HALO), :]


def message_kernel(raw, low, high, msg, edge):
    for h in range(2):
        for i in range(KINDS * LV):
            src = pl.ds(h * SIDE + i * HALO, HALO)
            edge[i, h, pl.ds(0, HALO), :] = low[src, :]
            edge[i, h, pl.ds(HALO, HALO), :] = high[src, :]
    for kind in range(KINDS):
        for xt in range(3):
            tiles = [
                [
                    raw[
                        pl.ds((kind * LV + l) * RX + 8 * xt, 8), pl.ds(h * LANES, LANES)
                    ]
                    if xt < 2
                    else edge[kind * LV + l, h]
                    for h in range(2)
                ]
                for l in range(LV)
            ]
            for d in range(NY // OWN):
                value = window(tiles, d * OWN - MARGIN)
                base = (d * KINDS + kind) * ROWS
                if xt < 2:
                    msg[pl.ds(base + HALO + 8 * xt, 8), :] = value
                else:
                    msg[pl.ds(base, HALO), :] = value[:HALO]
                    msg[pl.ds(base + HALO + RX, HALO), :] = value[HALO:]


def all_blocks(t):
    return t + pltpu.roll(t, 32, 1) + pltpu.roll(t, 64, 1) + pltpu.roll(t, 96, 1)


def product(a, b, dims):
    return lax.dot_general(a, b, (dims, ((), ())), precision=HIGH, preferred_element_type=F32)


def aligned(row):
    return pl.multiple_of(row, 8)


def patch_kernel(
    got, patch, low, high, place, share, msg, u, au, dx, dy, cf, t1, t2, va, pa, qa, s
):
    t, tiles, o = place[0, 0], place[0, 1], place[0, 2]
    lane = iota((8, LANES), 1)
    plus_level = jnp.where(lane < LANES - WIN, 0.1, 0.0)
    minus_level = jnp.where(lane >= WIN, 0.1, 0.0)
    col = o * OWN - MARGIN + lane % WIN
    inside = []
    for i in range(3):
        row = t * RX - HALO + 8 * i + iota((8, LANES), 0)
        inside.append((row >= 0) & (row < tiles * RX) & (col >= 0) & (col < NY))

    def levels(c):
        return plus_level * pltpu.roll(c, LANES - WIN, 1) + minus_level * pltpu.roll(c, WIN, 1)

    def right(c):
        return pltpu.roll(c, LANES - 1, 1)

    def left(c):
        return pltpu.roll(c, 1, 1)

    edge = jnp.zeros((PAD, LANES), F32)
    for ref in (u, va, pa, qa):
        ref[pl.ds(0, PAD), :] = edge
        ref[pl.ds(PAD + NP * ROWS, PAD), :] = edge
    for j in range(4):
        cf[pl.ds(j * (ROWS + 2 * PAD), PAD), :] = edge
        cf[pl.ds(j * (ROWS + 2 * PAD) + PAD + ROWS, PAD), :] = edge
    for ref in (t1, t2):
        for j in range(UNROLL):
            ref[pl.ds(j * (ROWS + 2 * PAD), PAD), :] = edge
            ref[pl.ds(j * (ROWS + 2 * PAD) + PAD + ROWS, PAD), :] = edge
    for p in range(NP):
        base = PAD + p * ROWS
        u[pl.ds(base, HALO), :] = low[pl.ds(2 * SIDE + p * HALO, HALO), :]
        u[pl.ds(base + HALO, RX), :] = patch[pl.ds(p * RX, RX), :]
        u[pl.ds(base + HALO + RX, HALO), :] = high[pl.ds(2 * SIDE + p * HALO, HALO), :]

    def shared(p, _):
        for i in range(3):
            at = aligned(p * ROWS + 8 * i)
            c = u[pl.ds(at + PAD, 8), :]
            xp, xm = u[pl.ds(at + PAD + 1, 8), :], u[pl.ds(at + PAD - 1, 8), :]
            yp, ym = right(c), left(c)
            mean = 0.2 * c + 0.15 * ((xp + xm) + (yp + ym)) + levels(c)
            au[pl.ds(at, 8), :] = jnp.where(inside[i], mean, 0.0)
            dx[pl.ds(at, 8), :] = jnp.where(inside[i], xp - xm, 0.0)
            dy[pl.ds(at, 8), :] = jnp.where(inside[i], yp - ym, 0.0)
            for ref in (va, pa, qa):
                ref[pl.ds(at + PAD, 8), :] = edge
        return 0

    lax.fori_loop(0, NP, shared, 0, unroll=4)

    def coef(j, i, off=0):
        return cf[pl.ds(j * (ROWS + 2 * PAD) + PAD + 8 * i + off, 8), :]

    def one_window(g, _):
        base = g * (KINDS * ROWS)

        def of(kind, i):
            return got[pl.ds(aligned(base + kind * ROWS + 8 * i), 8), :]

        for i in range(3):
            a, b = of(2, i), of(3, i)
            for j, value in enumerate((0.15 - a, 0.15 + a, 0.15 - b, 0.15 + b)):
                cf[pl.ds(j * (ROWS + 2 * PAD) + PAD + 8 * i, 8), :] = value

        def some(step, _):
            slots = range(UNROLL)
            at = [[aligned((step * UNROLL + q) * ROWS + 8 * i) for i in range(3)] for q in slots]
            slot = [[q * (ROWS + 2 * PAD) + PAD + 8 * i for i in range(3)] for q in slots]
            for i in range(3):
                a, b = of(0, i), of(1, i)
                for q in slots:
                    here = pl.ds(at[q][i], 8)
                    t1[pl.ds(slot[q][i], 8), :] = au[here, :] - a * dx[here, :] - b * dy[here, :]
            for i in range(3):
                cxp, cxm, cyp, cym = (coef(j, i) for j in range(4))
                w = of(4, i)
                for q in slots:
                    c = t1[pl.ds(slot[q][i], 8), :]
                    r = 0.2 * c + levels(c)
                    r += cxp * t1[pl.ds(slot[q][i] + 1, 8), :]
                    r += cxm * t1[pl.ds(slot[q][i] - 1, 8), :]
                    r += cyp * right(c) + cym * left(c)
                    t2[pl.ds(slot[q][i], 8), :] = w * r
            for i in range(3):
                cxp, cxm, cyp, cym = coef(0, i, -1), coef(1, i, 1), coef(2, i), coef(3, i)
                a, b = of(0, i), of(1, i)
                for q in slots:
                    c = t2[pl.ds(slot[q][i], 8), :]
                    r = 0.2 * c + levels(c)
                    r += cxm * t2[pl.ds(slot[q][i] + 1, 8), :]
                    r += cxp * t2[pl.ds(slot[q][i] - 1, 8), :]
                    r += right(cym * c) + left(cyp * c)
                    here = pl.ds(at[q][i] + PAD, 8)
                    va[here, :] += r
                    pa[here, :] += a * r
                    qa[here, :] += b * r
            return 0

        lax.fori_loop(0, NP // UNROLL, some, 0)
        return 0

    lax.fori_loop(0, got.shape[0] // (KINDS * ROWS), one_window, 0)

    def mask(p, _):
        for i in range(3):
            at = pl.ds(aligned(PAD + p * ROWS + 8 * i), 8)
            for ref in (va, pa, qa):
                ref[at, :] = jnp.where(inside[i], ref[at, :], 0.0)
        return 0

    lax.fori_loop(0, NP, mask, 0, unroll=4)
    core_lane = (lane % WIN >= MARGIN) & (lane % WIN < MARGIN + OWN)

    def last(p, _):
        for i in range(2):
            at = aligned(PAD + p * ROWS + 8 * i) + HALO
            c, q = va[pl.ds(at, 8), :], qa[pl.ds(at, 8), :]
            r = 0.2 * c + levels(c)
            r += 0.15 * ((va[pl.ds(at + 1, 8), :] + va[pl.ds(at - 1, 8), :]) + (right(c) + left(c)))
            r += (pa[pl.ds(at + 1, 8), :] - pa[pl.ds(at - 1, 8), :]) + (right(q) - left(q))
            s[pl.ds(aligned(p * RX + 8 * i), 8), :] = jnp.where(core_lane, r, 0.0)
        return 0

    lax.fori_loop(0, NP, last, 0, unroll=4)

    gram = jnp.zeros((NP, LANES), F32)
    cross = jnp.zeros((NP, LANES), F32)
    for x in range(RX):
        sx = s[pl.ds(x, NP, stride=RX), :]
        share[pl.ds(x * NP, NP), :] = sx
        four = jnp.concatenate([sx] * 4, axis=0)
        gram += product(sx, four, ((1,), (1,)))
        cross += product(u[pl.ds(PAD + HALO + x, NP, stride=ROWS), :], four, ((1,), (1,)))
    shifted = pltpu.roll(cross, 16, 1)
    lane = iota((8, 128), 1)
    packed = jnp.zeros((8, 128), F32)
    for b in range(4):
        packed = jnp.where(lane // 32 == b, gram[8 * b : 8 * b + 8], packed)
    spare = (lane < 64) & (lane % 32 >= 16)
    for kind in range(4):
        rb, src = kind // 2, (cross if kind % 2 else shifted)
        piece = jnp.where(lane < 32, src[16 * rb : 16 * rb + 8], src[16 * rb + 8 : 16 * rb + 16])
        value = jnp.where(spare, piece, packed)
        for i in range(4):
            msg[pl.ds((4 * i + kind) * 8, 8), :] = value


def sum_kernel(parts, msg):
    n = parts.shape[0] // 8
    s = parts[pl.ds(0, 8), :]
    for g in range(1, n):
        s = s + parts[pl.ds(8 * g, 8), :]
    for d in range(msg.shape[0] // 8):
        msg[pl.ds(8 * d, 8), :] = s


def basis_kernel(parts, share, msg, *, scale):
    n = parts.shape[0] // 8
    s = parts[pl.ds(0, 8), :]
    for g in range(1, n):
        s = s + parts[pl.ds(8 * g, 8), :]
    lane8 = iota((8, 128), 1) // 32
    rows = [all_blocks(jnp.where(lane8 == b, s, 0.0)) for b in range(4)]
    gram = jnp.concatenate(rows, axis=0)
    square = jnp.concatenate([gram] * 4, axis=0)
    flipped = square.T[:NP]
    row, lane = iota((NP, 128), 0), iota((NP, 128), 1)
    a = jnp.where((row < 16) & (lane % 32 >= 16), flipped, gram)
    a = jnp.where(lane < NP, a, jnp.where(lane - NP == row, 1.0, 0.0))
    for j in range(NP - 1):
        pivot = a[j : j + 1, :]
        scaled = pivot / a[j : j + 1, j : j + 1]
        factor = jnp.where(row > j, a[:, j : j + 1], 0.0)
        a = a - factor * scaled
    diag = jnp.sum(jnp.where(lane == row, a, 0.0), axis=1, keepdims=True)
    inverse = jnp.where(lane // 32 == 1, a * (scale / jnp.sqrt(diag)), 0.0)
    inverse = all_blocks(inverse)
    r = iota((NP, NP), 0)
    pick = (iota((NP, NP), 1) == 2 * (r % 16) + r // 16).astype(F32)
    rows = product(pick, inverse, ((1,), (0,)))[:, :NP]
    mine = (lane[:16] % WIN >= MARGIN) & (lane[:16] % WIN < MARGIN + OWN)
    for x in range(RX):
        out = product(rows, share[pl.ds(x * NP, NP), :], ((1,), (0,)))
        both = jnp.where(mine, out[:16], pltpu.roll(out[16:], OWN, 1))
        msg[pl.ds(x, 16, stride=24), :] = both
    for d in range(16):
        msg[pl.ds(24 * d + 16, 8), :] = s


def finish_kernel(got, basis, core, *, factor):
    lane = iota((8, 128), 1)
    for xt in range(2):
        for h in range(2):
            sources = [got[pl.ds(24 * (8 * h + d) + 8 * xt, 8), :] for d in range(8)]
            for j in range(2):
                for l in range(LV):
                    acc = jnp.zeros((8, 128), F32)
                    for d in range(8):
                        shift = (OWN * d - WIN * l - MARGIN - OWN * j) % LANES
                        acc = jnp.where(lane // OWN == d, pltpu.roll(sources[d], shift, 1), acc)
                    basis[
                        pl.ds((j * LV + l) * RX + 8 * xt, 8), pl.ds(h * LANES, LANES)
                    ] = acc
    rows = []
    for rb in range(2):
        for half in range(2):
            first = 16 + 32 * half
            row = jnp.zeros((8, 128), F32)
            for cb in range(2):
                tile = got[pl.ds((3 * (2 * rb + cb) + 2) * 8, 8), :]
                moved = pltpu.roll(tile, (16 * cb - first) % 128, 1)
                row = jnp.where(lane // 16 == cb, moved, row)
            rows.append(row)
    core[...] = jnp.concatenate(rows, axis=0)[:, :NP] * factor


def shape(*dims):
    return jax.ShapeDtypeStruct(dims, F32)


def call(kernel, specs, outs, scratch=()):
    many = isinstance(outs, tuple)
    return pl.pallas_call(
        kernel,
        out_shape=outs,
        in_specs=specs,
        out_specs=(VM,) * len(outs) if many else VM,
        scratch_shapes=list(scratch),
    )


def on_device(probes, wind, station_cell, obs_count, obs_weight):
    tiles, groups = lax.axis_size("space"), lax.axis_size("obs")
    place = jnp.stack([lax.axis_index("space"), tiles, lax.axis_index("obs")])
    place = place.reshape(1, 3).astype(jnp.int32)
    raw, patch, up, down = call(
        prepare_kernel,
        [VM] * 4 + [SM] * 2,
        (
            shape(KINDS * LV * RX, NY),
            shape(NP * RX, LANES),
            shape(MSG, LANES),
            shape(MSG, LANES),
        ),
    )(
        probes.reshape(NP * LV * RX, NY),
        wind.reshape(4 * LV * RX, NY),
        station_cell,
        obs_weight,
        obs_count,
        place,
    )
    low = lax.ppermute(up, "space", [(i, i + 1) for i in range(tiles - 1)])
    high = lax.ppermute(down, "space", [(i + 1, i) for i in range(tiles - 1)])
    msg = call(
        message_kernel,
        [VM] * 3,
        shape(groups * KINDS * ROWS, LANES),
        (pltpu.VMEM((KINDS * LV, 2, 8, LANES), F32),),
    )(raw, low, high)
    got = lax.all_to_all(msg.reshape(groups, KINDS * ROWS, LANES), "obs", 0, 0, tiled=True)
    field = pltpu.VMEM((NP * ROWS, LANES), F32)
    padded = pltpu.VMEM((NP * ROWS + 2 * PAD, LANES), F32)
    share, msg = call(
        patch_kernel,
        [VM] * 4 + [SM],
        (shape(RX * NP, LANES), shape(groups * 8, 128)),
        (
            padded,
            field,
            field,
            field,
            pltpu.VMEM((4 * (ROWS + 2 * PAD), LANES), F32),
            pltpu.VMEM((UNROLL * (ROWS + 2 * PAD), LANES), F32),
            pltpu.VMEM((UNROLL * (ROWS + 2 * PAD), LANES), F32),
            padded,
            padded,
            padded,
            pltpu.VMEM((NP * RX, LANES), F32),
        ),
    )(got.reshape(groups * KINDS * ROWS, LANES), patch, low, high, place)
    got = lax.all_to_all(msg.reshape(groups, 8, 128), "obs", 0, 0, tiled=True)
    msg = call(sum_kernel, [VM], shape(tiles * 8, 128))(got.reshape(groups * 8, 128))
    got = lax.all_to_all(msg.reshape(tiles, 8, 128), "space", 0, 0, tiled=True)
    scale = math.sqrt(LV * RX * tiles * NY)
    msg = call(
        lambda *refs: basis_kernel(*refs, scale=scale), [VM] * 2, shape(groups * 24, LANES)
    )(got.reshape(tiles * 8, 128), share)
    got = lax.all_to_all(msg.reshape(groups, 24, LANES), "obs", 0, 0, tiled=True)
    factor = 1.0 / (groups * tiles * station_cell.shape[1])
    basis, core = call(
        lambda *refs: finish_kernel(*refs, factor=factor),
        [VM],
        (shape(2 * LV * RX, NY), shape(NP, NP)),
    )(got.reshape(groups * 24, LANES))
    return basis.reshape(2, LV, RX, NY), core


def solution(mesh):
    in_specs = (
        P(None, None, "space", None),
        P("obs", None, None, None, "space", None),
        P("obs", "space"),
        P("obs", "space"),
        P("obs", "space"),
    )
    out_specs = (P("obs", None, "space", None), P())
    return jax.shard_map(
        on_device, mesh=mesh, in_specs=in_specs, out_specs=out_specs, check_vma=False
    )
```

time: 147 us -> 146 us (level)
  waiting for transfers between devices: 27.9 us -> 3.85 us
  Pallas kernels: 31.3 us -> 53.5 us
  blocking collectives: 72.3 us -> 82.8 us
  starting transfers between devices: 10.5 us -> 3.03 us
  local copies, waits for them, and re-layouts: 2.17 us -> 0.67 us
    all_to_all x1 -> x0, waiting for transfers between devices: 24.1 us -> none  [on_device(): lax.all_to_all(local.reshape(groups, LINE, LANES), 'obs', 0, 0, tiled=True)]
    all_to_all x0 -> x1, blocking collectives: none -> 22.8 us  [on_device(): lax.all_to_all(msg.reshape(groups, KINDS * ROWS, LANES), 'obs', 0, 0, til...]
    pallas_call x3, Pallas kernels: 23.2 us -> 44.8 us  [the longest x1 37 us: on_device(): call(patch_kernel, [VM] * 4 + [SM], (shape(RX * NP, LANES), shape(groups...]
    all_to_all x1, blocking collectives: 47.2 us -> 35.6 us  [on_device(): got = lax.all_to_all(msg.reshape(tiles, 8, 128), 'space', 0, 0, tiled=True)]
    all_to_all x1 -> x0, starting transfers between devices: 7.48 us -> none  [on_device(): lax.all_to_all(local.reshape(groups, LINE, LANES), 'obs', 0, 0, tiled=True)]
    unnamed x6 -> x4, local copies, waits for them, and re-layouts: 2.17 us -> 0.67 us
  transfers between devices with their start and end apart: 3 -> 2, of which waited for: 2 -> 1; matrix products, arithmetic and copies ran while one was open for 0% -> 0% of each run, Pallas kernels for 0% -> 0%
where the time goes in v2:
time: 146 us
  blocking collectives  82.8 us (57%)
  Pallas kernels  53.5 us (37%)
  waiting for transfers between devices  3.85 us (3%)
  starting transfers between devices  3.03 us (2%)
    pallas_call x1, Pallas kernels, on_device(): call(patch_kernel, [VM] * 4 + [SM], (shape(RX * NP, LANES), shape(groups...  37 us
    all_to_all x1, blocking collectives, on_device(): got = lax.all_to_all(msg.reshape(tiles, 8, 128), 'space', 0, 0, tiled=True)  35.6 us
    all_to_all x1, blocking collectives, on_device(): lax.all_to_all(msg.reshape(groups, KINDS * ROWS, LANES), 'obs', 0, 0, til...  22.8 us
    all_to_all x1, blocking collectives, on_device(): lax.all_to_all(msg.reshape(groups, 24, LANES), 'obs', 0, 0, tiled=True)  12.5 us
    all_to_all x1, blocking collectives, on_device(): got = lax.all_to_all(msg.reshape(groups, 8, 128), 'obs', 0, 0, tiled=True)  11.9 us
    pallas_call x1, Pallas kernels, on_device(): call(lambda *refs: basis_kernel(*refs, scale=scale), [VM] * 2, shape(grou...  5.21 us
    pallas_call x1, Pallas kernels, on_device(): call(prepare_kernel, [VM] * 4 + [SM] * 2, (shape(KINDS * LV * RX, NY), sh...  4.67 us
    ppermute x1, waiting for transfers between devices, on_device(): high = lax.ppermute(down, 'space', [(i + 1, i) for i in range(tiles - 1)])  3.85 us
  transfers between devices with their start and end apart: 2, of which 1 were waited for; matrix products, arithmetic and copies ran while one was open for 0% of the time, Pallas kernels for 0%

profile of v2, /device:TPU:2, one launch (start us, length us, event | category | flops | bytes accessed | tf_op | source)
XLA Modules:
  0.0 145.8 jit_solution(3951874209173645323)
XLA Ops:
  1.3 0.7 add_bitcast_fusion.place
  1.9 4.7 %shard_map.68 = (f32[320,256]{1,0:T(8,128)}, f32[512,128]{1,0:T(8,128)}, f32[288,128]{1,0:T(8,128)}, f32[288,128]{1,0:T(8,128)}) custom-call(f32[2048,256]{1,0:T(8,128)} %bitcast.17, f32[256,256]{1,0:T(8,128)} %bitcast.22, s32[1,256]{1,0:T(1,128)} %cells.1, f32[1,256]{1,0:T(1,128)} %weight.1, s32[1,1]{1,0:T(1,128)S(6)} %copy.7.count, ...), custom_call_target="tpu_custom_call" | custom-call | tf_op jit(solution)/shard_map/pallas_call | solution.py:395
  6.6 1.7 %collective-permute-start = (f32[288,128]{1,0:T(8,128)}, f32[288,128]{1,0:T(8,128)S(1)}, u32[]{:S(2)}, u32[]{:S(2)}) collective-permute-start(f32[288,128]{1,0:T(8,128)} %get-tuple-element.11), channel_id=1, source_target_pairs={{0,1},{1,2},{2,3},{3,4},{4,5},{5,6},{6,7},{7,8},{8,9},{9,10},{10,1... | collective-permute-start | bytes 442376 | tf_op jit(solution)/shard_map/ppermute | solution.py:412
  8.4 1.3 collective-permute-start.1
  9.7 0.0 collective-permute-done.low
  9.7 0.0 copy-start
  9.7 3.8 %collective-permute-done.1.high = f32[288,128]{1,0:T(8,128)S(1)} collective-permute-done((f32[288,128]{1,0:T(8,128)}, f32[288,128]{1,0:T(8,128)S(1)}, u32[]{:S(2)}, u32[]{:S(2)}) %collective-permute-start.1) | collective-permute-done | bytes 147488 | tf_op jit(solution)/shard_map/ppermute | solution.py:413
  13.5 0.0 copy-start.1
  13.5 0.0 copy-done
  13.5 0.7 copy-done.1
  14.2 3.2 %shard_map.69 = f32[1920,128]{1,0:T(8,128)} custom-call(f32[320,256]{1,0:T(8,128)} %get-tuple-element.10.raw, f32[288,128]{1,0:T(8,128)} %copy-done, f32[288,128]{1,0:T(8,128)} %copy-done.1), custom_call_target="tpu_custom_call" | custom-call | tf_op jit(solution)/shard_map/pallas_call | solution.py:414
  17.4 22.8 %all_to_all.20 = f32[16,120,128]{2,1,0:T(8,128)} all-to-all(f32[16,120,128]{2,1,0:T(8,128)} %bitcast.16), channel_id=1, replica_groups=mesh['obs'=16,'space'=32] {'obs'}, dimensions={0} | all-to-all | bytes 1966080 | tf_op jit(solution)/shard_map/all_to_all | solution.py:420
  40.2 37.0 %shard_map.70 = (f32[512,128]{1,0:T(8,128)}, f32[128,128]{1,0:T(8,128)}) custom-call(f32[1920,128]{1,0:T(8,128)} %bitcast.15, f32[512,128]{1,0:T(8,128)} %get-tuple-element.13.patch, f32[288,128]{1,0:T(8,128)} %copy-done, f32[288,128]{1,0:T(8,128)} %copy-done.1, s32[1,3]{1,0:T(1,128)} %add_bitcast_fusion.place), custom_call_target="tpu_custom_call" | custom-call | tf_op jit(solution)/shard_map/pallas_call | solution.py:423
  77.2 11.9 %all_to_all.21 = f32[16,8,128]{2,1,0:T(8,128)} all-to-all(f32[16,8,128]{2,1,0:T(8,128)} %bitcast.24), channel_id=1, replica_groups=mesh['obs'=16,'space'=32] {'obs'}, dimensions={0} | all-to-all | bytes 131072 | tf_op jit(solution)/shard_map/all_to_all | solution.py:441
  89.1 1.5 %shard_map.71 = f32[256,128]{1,0:T(8,128)} custom-call(f32[128,128]{1,0:T(8,128)} %bitcast.23), custom_call_target="tpu_custom_call" | custom-call | tf_op jit(solution)/shard_map/pallas_call | solution.py:442
  90.6 35.6 %all_to_all.22 = f32[32,8,128]{2,1,0:T(8,128)} all-to-all(f32[32,8,128]{2,1,0:T(8,128)} %bitcast.20), channel_id=1, replica_groups=mesh['obs'=16,'space'=32] {'space'}, dimensions={0} | all-to-all | bytes 262144 | tf_op jit(solution)/shard_map/all_to_all | solution.py:443
  126.2 5.2 %shard_map.72 = f32[384,128]{1,0:T(8,128)} custom-call(f32[256,128]{1,0:T(8,128)} %bitcast.21, f32[512,128]{1,0:T(8,128)} %get-tuple-element.15.refs_1_), custom_call_target="tpu_custom_call" | custom-call | tf_op jit(solution)/shard_map/pallas_call | solution.py:445
  131.4 12.5 %all_to_all.23 = f32[16,24,128]{2,1,0:T(8,128)} all-to-all(f32[16,24,128]{2,1,0:T(8,128)} %bitcast.19), channel_id=1, replica_groups=mesh['obs'=16,'space'=32] {'obs'}, dimensions={0} | all-to-all | bytes 393216 | tf_op jit(solution)/shard_map/all_to_all | solution.py:448
  143.9 1.9 %shard_map.73 = (f32[128,256]{1,0:T(8,128)}, f32[32,32]{1,0:T(8,128)}) custom-call(f32[384,128]{1,0:T(8,128)} %bitcast.18), custom_call_target="tpu_custom_call" | custom-call | tf_op jit(solution)/shard_map/pallas_call | solution.py:450
Async XLA Ops:
  6.6 3.0 %collective-permute-start = (f32[288,128]{1,0:T(8,128)}, f32[288,128]{1,0:T(8,128)S(1)}, u32[]{:S(2)}, u32[]{:S(2)}) collective-permute-start(f32[288,128]{1,0:T(8,128)} %get-tuple-element.11), channel_id=1, source_target_pairs={{0,1},{1,2},{2,3},{3,4},{4,5},{5,6},{6,7},{7,8},{8,9},{9,10},{10,1... | collective-permute-start | bytes 442376 | tf_op jit(solution)/shard_map/ppermute | solution.py:412
  8.4 5.2 %collective-permute-start.1 = (f32[288,128]{1,0:T(8,128)}, f32[288,128]{1,0:T(8,128)S(1)}, u32[]{:S(2)}, u32[]{:S(2)}) collective-permute-start(f32[288,128]{1,0:T(8,128)} %get-tuple-element.12), channel_id=1, source_target_pairs={{1,0},{2,1},{3,2},{4,3},{5,4},{6,5},{7,6},{8,7},{9,8},{10,9},{11,1... | collective-permute-start | bytes 442376 | tf_op jit(solution)/shard_map/ppermute | solution.py:413
  9.7 3.9 %copy-start = (f32[288,128]{1,0:T(8,128)}, f32[288,128]{1,0:T(8,128)S(1)}, u32[]{:S(2)}) copy-start(f32[288,128]{1,0:T(8,128)S(1)} %collective-permute-done.low) | copy-start | bytes 442372
  13.5 0.7 copy-start.1

commit v3 on v2

--- a/solution.py
+++ b/solution.py
@@ -20,8 +20,10 @@
 HALO = 4
 ROWS = RX + 2 * HALO
 LANES = 128
+GROUP = LANES // WIN
 PAD = 8
 UNROLL = 4
+SLOT = ROWS + 2 * PAD
 KINDS = 5
 SIDE = KINDS * LV * HALO
 MSG = 2 * SIDE + NP * HALO
@@ -29,6 +31,10 @@
 
 def iota(shape, dim):
     return lax.broadcasted_iota(jnp.int32, shape, dim)
+
+
+def aligned(row):
+    return pl.multiple_of(row, 8)
 
 
 def live_weights(weight_ref, count_ref):
@@ -56,25 +62,19 @@
     shape = tiles[0][0].shape
     lane = iota(shape, 1)
     col = first + lane % WIN
-    halves = []
-    for h in range(2):
-        start = first - h * LANES
-        if isinstance(first, int) and not (-WIN < start < LANES):
-            halves.append(None)
-            continue
-        acc = jnp.zeros(shape, F32)
-        for l in range(LV):
-            shift = l * WIN - start
-            shift = shift % LANES if isinstance(first, int) else (shift + 2 * LANES) % LANES
-            acc = jnp.where(lane // WIN == l, pltpu.roll(tiles[l][h], shift, 1), acc)
-        halves.append(acc)
-    if halves[0] is None:
-        value = halves[1]
-    elif halves[1] is None:
-        value = halves[0]
-    else:
-        value = jnp.where(col < LANES, halves[0], halves[1])
-    return jnp.where((col >= 0) & (col < NY), value, 0.0)
+    acc = None
+    for k, (lo, hi) in enumerate(tiles):
+        if isinstance(first, int) and first + WIN <= LANES:
+            both = lo
+        elif isinstance(first, int) and first >= LANES:
+            both = hi
+        else:
+            both = jnp.where((lane >= first) & (lane < first + WIN), lo, hi)
+        shift = k * WIN - first + 2 * LANES
+        shift = shift % LANES if isinstance(first, int) else lax.rem(shift, LANES)
+        both = pltpu.roll(both, shift, 1)
+        acc = both if acc is None else jnp.where(lane // WIN == k, both, acc)
+    return jnp.where((col >= 0) & (col < NY), acc, 0.0)
 
 
 def prepare_kernel(probes, wind, cells, weight, count, place, raw, patch, up, down):
@@ -86,21 +86,22 @@
     )
 
     def one(p, _):
-        for xt in range(2):
-            tiles = [
-                [
-                    probes[
-                        pl.ds(pl.multiple_of((p * LV + l) * RX + 8 * xt, 8), 8),
-                        pl.ds(h * LANES, LANES),
+        for l in range(LV):
+            for xt in range(2):
+                tiles = [
+                    [
+                        probes[
+                            pl.ds(aligned(((p * GROUP + k) * LV + l) * RX + 8 * xt), 8),
+                            pl.ds(h * LANES, LANES),
+                        ]
+                        for h in range(2)
                     ]
-                    for h in range(2)
+                    for k in range(GROUP)
                 ]
-                for l in range(LV)
-            ]
-            patch[pl.ds(pl.multiple_of(p * RX + 8 * xt, 8), 8), :] = window(tiles, first)
+                patch[pl.ds(aligned((p * LV + l) * RX + 8 * xt), 8), :] = window(tiles, first)
         return 0
 
-    lax.fori_loop(0, NP, one, 0, unroll=2)
+    lax.fori_loop(0, NP // GROUP, one, 0)
     for out, start in ((up, RX - HALO), (down, 0)):
         for h in range(2):
             for i in range(KINDS * LV):
@@ -148,121 +149,152 @@
     return lax.dot_general(a, b, (dims, ((), ())), precision=HIGH, preferred_element_type=F32)
 
 
-def aligned(row):
-    return pl.multiple_of(row, 8)
+def level_sum(c, l):
+    if l == 0:
+        return c[1]
+    if l == LV - 1:
+        return c[l - 1]
+    return c[l - 1] + c[l + 1]
+
+
+def swap_groups(v):
+    lane = iota(v[0].shape, 1)
+    low, even = lane < 64, lane // 32 % 2 == 0
+
+    def half(w):
+        return pltpu.roll(w, 64, 1)
+
+    x = [
+        jnp.where(low, v[0], half(v[2])),
+        jnp.where(low, v[1], half(v[3])),
+        jnp.where(low, half(v[0]), v[2]),
+        jnp.where(low, half(v[1]), v[3]),
+    ]
+    out = []
+    for a in (0, 2):
+        out.append(jnp.where(even, x[a], pltpu.roll(x[a + 1], 32, 1)))
+        out.append(jnp.where(even, pltpu.roll(x[a], 96, 1), x[a + 1]))
+    return out
 
 
 def patch_kernel(
-    got, patch, low, high, place, share, msg, u, au, dx, dy, cf, t1, t2, va, pa, qa, s
+    got, patch, low, high, place, share, msg, u, au, dx, dy, cf, t1, t2, va, pa, qa, s, om
 ):
     t, tiles, o = place[0, 0], place[0, 1], place[0, 2]
     lane = iota((8, LANES), 1)
-    plus_level = jnp.where(lane < LANES - WIN, 0.1, 0.0)
-    minus_level = jnp.where(lane >= WIN, 0.1, 0.0)
     col = o * OWN - MARGIN + lane % WIN
     inside = []
     for i in range(3):
         row = t * RX - HALO + 8 * i + iota((8, LANES), 0)
         inside.append((row >= 0) & (row < tiles * RX) & (col >= 0) & (col < NY))
 
-    def levels(c):
-        return plus_level * pltpu.roll(c, LANES - WIN, 1) + minus_level * pltpu.roll(c, WIN, 1)
-
     def right(c):
         return pltpu.roll(c, LANES - 1, 1)
 
     def left(c):
         return pltpu.roll(c, 1, 1)
+
+    def levels(c, l):
+        return 0.2 * c[l] + 0.1 * level_sum(c, l)
 
     edge = jnp.zeros((PAD, LANES), F32)
     for ref in (u, va, pa, qa):
         ref[pl.ds(0, PAD), :] = edge
         ref[pl.ds(PAD + NP * ROWS, PAD), :] = edge
-    for j in range(4):
-        cf[pl.ds(j * (ROWS + 2 * PAD), PAD), :] = edge
-        cf[pl.ds(j * (ROWS + 2 * PAD) + PAD + ROWS, PAD), :] = edge
-    for ref in (t1, t2):
-        for j in range(UNROLL):
-            ref[pl.ds(j * (ROWS + 2 * PAD), PAD), :] = edge
-            ref[pl.ds(j * (ROWS + 2 * PAD) + PAD + ROWS, PAD), :] = edge
-    for p in range(NP):
-        base = PAD + p * ROWS
-        u[pl.ds(base, HALO), :] = low[pl.ds(2 * SIDE + p * HALO, HALO), :]
-        u[pl.ds(base + HALO, RX), :] = patch[pl.ds(p * RX, RX), :]
-        u[pl.ds(base + HALO + RX, HALO), :] = high[pl.ds(2 * SIDE + p * HALO, HALO), :]
+    for ref, n in ((cf, 2 * LV), (t1, UNROLL * LV), (t2, UNROLL * LV)):
+        for j in range(n):
+            ref[pl.ds(j * SLOT, PAD), :] = edge
+            ref[pl.ds(j * SLOT + PAD + ROWS, PAD), :] = edge
+    for f in range(NP):
+        base = PAD + f * ROWS
+        u[pl.ds(base, HALO), :] = low[pl.ds(2 * SIDE + f * HALO, HALO), :]
+        u[pl.ds(base + HALO, RX), :] = patch[pl.ds(f * RX, RX), :]
+        u[pl.ds(base + HALO + RX, HALO), :] = high[pl.ds(2 * SIDE + f * HALO, HALO), :]
 
     def shared(p, _):
         for i in range(3):
-            at = aligned(p * ROWS + 8 * i)
-            c = u[pl.ds(at + PAD, 8), :]
-            xp, xm = u[pl.ds(at + PAD + 1, 8), :], u[pl.ds(at + PAD - 1, 8), :]
-            yp, ym = right(c), left(c)
-            mean = 0.2 * c + 0.15 * ((xp + xm) + (yp + ym)) + levels(c)
-            au[pl.ds(at, 8), :] = jnp.where(inside[i], mean, 0.0)
-            dx[pl.ds(at, 8), :] = jnp.where(inside[i], xp - xm, 0.0)
-            dy[pl.ds(at, 8), :] = jnp.where(inside[i], yp - ym, 0.0)
-            for ref in (va, pa, qa):
-                ref[pl.ds(at + PAD, 8), :] = edge
+            at = [aligned((p * LV + l) * ROWS + 8 * i) for l in range(LV)]
+            c = [u[pl.ds(at[l] + PAD, 8), :] for l in range(LV)]
+            for l in range(LV):
+                xp, xm = u[pl.ds(at[l] + PAD + 1, 8), :], u[pl.ds(at[l] + PAD - 1, 8), :]
+                yp, ym = right(c[l]), left(c[l])
+                mean = levels(c, l) + 0.15 * ((xp + xm) + (yp + ym))
+                here = pl.ds(at[l], 8)
+                au[here, :] = jnp.where(inside[i], mean, 0.0)
+                dx[here, :] = jnp.where(inside[i], xp - xm, 0.0)
+                dy[here, :] = jnp.where(inside[i], yp - ym, 0.0)
+                for ref in (va, pa, qa):
+                    ref[pl.ds(at[l] + PAD, 8), :] = edge
         return 0
 
-    lax.fori_loop(0, NP, shared, 0, unroll=4)
-
-    def coef(j, i, off=0):
-        return cf[pl.ds(j * (ROWS + 2 * PAD) + PAD + 8 * i + off, 8), :]
+    lax.fori_loop(0, NP // GROUP, shared, 0)
+
+    def coef(j, l, i, off=0):
+        return cf[pl.ds((j * LV + l) * SLOT + PAD + 8 * i + off, 8), :]
 
     def one_window(g, _):
         base = g * (KINDS * ROWS)
-
-        def of(kind, i):
-            return got[pl.ds(aligned(base + kind * ROWS + 8 * i), 8), :]
-
         for i in range(3):
-            a, b = of(2, i), of(3, i)
-            for j, value in enumerate((0.15 - a, 0.15 + a, 0.15 - b, 0.15 + b)):
-                cf[pl.ds(j * (ROWS + 2 * PAD) + PAD + 8 * i, 8), :] = value
+            for kind in range(KINDS):
+                tile = got[pl.ds(aligned(base + kind * ROWS + 8 * i), 8), :]
+                for l in range(LV):
+                    m = jnp.take_along_axis(tile, l * WIN + lane % WIN, axis=1)
+                    if kind in (2, 3):
+                        pair = ((2 * kind - 4, 0.15 - m), (2 * kind - 3, 0.15 + m))
+                    else:
+                        pair = (({0: 4, 1: 5, 4: 6}[kind], m),)
+                    for j, value in pair:
+                        cf[pl.ds((j * LV + l) * SLOT + PAD + 8 * i, 8), :] = value
 
         def some(step, _):
             slots = range(UNROLL)
-            at = [[aligned((step * UNROLL + q) * ROWS + 8 * i) for i in range(3)] for q in slots]
-            slot = [[q * (ROWS + 2 * PAD) + PAD + 8 * i for i in range(3)] for q in slots]
+
+            def at(q, l, i):
+                return aligned(((step * UNROLL + q) * LV + l) * ROWS + 8 * i)
+
+            def slot(q, l, i, off=0):
+                return pl.ds((q * LV + l) * SLOT + PAD + 8 * i + off, 8)
+
             for i in range(3):
-                a, b = of(0, i), of(1, i)
-                for q in slots:
-                    here = pl.ds(at[q][i], 8)
-                    t1[pl.ds(slot[q][i], 8), :] = au[here, :] - a * dx[here, :] - b * dy[here, :]
+                for l in range(LV):
+                    a, b = coef(4, l, i), coef(5, l, i)
+                    for q in slots:
+                        here = pl.ds(at(q, l, i), 8)
+                        t1[slot(q, l, i), :] = au[here, :] - a * dx[here, :] - b * dy[here, :]
             for i in range(3):
-                cxp, cxm, cyp, cym = (coef(j, i) for j in range(4))
-                w = of(4, i)
-                for q in slots:
-                    c = t1[pl.ds(slot[q][i], 8), :]
-                    r = 0.2 * c + levels(c)
-                    r += cxp * t1[pl.ds(slot[q][i] + 1, 8), :]
-                    r += cxm * t1[pl.ds(slot[q][i] - 1, 8), :]
-                    r += cyp * right(c) + cym * left(c)
-                    t2[pl.ds(slot[q][i], 8), :] = w * r
+                c = [[t1[slot(q, l, i), :] for l in range(LV)] for q in slots]
+                for l in range(LV):
+                    cxp, cxm, cyp, cym = (coef(j, l, i) for j in range(4))
+                    w = coef(6, l, i)
+                    for q in slots:
+                        r = levels(c[q], l)
+                        r += cxp * t1[slot(q, l, i, 1), :] + cxm * t1[slot(q, l, i, -1), :]
+                        r += cyp * right(c[q][l]) + cym * left(c[q][l])
+                        t2[slot(q, l, i), :] = w * r
             for i in range(3):
-                cxp, cxm, cyp, cym = coef(0, i, -1), coef(1, i, 1), coef(2, i), coef(3, i)
-                a, b = of(0, i), of(1, i)
-                for q in slots:
-                    c = t2[pl.ds(slot[q][i], 8), :]
-                    r = 0.2 * c + levels(c)
-                    r += cxm * t2[pl.ds(slot[q][i] + 1, 8), :]
-                    r += cxp * t2[pl.ds(slot[q][i] - 1, 8), :]
-                    r += right(cym * c) + left(cyp * c)
-                    here = pl.ds(at[q][i] + PAD, 8)
-                    va[here, :] += r
-                    pa[here, :] += a * r
-                    qa[here, :] += b * r
+                c = [[t2[slot(q, l, i), :] for l in range(LV)] for q in slots]
+                for l in range(LV):
+                    cxp, cxm = coef(0, l, i, -1), coef(1, l, i, 1)
+                    cyp, cym = coef(2, l, i), coef(3, l, i)
+                    a, b = coef(4, l, i), coef(5, l, i)
+                    for q in slots:
+                        r = levels(c[q], l)
+                        r += cxm * t2[slot(q, l, i, 1), :] + cxp * t2[slot(q, l, i, -1), :]
+                        r += right(cym * c[q][l]) + left(cyp * c[q][l])
+                        here = pl.ds(at(q, l, i) + PAD, 8)
+                        va[here, :] += r
+                        pa[here, :] += a * r
+                        qa[here, :] += b * r
             return 0
 
-        lax.fori_loop(0, NP // UNROLL, some, 0)
+        lax.fori_loop(0, NP // GROUP // UNROLL, some, 0)
         return 0
 
     lax.fori_loop(0, got.shape[0] // (KINDS * ROWS), one_window, 0)
 
-    def mask(p, _):
+    def mask(f, _):
         for i in range(3):
-            at = pl.ds(aligned(PAD + p * ROWS + 8 * i), 8)
+            at = pl.ds(aligned(PAD + f * ROWS + 8 * i), 8)
             for ref in (va, pa, qa):
                 ref[at, :] = jnp.where(inside[i], ref[at, :], 0.0)
         return 0
@@ -272,24 +304,37 @@
 
     def last(p, _):
         for i in range(2):
-            at = aligned(PAD + p * ROWS + 8 * i) + HALO
-            c, q = va[pl.ds(at, 8), :], qa[pl.ds(at, 8), :]
-            r = 0.2 * c + levels(c)
-            r += 0.15 * ((va[pl.ds(at + 1, 8), :] + va[pl.ds(at - 1, 8), :]) + (right(c) + left(c)))
-            r += (pa[pl.ds(at + 1, 8), :] - pa[pl.ds(at - 1, 8), :]) + (right(q) - left(q))
-            s[pl.ds(aligned(p * RX + 8 * i), 8), :] = jnp.where(core_lane, r, 0.0)
+            at = [aligned(PAD + (p * LV + l) * ROWS + 8 * i) + HALO for l in range(LV)]
+            c = [va[pl.ds(at[l], 8), :] for l in range(LV)]
+            done = []
+            for l in range(LV):
+                q = qa[pl.ds(at[l], 8), :]
+                r = levels(c, l)
+                xs = va[pl.ds(at[l] + 1, 8), :] + va[pl.ds(at[l] - 1, 8), :]
+                r += 0.15 * (xs + (right(c[l]) + left(c[l])))
+                r += (pa[pl.ds(at[l] + 1, 8), :] - pa[pl.ds(at[l] - 1, 8), :]) + (
+                    right(q) - left(q)
+                )
+                done.append(jnp.where(core_lane, r, 0.0))
+            for ref, values in (
+                (s, swap_groups(done)),
+                (om, swap_groups([u[pl.ds(at[l], 8), :] for l in range(LV)])),
+            ):
+                for k in range(GROUP):
+                    ref[pl.ds(aligned((p * GROUP + k) * RX + 8 * i), 8), :] = values[k]
         return 0
 
-    lax.fori_loop(0, NP, last, 0, unroll=4)
-
-    gram = jnp.zeros((NP, LANES), F32)
-    cross = jnp.zeros((NP, LANES), F32)
+    lax.fori_loop(0, NP // GROUP, last, 0)
+
+    both = jnp.zeros((2 * NP, NP), F32)
     for x in range(RX):
         sx = s[pl.ds(x, NP, stride=RX), :]
         share[pl.ds(x * NP, NP), :] = sx
-        four = jnp.concatenate([sx] * 4, axis=0)
-        gram += product(sx, four, ((1,), (1,)))
-        cross += product(u[pl.ds(PAD + HALO + x, NP, stride=ROWS), :], four, ((1,), (1,)))
+        rows = jnp.concatenate([sx, om[pl.ds(x, NP, stride=RX), :]], axis=0)
+        both += product(rows, sx, ((1,), (1,)))
+    spread = (iota((NP, LANES), 1) % NP == iota((NP, LANES), 0)).astype(F32)
+    both = product(both, spread, ((1,), (0,)))
+    gram, cross = both[:NP], both[NP:]
     shifted = pltpu.roll(cross, 16, 1)
     lane = iota((8, 128), 1)
     packed = jnp.zeros((8, 128), F32)
@@ -429,12 +474,13 @@
             field,
             field,
             field,
-            pltpu.VMEM((4 * (ROWS + 2 * PAD), LANES), F32),
-            pltpu.VMEM((UNROLL * (ROWS + 2 * PAD), LANES), F32),
-            pltpu.VMEM((UNROLL * (ROWS + 2 * PAD), LANES), F32),
+            pltpu.VMEM((7 * LV * SLOT, LANES), F32),
+            pltpu.VMEM((UNROLL * LV * SLOT, LANES), F32),
+            pltpu.VMEM((UNROLL * LV * SLOT, LANES), F32),
             padded,
             padded,
             padded,
+            pltpu.VMEM((NP * RX, LANES), F32),
             pltpu.VMEM((NP * RX, LANES), F32),
         ),
     )(got.reshape(groups * KINDS * ROWS, LANES), patch, low, high, place)

time: 146 us -> 128 us (0.88)
  Pallas kernels: 53.5 us -> 35.2 us
    pallas_call x1, Pallas kernels: 37 us -> 19.6 us  [on_device(): call(patch_kernel, [VM] * 4 + [SM], (shape(RX * NP, LANES), shape(groups...]
where the time goes in v3:
time: 128 us; the launch traced here: 127 us
  blocking collectives  82.8 us (65%)
  Pallas kernels  35.2 us (28%)
  waiting for transfers between devices  3.85 us (3%)
  starting transfers between devices  3.03 us (2%)
  between operations  1.32 us (1%)
    all_to_all x1, blocking collectives, on_device(): got = lax.all_to_all(msg.reshape(tiles, 8, 128), 'space', 0, 0, tiled=True)  35.6 us
    all_to_all x1, blocking collectives, on_device(): lax.all_to_all(msg.reshape(groups, KINDS * ROWS, LANES), 'obs', 0, 0, til...  22.8 us
    pallas_call x1, Pallas kernels, on_device(): call(patch_kernel, [VM] * 4 + [SM], (shape(RX * NP, LANES), shape(groups...  19.6 us
    all_to_all x1, blocking collectives, on_device(): lax.all_to_all(msg.reshape(groups, 24, LANES), 'obs', 0, 0, tiled=True)  12.5 us
    all_to_all x1, blocking collectives, on_device(): got = lax.all_to_all(msg.reshape(groups, 8, 128), 'obs', 0, 0, tiled=True)  11.9 us
    pallas_call x1, Pallas kernels, on_device(): call(lambda *refs: basis_kernel(*refs, scale=scale), [VM] * 2, shape(grou...  5.21 us
    ppermute x1, waiting for transfers between devices, on_device(): high = lax.ppermute(down, 'space', [(i + 1, i) for i in range(tiles - 1)])  3.85 us
    pallas_call x1, Pallas kernels, on_device(): call(prepare_kernel, [VM] * 4 + [SM] * 2, (shape(KINDS * LV * RX, NY), sh...  3.76 us
  transfers between devices with their start and end apart: 2, of which 1 were waited for; matrix products, arithmetic and copies ran while one was open for 0% of the time, Pallas kernels for 0%

profile of v3, /device:TPU:2, one launch (start us, length us, event | category | flops | bytes accessed | tf_op | source)
XLA Modules:
  0.0 127.5 jit_solution(1387940232050765264)
XLA Ops:
  1.3 0.7 add_bitcast_fusion.place
  1.9 3.8 %shard_map.68 = (f32[320,256]{1,0:T(8,128)}, f32[512,128]{1,0:T(8,128)}, f32[288,128]{1,0:T(8,128)}, f32[288,128]{1,0:T(8,128)}) custom-call(f32[2048,256]{1,0:T(8,128)} %bitcast.17, f32[256,256]{1,0:T(8,128)} %bitcast.22, s32[1,256]{1,0:T(1,128)} %cells.1, f32[1,256]{1,0:T(1,128)} %weight.1, s32[1,1]{1,0:T(1,128)S(6)} %copy.7.count, ...), custom_call_target="tpu_custom_call" | custom-call | tf_op jit(solution)/shard_map/pallas_call | solution.py:440
  5.7 1.7 %collective-permute-start = (f32[288,128]{1,0:T(8,128)}, f32[288,128]{1,0:T(8,128)S(1)}, u32[]{:S(2)}, u32[]{:S(2)}) collective-permute-start(f32[288,128]{1,0:T(8,128)} %get-tuple-element.11), channel_id=1, source_target_pairs={{0,1},{1,2},{2,3},{3,4},{4,5},{5,6},{6,7},{7,8},{8,9},{9,10},{10,1... | collective-permute-start | bytes 442376 | tf_op jit(solution)/shard_map/ppermute | solution.py:457
  7.4 1.3 %collective-permute-start.1 = (f32[288,128]{1,0:T(8,128)}, f32[288,128]{1,0:T(8,128)S(1)}, u32[]{:S(2)}, u32[]{:S(2)}) collective-permute-start(f32[288,128]{1,0:T(8,128)} %get-tuple-element.12), channel_id=1, source_target_pairs={{1,0},{2,1},{3,2},{4,3},{5,4},{6,5},{7,6},{8,7},{9,8},{10,9},{11,1... | collective-permute-start | bytes 442376 | tf_op jit(solution)/shard_map/ppermute | solution.py:458
  8.7 0.0 collective-permute-done.low
  8.7 0.0 copy-start
  8.8 3.8 %collective-permute-done.1.high = f32[288,128]{1,0:T(8,128)S(1)} collective-permute-done((f32[288,128]{1,0:T(8,128)}, f32[288,128]{1,0:T(8,128)S(1)}, u32[]{:S(2)}, u32[]{:S(2)}) %collective-permute-start.1) | collective-permute-done | bytes 147488 | tf_op jit(solution)/shard_map/ppermute | solution.py:458
  12.6 0.0 copy-start.1
  12.6 0.0 copy-done
  12.6 0.7 copy-done.1
  13.3 3.2 %shard_map.69 = f32[1920,128]{1,0:T(8,128)} custom-call(f32[320,256]{1,0:T(8,128)} %get-tuple-element.10.raw, f32[288,128]{1,0:T(8,128)} %copy-done, f32[288,128]{1,0:T(8,128)} %copy-done.1), custom_call_target="tpu_custom_call" | custom-call | tf_op jit(solution)/shard_map/pallas_call | solution.py:459
  16.5 22.8 %all_to_all.20 = f32[16,120,128]{2,1,0:T(8,128)} all-to-all(f32[16,120,128]{2,1,0:T(8,128)} %bitcast.16), channel_id=1, replica_groups=mesh['obs'=16,'space'=32] {'obs'}, dimensions={0} | all-to-all | bytes 1966080 | tf_op jit(solution)/shard_map/all_to_all | solution.py:465
  39.3 19.6 %shard_map.70 = (f32[512,128]{1,0:T(8,128)}, f32[128,128]{1,0:T(8,128)}) custom-call(f32[1920,128]{1,0:T(8,128)} %bitcast.15, f32[512,128]{1,0:T(8,128)} %get-tuple-element.13.patch, f32[288,128]{1,0:T(8,128)} %copy-done, f32[288,128]{1,0:T(8,128)} %copy-done.1, s32[1,3]{1,0:T(1,128)} %add_bitcast_fusion.place), custom_call_target="tpu_custom_call" | custom-call | tf_op jit(solution)/shard_map/pallas_call | solution.py:468
  58.8 11.9 %all_to_all.21 = f32[16,8,128]{2,1,0:T(8,128)} all-to-all(f32[16,8,128]{2,1,0:T(8,128)} %bitcast.24), channel_id=1, replica_groups=mesh['obs'=16,'space'=32] {'obs'}, dimensions={0} | all-to-all | bytes 131072 | tf_op jit(solution)/shard_map/all_to_all | solution.py:487
  70.7 1.5 %shard_map.71 = f32[256,128]{1,0:T(8,128)} custom-call(f32[128,128]{1,0:T(8,128)} %bitcast.23), custom_call_target="tpu_custom_call" | custom-call | tf_op jit(solution)/shard_map/pallas_call | solution.py:488
  72.2 35.6 %all_to_all.22 = f32[32,8,128]{2,1,0:T(8,128)} all-to-all(f32[32,8,128]{2,1,0:T(8,128)} %bitcast.20), channel_id=1, replica_groups=mesh['obs'=16,'space'=32] {'space'}, dimensions={0} | all-to-all | bytes 262144 | tf_op jit(solution)/shard_map/all_to_all | solution.py:489
  107.8 5.2 %shard_map.72 = f32[384,128]{1,0:T(8,128)} custom-call(f32[256,128]{1,0:T(8,128)} %bitcast.21, f32[512,128]{1,0:T(8,128)} %get-tuple-element.15.refs_1_), custom_call_target="tpu_custom_call" | custom-call | tf_op jit(solution)/shard_map/pallas_call | solution.py:491
  113.0 12.5 %all_to_all.23 = f32[16,24,128]{2,1,0:T(8,128)} all-to-all(f32[16,24,128]{2,1,0:T(8,128)} %bitcast.19), channel_id=1, replica_groups=mesh['obs'=16,'space'=32] {'obs'}, dimensions={0} | all-to-all | bytes 393216 | tf_op jit(solution)/shard_map/all_to_all | solution.py:494
  125.5 1.9 %shard_map.73 = (f32[128,256]{1,0:T(8,128)}, f32[32,32]{1,0:T(8,128)}) custom-call(f32[384,128]{1,0:T(8,128)} %bitcast.18), custom_call_target="tpu_custom_call" | custom-call | tf_op jit(solution)/shard_map/pallas_call | solution.py:496
Async XLA Ops:
  5.7 3.0 %collective-permute-start = (f32[288,128]{1,0:T(8,128)}, f32[288,128]{1,0:T(8,128)S(1)}, u32[]{:S(2)}, u32[]{:S(2)}) collective-permute-start(f32[288,128]{1,0:T(8,128)} %get-tuple-element.11), channel_id=1, source_target_pairs={{0,1},{1,2},{2,3},{3,4},{4,5},{5,6},{6,7},{7,8},{8,9},{9,10},{10,1... | collective-permute-start | bytes 442376 | tf_op jit(solution)/shard_map/ppermute | solution.py:457
  7.4 5.2 %collective-permute-start.1 = (f32[288,128]{1,0:T(8,128)}, f32[288,128]{1,0:T(8,128)S(1)}, u32[]{:S(2)}, u32[]{:S(2)}) collective-permute-start(f32[288,128]{1,0:T(8,128)} %get-tuple-element.12), channel_id=1, source_target_pairs={{1,0},{2,1},{3,2},{4,3},{5,4},{6,5},{7,6},{8,7},{9,8},{10,9},{11,1... | collective-permute-start | bytes 442376 | tf_op jit(solution)/shard_map/ppermute | solution.py:458
  8.7 3.9 %copy-start = (f32[288,128]{1,0:T(8,128)}, f32[288,128]{1,0:T(8,128)S(1)}, u32[]{:S(2)}) copy-start(f32[288,128]{1,0:T(8,128)S(1)} %collective-permute-done.low) | copy-start | bytes 442372
  12.6 0.7 copy-start.1

commit v4 on v3

--- a/solution.py
+++ b/solution.py
@@ -77,8 +77,8 @@
     return jnp.where((col >= 0) & (col < NY), acc, 0.0)
 
 
-def prepare_kernel(probes, wind, cells, weight, count, place, raw, patch, up, down):
-    first = place[0, 2] * OWN - MARGIN
+def prepare_kernel(probes, wind, cells, weight, count, raw, patch, up, down):
+    first = lax.axis_index("obs") * OWN - MARGIN
     for i in range(4 * LV):
         raw[pl.ds(i * RX, RX), :] = 0.5 * wind[pl.ds(i * RX, RX), :]
     raw[pl.ds(4 * LV * RX, LV * RX), :] = weight_map(
@@ -112,33 +112,36 @@
             out[pl.ds(2 * SIDE + p * HALO, HALO), :] = patch[pl.ds(p * RX + start, HALO), :]
 
 
-def message_kernel(raw, low, high, msg, edge):
+def own_kernel(raw, own):
+    for kind in range(KINDS):
+        for xt in range(2):
+            tiles = [
+                [
+                    raw[pl.ds((kind * LV + l) * RX + 8 * xt, 8), pl.ds(h * LANES, LANES)]
+                    for h in range(2)
+                ]
+                for l in range(LV)
+            ]
+            for d in range(NY // OWN):
+                own[pl.ds((d * KINDS + kind) * RX + 8 * xt, 8), :] = window(
+                    tiles, d * OWN - MARGIN
+                )
+
+
+def message_kernel(own, low, high, msg, edge):
     for h in range(2):
         for i in range(KINDS * LV):
             src = pl.ds(h * SIDE + i * HALO, HALO)
             edge[i, h, pl.ds(0, HALO), :] = low[src, :]
             edge[i, h, pl.ds(HALO, HALO), :] = high[src, :]
     for kind in range(KINDS):
-        for xt in range(3):
-            tiles = [
-                [
-                    raw[
-                        pl.ds((kind * LV + l) * RX + 8 * xt, 8), pl.ds(h * LANES, LANES)
-                    ]
-                    if xt < 2
-                    else edge[kind * LV + l, h]
-                    for h in range(2)
-                ]
-                for l in range(LV)
-            ]
-            for d in range(NY // OWN):
-                value = window(tiles, d * OWN - MARGIN)
-                base = (d * KINDS + kind) * ROWS
-                if xt < 2:
-                    msg[pl.ds(base + HALO + 8 * xt, 8), :] = value
-                else:
-                    msg[pl.ds(base, HALO), :] = value[:HALO]
-                    msg[pl.ds(base + HALO + RX, HALO), :] = value[HALO:]
+        tiles = [[edge[kind * LV + l, h] for h in range(2)] for l in range(LV)]
+        for d in range(NY // OWN):
+            value = window(tiles, d * OWN - MARGIN)
+            base = (d * KINDS + kind) * ROWS
+            msg[pl.ds(base, HALO), :] = value[:HALO]
+            msg[pl.ds(base + HALO, RX), :] = own[pl.ds((d * KINDS + kind) * RX, RX), :]
+            msg[pl.ds(base + HALO + RX, HALO), :] = value[HALO:]
 
 
 def all_blocks(t):
@@ -178,9 +181,10 @@
 
 
 def patch_kernel(
-    got, patch, low, high, place, share, msg, u, au, dx, dy, cf, t1, t2, va, pa, qa, s, om
+    got, patch, low, high, share, msg, u, au, dx, dy, cf, t1, t2, va, pa, qa, s, om
 ):
-    t, tiles, o = place[0, 0], place[0, 1], place[0, 2]
+    t, o = lax.axis_index("space"), lax.axis_index("obs")
+    tiles = lax.axis_size("space")
     lane = iota((8, LANES), 1)
     col = o * OWN - MARGIN + lane % WIN
     inside = []
@@ -196,6 +200,9 @@
 
     def levels(c, l):
         return 0.2 * c[l] + 0.1 * level_sum(c, l)
+
+    def tenfold(c, l):
+        return (c[l] + c[l]) + level_sum(c, l)
 
     edge = jnp.zeros((PAD, LANES), F32)
     for ref in (u, va, pa, qa):
@@ -218,11 +225,11 @@
             for l in range(LV):
                 xp, xm = u[pl.ds(at[l] + PAD + 1, 8), :], u[pl.ds(at[l] + PAD - 1, 8), :]
                 yp, ym = right(c[l]), left(c[l])
-                mean = levels(c, l) + 0.15 * ((xp + xm) + (yp + ym))
+                mean = 0.01 * tenfold(c, l) + 0.015 * ((xp + xm) + (yp + ym))
                 here = pl.ds(at[l], 8)
                 au[here, :] = jnp.where(inside[i], mean, 0.0)
-                dx[here, :] = jnp.where(inside[i], xp - xm, 0.0)
-                dy[here, :] = jnp.where(inside[i], yp - ym, 0.0)
+                dx[here, :] = jnp.where(inside[i], 0.1 * (xp - xm), 0.0)
+                dy[here, :] = jnp.where(inside[i], 0.1 * (yp - ym), 0.0)
                 for ref in (va, pa, qa):
                     ref[pl.ds(at[l] + PAD, 8), :] = edge
         return 0
@@ -240,9 +247,10 @@
                 for l in range(LV):
                     m = jnp.take_along_axis(tile, l * WIN + lane % WIN, axis=1)
                     if kind in (2, 3):
-                        pair = ((2 * kind - 4, 0.15 - m), (2 * kind - 3, 0.15 + m))
+                        m = 10.0 * m
+                        pair = ((2 * kind - 4, 1.5 - m), (2 * kind - 3, 1.5 + m))
                     else:
-                        pair = (({0: 4, 1: 5, 4: 6}[kind], m),)
+                        pair = (({0: 4, 1: 5, 4: 6}[kind], 0.1 * m if kind == 4 else m),)
                     for j, value in pair:
                         cf[pl.ds((j * LV + l) * SLOT + PAD + 8 * i, 8), :] = value
 
@@ -267,7 +275,7 @@
                     cxp, cxm, cyp, cym = (coef(j, l, i) for j in range(4))
                     w = coef(6, l, i)
                     for q in slots:
-                        r = levels(c[q], l)
+                        r = tenfold(c[q], l)
                         r += cxp * t1[slot(q, l, i, 1), :] + cxm * t1[slot(q, l, i, -1), :]
                         r += cyp * right(c[q][l]) + cym * left(c[q][l])
                         t2[slot(q, l, i), :] = w * r
@@ -278,7 +286,7 @@
                     cyp, cym = coef(2, l, i), coef(3, l, i)
                     a, b = coef(4, l, i), coef(5, l, i)
                     for q in slots:
-                        r = levels(c[q], l)
+                        r = tenfold(c[q], l)
                         r += cxm * t2[slot(q, l, i, 1), :] + cxp * t2[slot(q, l, i, -1), :]
                         r += right(cym * c[q][l]) + left(cyp * c[q][l])
                         here = pl.ds(at(q, l, i) + PAD, 8)
@@ -371,11 +379,19 @@
     row, lane = iota((NP, 128), 0), iota((NP, 128), 1)
     a = jnp.where((row < 16) & (lane % 32 >= 16), flipped, gram)
     a = jnp.where(lane < NP, a, jnp.where(lane - NP == row, 1.0, 0.0))
-    for j in range(NP - 1):
-        pivot = a[j : j + 1, :]
-        scaled = pivot / a[j : j + 1, j : j + 1]
-        factor = jnp.where(row > j, a[:, j : j + 1], 0.0)
-        a = a - factor * scaled
+    for j in range(0, NP - 2, 2):
+        f0 = jnp.broadcast_to(a[:, j : j + 1], a.shape)
+        f1 = jnp.broadcast_to(a[:, j + 1 : j + 2], a.shape)
+        r0, r1 = a[j : j + 1], a[j + 1 : j + 2]
+        p, q, r = f0[j : j + 1], f0[j + 1 : j + 2], f1[j + 1 : j + 2]
+        inv = 1.0 / (p * r - q * q)
+        s0, s1 = (r * r0 - q * r1) * inv, (p * r1 - q * r0) * inv
+        a = a - jnp.where(row > j + 1, f0 * s0 + f1 * s1, 0.0)
+    above = pltpu.roll(a, 1, 0)
+    left = lane == row - 1
+    p = jnp.sum(jnp.where(left, above, 0.0), axis=1, keepdims=True)
+    q = jnp.sum(jnp.where(left, a, 0.0), axis=1, keepdims=True)
+    a = jnp.where(row % 2 == 1, a - (q / jnp.where(p > 0.0, p, 1.0)) * above, a)
     diag = jnp.sum(jnp.where(lane == row, a, 0.0), axis=1, keepdims=True)
     inverse = jnp.where(lane // 32 == 1, a * (scale / jnp.sqrt(diag)), 0.0)
     inverse = all_blocks(inverse)
@@ -422,7 +438,7 @@
     return jax.ShapeDtypeStruct(dims, F32)
 
 
-def call(kernel, specs, outs, scratch=()):
+def call(kernel, specs, outs, scratch=(), cost=None):
     many = isinstance(outs, tuple)
     return pl.pallas_call(
         kernel,
@@ -430,16 +446,16 @@
         in_specs=specs,
         out_specs=(VM,) * len(outs) if many else VM,
         scratch_shapes=list(scratch),
+        cost_estimate=cost,
+        compiler_params=pltpu.CompilerParams(vmem_limit_bytes=24 << 20),
     )
 
 
 def on_device(probes, wind, station_cell, obs_count, obs_weight):
     tiles, groups = lax.axis_size("space"), lax.axis_size("obs")
-    place = jnp.stack([lax.axis_index("space"), tiles, lax.axis_index("obs")])
-    place = place.reshape(1, 3).astype(jnp.int32)
     raw, patch, up, down = call(
         prepare_kernel,
-        [VM] * 4 + [SM] * 2,
+        [VM] * 4 + [SM],
         (
             shape(KINDS * LV * RX, NY),
             shape(NP * RX, LANES),
@@ -452,22 +468,27 @@
         station_cell,
         obs_weight,
         obs_count,
-        place,
     )
     low = lax.ppermute(up, "space", [(i, i + 1) for i in range(tiles - 1)])
     high = lax.ppermute(down, "space", [(i + 1, i) for i in range(tiles - 1)])
+    own = call(
+        own_kernel,
+        [VM],
+        shape(groups * KINDS * RX, LANES),
+        cost=pl.CostEstimate(flops=2000000, bytes_accessed=4000000, transcendentals=0),
+    )(raw)
     msg = call(
         message_kernel,
         [VM] * 3,
         shape(groups * KINDS * ROWS, LANES),
         (pltpu.VMEM((KINDS * LV, 2, 8, LANES), F32),),
-    )(raw, low, high)
+    )(own, low, high)
     got = lax.all_to_all(msg.reshape(groups, KINDS * ROWS, LANES), "obs", 0, 0, tiled=True)
     field = pltpu.VMEM((NP * ROWS, LANES), F32)
     padded = pltpu.VMEM((NP * ROWS + 2 * PAD, LANES), F32)
     share, msg = call(
         patch_kernel,
-        [VM] * 4 + [SM],
+        [VM] * 4,
         (shape(RX * NP, LANES), shape(groups * 8, 128)),
         (
             padded,
@@ -483,7 +504,7 @@
             pltpu.VMEM((NP * RX, LANES), F32),
             pltpu.VMEM((NP * RX, LANES), F32),
         ),
-    )(got.reshape(groups * KINDS * ROWS, LANES), patch, low, high, place)
+    )(got.reshape(groups * KINDS * ROWS, LANES), patch, low, high)
     got = lax.all_to_all(msg.reshape(groups, 8, 128), "obs", 0, 0, tiled=True)
     msg = call(sum_kernel, [VM], shape(tiles * 8, 128))(got.reshape(groups * 8, 128))
     got = lax.all_to_all(msg.reshape(tiles, 8, 128), "space", 0, 0, tiled=True)

time: 128 us -> 115 us (0.90)
  Pallas kernels: 35.2 us -> 23.2 us
  local copies, waits for them, and re-layouts: 0.67 us -> 3.89 us
  blocking collectives: 82.8 us -> 80 us
    pallas_call x2 -> x3, Pallas kernels: 23.3 us -> 19.4 us  [the longest x1 17.5 us: on_device(): call(patch_kernel, [VM] * 4, (shape(RX * NP, LANES), shape(groups * 8, 12...]
    unnamed x4 -> x8, local copies, waits for them, and re-layouts: 0.67 us -> 3.89 us
    pallas_call x1, Pallas kernels: 5.21 us -> 2.38 us  [on_device(): call(lambda *refs: basis_kernel(*refs, scale=scale), [VM] * 2, shape(grou...]
    pallas_call x1, Pallas kernels: 3.18 us -> 0.41 us  [on_device(): call(message_kernel, [VM] * 3, shape(groups * KINDS * ROWS, LANES), (pltp...]
    all_to_all x1, blocking collectives: 11.9 us -> 10.3 us  [on_device(): got = lax.all_to_all(msg.reshape(groups, 8, 128), 'obs', 0, 0, tiled=True)]
    pallas_call x1, Pallas kernels: 1.52 us -> 0.03 us  [on_device(): call(sum_kernel, [VM], shape(tiles * 8, 128))(got.reshape(groups * 8, 128))]
  transfers between devices with their start and end apart: 2 -> 2, of which waited for: 1 -> 1; matrix products, arithmetic and copies ran while one was open for 0% -> 0% of each run, Pallas kernels for 0% -> 1%
where the time goes in v4:
time: 115 us; the launch traced here: 114 us
  blocking collectives  80 us (70%)
  Pallas kernels  23.2 us (20%)
  local copies, waits for them, and re-layouts  3.89 us (3%)
  starting transfers between devices  3.04 us (3%)
  waiting for transfers between devices  2.91 us (3%)
  between operations  1.34 us (1%)
    all_to_all x1, blocking collectives, on_device(): got = lax.all_to_all(msg.reshape(tiles, 8, 128), 'space', 0, 0, tiled=True)  36.4 us
    all_to_all x1, blocking collectives, on_device(): lax.all_to_all(msg.reshape(groups, KINDS * ROWS, LANES), 'obs', 0, 0, til...  21.9 us
    pallas_call x1, Pallas kernels, on_device(): call(patch_kernel, [VM] * 4, (shape(RX * NP, LANES), shape(groups * 8, 12...  17.5 us
    all_to_all x1, blocking collectives, on_device(): lax.all_to_all(msg.reshape(groups, 24, LANES), 'obs', 0, 0, tiled=True)  11.5 us
    all_to_all x1, blocking collectives, on_device(): got = lax.all_to_all(msg.reshape(groups, 8, 128), 'obs', 0, 0, tiled=True)  10.3 us
    unnamed x8, local copies, waits for them, and re-layouts  3.89 us
    ppermute x1, waiting for transfers between devices, on_device(): high = lax.ppermute(down, 'space', [(i + 1, i) for i in range(tiles - 1)])  2.9 us
    pallas_call x1, Pallas kernels, on_device(): call(lambda *refs: basis_kernel(*refs, scale=scale), [VM] * 2, shape(grou...  2.38 us
  transfers between devices with their start and end apart: 2, of which 1 were waited for; matrix products, arithmetic and copies ran while one was open for 0% of the time, Pallas kernels for 1%

profile of v4, /device:TPU:2, one launch (start us, length us, event | category | flops | bytes accessed | tf_op | source)
XLA Modules:
  0.0 114.5 jit_solution(2745143171494647914)
XLA Ops:
  1.3 0.0 copy-start
  1.3 1.6 %copy-done = f32[32,4,16,256]{3,2,1,0:T(8,128)S(1)} copy-done((f32[32,4,16,256]{3,2,1,0:T(8,128)S(1)}, f32[32,4,16,256]{3,2,1,0:T(8,128)}, u32[]{:S(2)}) %copy-start) | copy-done | bytes 2097176
  2.9 0.0 copy-start.1
  2.9 0.9 copy-done.1
  3.8 0.0 copy-start.2
  3.8 0.7 copy-done.2
  4.5 0.0 copy-start.3
  4.5 0.7 copy-done.3
  5.2 1.2 %shard_map.68 = (f32[320,256]{1,0:T(8,128)S(1)}, f32[512,128]{1,0:T(8,128)S(1)}, f32[288,128]{1,0:T(8,128)S(1)}, f32[288,128]{1,0:T(8,128)S(1)}) custom-call(f32[2048,256]{1,0:T(8,128)S(1)} %bitcast.13, f32[256,256]{1,0:T(8,128)S(1)} %bitcast.18, s32[1,256]{1,0:T(1,128)S(1)} %copy-done.2, f32[1,256]{1,0:T(1,128)S(1)} %copy-done.3, s32[1,1]{1,0:T(1,128)S(6)} %copy.7.count), custom_call_target="tpu_custom_call" | custom-call | tf_op jit(solution)/shard_map/pallas_call | solution.py:456
  6.4 1.7 %collective-permute-start = (f32[288,128]{1,0:T(8,128)S(1)}, f32[288,128]{1,0:T(8,128)S(1)}, u32[]{:S(2)}, u32[]{:S(2)}) collective-permute-start(f32[288,128]{1,0:T(8,128)S(1)} %get-tuple-element.11), channel_id=1, source_target_pairs={{0,1},{1,2},{2,3},{3,4},{4,5},{5,6},{6,7},{7,8},{8,9},{9,10},{10,1... | collective-permute-start | bytes 442376 | tf_op jit(solution)/shard_map/ppermute | solution.py:472
  8.1 1.3 %collective-permute-start.1 = (f32[288,128]{1,0:T(8,128)S(1)}, f32[288,128]{1,0:T(8,128)S(1)}, u32[]{:S(2)}, u32[]{:S(2)}) collective-permute-start(f32[288,128]{1,0:T(8,128)S(1)} %get-tuple-element.12), channel_id=1, source_target_pairs={{1,0},{2,1},{3,2},{4,3},{5,4},{6,5},{7,6},{8,7},{9,8},{10,9},{11,1... | collective-permute-start | bytes 442376 | tf_op jit(solution)/shard_map/ppermute | solution.py:473
  9.4 0.7 shard_map.69.own
  10.2 0.0 collective-permute-done.low
  10.2 2.9 %collective-permute-done.1.high = f32[288,128]{1,0:T(8,128)S(1)} collective-permute-done((f32[288,128]{1,0:T(8,128)S(1)}, f32[288,128]{1,0:T(8,128)S(1)}, u32[]{:S(2)}, u32[]{:S(2)}) %collective-permute-start.1) | collective-permute-done | bytes 147488 | tf_op jit(solution)/shard_map/ppermute | solution.py:473
  13.1 0.4 shard_map.70
  13.5 21.9 %all_to_all.20 = f32[16,120,128]{2,1,0:T(8,128)S(1)} all-to-all(f32[16,120,128]{2,1,0:T(8,128)S(1)} %bitcast.12), channel_id=1, replica_groups=mesh['obs'=16,'space'=32] {'obs'}, dimensions={0} | all-to-all | bytes 1966080 | tf_op jit(solution)/shard_map/all_to_all | solution.py:486
  35.4 17.5 %shard_map.71 = (f32[512,128]{1,0:T(8,128)S(1)}, f32[128,128]{1,0:T(8,128)S(1)}) custom-call(f32[1920,128]{1,0:T(8,128)S(1)} %bitcast.11, f32[512,128]{1,0:T(8,128)S(1)} %get-tuple-element.13.patch, f32[288,128]{1,0:T(8,128)S(1)} %collective-permute-done.low, f32[288,128]{1,0:T(8,128)S(1)} %collective-permute-done.1.high), custom_call_target="tpu_custom_call" | custom-call | tf_op jit(solution)/shard_map/pallas_call | solution.py:489
  52.9 10.3 %all_to_all.21 = f32[16,8,128]{2,1,0:T(8,128)S(1)} all-to-all(f32[16,8,128]{2,1,0:T(8,128)S(1)} %bitcast.20), channel_id=1, replica_groups=mesh['obs'=16,'space'=32] {'obs'}, dimensions={0} | all-to-all | bytes 131072 | tf_op jit(solution)/shard_map/all_to_all | solution.py:508
  63.2 36.4 %all_to_all.22 = f32[32,8,128]{2,1,0:T(8,128)S(1)} all-to-all(f32[32,8,128]{2,1,0:T(8,128)S(1)} %bitcast.16), channel_id=1, replica_groups=mesh['obs'=16,'space'=32] {'space'}, dimensions={0} | all-to-all | bytes 262144 | tf_op jit(solution)/shard_map/all_to_all | solution.py:510
  99.6 2.4 %shard_map.73 = f32[384,128]{1,0:T(8,128)S(1)} custom-call(f32[256,128]{1,0:T(8,128)S(1)} %bitcast.17, f32[512,128]{1,0:T(8,128)S(1)} %get-tuple-element.15.refs_1_), custom_call_target="tpu_custom_call" | custom-call | tf_op jit(solution)/shard_map/pallas_call | solution.py:512
  102.0 11.5 %all_to_all.23 = f32[16,24,128]{2,1,0:T(8,128)S(1)} all-to-all(f32[16,24,128]{2,1,0:T(8,128)S(1)} %bitcast.15), channel_id=1, replica_groups=mesh['obs'=16,'space'=32] {'obs'}, dimensions={0} | all-to-all | bytes 393216 | tf_op jit(solution)/shard_map/all_to_all | solution.py:515
  113.5 1.0 shard_map.74
  (1 shorter events, 0.0 us)
Async XLA Ops:
  1.3 1.6 %copy-start = (f32[32,4,16,256]{3,2,1,0:T(8,128)S(1)}, f32[32,4,16,256]{3,2,1,0:T(8,128)}, u32[]{:S(2)}) copy-start(f32[32,4,16,256]{3,2,1,0:T(8,128)} %param.5) | copy-start | bytes 6291460
  2.9 0.9 copy-start.1
  3.8 0.7 copy-start.2
  4.5 0.7 copy-start.3
  6.4 3.8 %collective-permute-start = (f32[288,128]{1,0:T(8,128)S(1)}, f32[288,128]{1,0:T(8,128)S(1)}, u32[]{:S(2)}, u32[]{:S(2)}) collective-permute-start(f32[288,128]{1,0:T(8,128)S(1)} %get-tuple-element.11), channel_id=1, source_target_pairs={{0,1},{1,2},{2,3},{3,4},{4,5},{5,6},{6,7},{7,8},{8,9},{9,10},{10,1... | collective-permute-start | bytes 442376 | tf_op jit(solution)/shard_map/ppermute | solution.py:472
  8.1 5.0 %collective-permute-start.1 = (f32[288,128]{1,0:T(8,128)S(1)}, f32[288,128]{1,0:T(8,128)S(1)}, u32[]{:S(2)}, u32[]{:S(2)}) collective-permute-start(f32[288,128]{1,0:T(8,128)S(1)} %get-tuple-element.12), channel_id=1, source_target_pairs={{1,0},{2,1},{3,2},{4,3},{5,4},{6,5},{7,6},{8,7},{9,8},{10,9},{11,1... | collective-permute-start | bytes 442376 | tf_op jit(solution)/shard_map/ppermute | solution.py:473

commit v5 on v4

--- a/solution.py
+++ b/solution.py
@@ -25,6 +25,10 @@
 UNROLL = 4
 SLOT = ROWS + 2 * PAD
 KINDS = 5
+FIRST = (1, 1, 2, 2, 2)
+COUNT = tuple(ROWS - 2 * f for f in FIRST)
+START = tuple(sum(COUNT[:k]) for k in range(KINDS))
+TALL = sum(COUNT)
 SIDE = KINDS * LV * HALO
 MSG = 2 * SIDE + NP * HALO
 
@@ -77,13 +81,34 @@
     return jnp.where((col >= 0) & (col < NY), acc, 0.0)
 
 
-def prepare_kernel(probes, wind, cells, weight, count, raw, patch, up, down):
+def prepare_kernel(
+    probes_far, wind_far, cells_far, weight_far, count, raw, patch, up, down,
+    probes, wind, cells, weight, sems,
+):
+    copies = [
+        pltpu.make_async_copy(far, near, sems.at[i])
+        for i, (far, near) in enumerate(
+            (
+                (cells_far, cells),
+                (weight_far, weight),
+                (wind_far, wind),
+                (probes_far, probes),
+            )
+        )
+    ]
+    for copy in copies:
+        copy.start()
     first = lax.axis_index("obs") * OWN - MARGIN
+    copies[0].wait()
+    copies[1].wait()
+    copies[2].wait()
     for i in range(4 * LV):
         raw[pl.ds(i * RX, RX), :] = 0.5 * wind[pl.ds(i * RX, RX), :]
     raw[pl.ds(4 * LV * RX, LV * RX), :] = weight_map(
         cells[...].astype(F32), live_weights(weight, count)
     )
+
+    copies[3].wait()
 
     def one(p, _):
         for l in range(LV):
@@ -138,10 +163,10 @@
         tiles = [[edge[kind * LV + l, h] for h in range(2)] for l in range(LV)]
         for d in range(NY // OWN):
             value = window(tiles, d * OWN - MARGIN)
-            base = (d * KINDS + kind) * ROWS
-            msg[pl.ds(base, HALO), :] = value[:HALO]
-            msg[pl.ds(base + HALO, RX), :] = own[pl.ds((d * KINDS + kind) * RX, RX), :]
-            msg[pl.ds(base + HALO + RX, HALO), :] = value[HALO:]
+            base, n = d * TALL + START[kind], HALO - FIRST[kind]
+            msg[pl.ds(base, n), :] = value[HALO - n : HALO]
+            msg[pl.ds(base + n, RX), :] = own[pl.ds((d * KINDS + kind) * RX, RX), :]
+            msg[pl.ds(base + n + RX, n), :] = value[HALO : HALO + n]
 
 
 def all_blocks(t):
@@ -208,7 +233,8 @@
     for ref in (u, va, pa, qa):
         ref[pl.ds(0, PAD), :] = edge
         ref[pl.ds(PAD + NP * ROWS, PAD), :] = edge
-    for ref, n in ((cf, 2 * LV), (t1, UNROLL * LV), (t2, UNROLL * LV)):
+    cf[...] = jnp.zeros(cf.shape, F32)
+    for ref, n in ((t1, UNROLL * LV), (t2, UNROLL * LV)):
         for j in range(n):
             ref[pl.ds(j * SLOT, PAD), :] = edge
             ref[pl.ds(j * SLOT + PAD + ROWS, PAD), :] = edge
@@ -240,10 +266,11 @@
         return cf[pl.ds((j * LV + l) * SLOT + PAD + 8 * i + off, 8), :]
 
     def one_window(g, _):
-        base = g * (KINDS * ROWS)
-        for i in range(3):
-            for kind in range(KINDS):
-                tile = got[pl.ds(aligned(base + kind * ROWS + 8 * i), 8), :]
+        base = g * TALL
+        for kind in range(KINDS):
+            for off in (0, 8, COUNT[kind] - 8):
+                tile = got[pl.ds(base + START[kind] + off, 8), :]
+                row = PAD + FIRST[kind] + off
                 for l in range(LV):
                     m = jnp.take_along_axis(tile, l * WIN + lane % WIN, axis=1)
                     if kind in (2, 3):
@@ -252,7 +279,7 @@
                     else:
                         pair = (({0: 4, 1: 5, 4: 6}[kind], 0.1 * m if kind == 4 else m),)
                     for j, value in pair:
-                        cf[pl.ds((j * LV + l) * SLOT + PAD + 8 * i, 8), :] = value
+                        cf[pl.ds((j * LV + l) * SLOT + row, 8), :] = value
 
         def some(step, _):
             slots = range(UNROLL)
@@ -298,7 +325,7 @@
         lax.fori_loop(0, NP // GROUP // UNROLL, some, 0)
         return 0
 
-    lax.fori_loop(0, got.shape[0] // (KINDS * ROWS), one_window, 0)
+    lax.fori_loop(0, got.shape[0] // TALL, one_window, 0)
 
     def mask(f, _):
         for i in range(3):
@@ -311,6 +338,7 @@
     core_lane = (lane % WIN >= MARGIN) & (lane % WIN < MARGIN + OWN)
 
     def last(p, _):
+        tiles_of = []
         for i in range(2):
             at = [aligned(PAD + (p * LV + l) * ROWS + 8 * i) + HALO for l in range(LV)]
             c = [va[pl.ds(at[l], 8), :] for l in range(LV)]
@@ -324,21 +352,21 @@
                     right(q) - left(q)
                 )
                 done.append(jnp.where(core_lane, r, 0.0))
-            for ref, values in (
-                (s, swap_groups(done)),
-                (om, swap_groups([u[pl.ds(at[l], 8), :] for l in range(LV)])),
-            ):
-                for k in range(GROUP):
-                    ref[pl.ds(aligned((p * GROUP + k) * RX + 8 * i), 8), :] = values[k]
+            own = [jnp.where(core_lane, u[pl.ds(at[l], 8), :], 0.0) for l in range(LV)]
+            tiles_of.append((swap_groups(done), swap_groups(own)))
+        for n, ref in enumerate((s, om)):
+            for k in range(GROUP):
+                first, second = tiles_of[0][n][k], tiles_of[1][n][k]
+                ref[pl.ds(aligned((p * GROUP + k) * 8), 8), :] = first + pltpu.roll(second, OWN, 1)
         return 0
 
     lax.fori_loop(0, NP // GROUP, last, 0)
 
     both = jnp.zeros((2 * NP, NP), F32)
-    for x in range(RX):
-        sx = s[pl.ds(x, NP, stride=RX), :]
+    for x in range(8):
+        sx = s[pl.ds(x, NP, stride=8), :]
         share[pl.ds(x * NP, NP), :] = sx
-        rows = jnp.concatenate([sx, om[pl.ds(x, NP, stride=RX), :]], axis=0)
+        rows = jnp.concatenate([sx, om[pl.ds(x, NP, stride=8), :]], axis=0)
         both += product(rows, sx, ((1,), (1,)))
     spread = (iota((NP, LANES), 1) % NP == iota((NP, LANES), 0)).astype(F32)
     both = product(both, spread, ((1,), (0,)))
@@ -398,25 +426,24 @@
     r = iota((NP, NP), 0)
     pick = (iota((NP, NP), 1) == 2 * (r % 16) + r // 16).astype(F32)
     rows = product(pick, inverse, ((1,), (0,)))[:, :NP]
-    mine = (lane[:16] % WIN >= MARGIN) & (lane[:16] % WIN < MARGIN + OWN)
-    for x in range(RX):
+    for x in range(8):
         out = product(rows, share[pl.ds(x * NP, NP), :], ((1,), (0,)))
-        both = jnp.where(mine, out[:16], pltpu.roll(out[16:], OWN, 1))
-        msg[pl.ds(x, 16, stride=24), :] = both
+        for j in range(2):
+            msg[pl.ds(8 * j + x, 16, stride=24), :] = out[16 * j : 16 * j + 16]
     for d in range(16):
         msg[pl.ds(24 * d + 16, 8), :] = s
 
 
 def finish_kernel(got, basis, core, *, factor):
     lane = iota((8, 128), 1)
-    for xt in range(2):
+    for j in range(2):
         for h in range(2):
-            sources = [got[pl.ds(24 * (8 * h + d) + 8 * xt, 8), :] for d in range(8)]
-            for j in range(2):
+            sources = [got[pl.ds(24 * (8 * h + d) + 8 * j, 8), :] for d in range(8)]
+            for xt in range(2):
                 for l in range(LV):
                     acc = jnp.zeros((8, 128), F32)
                     for d in range(8):
-                        shift = (OWN * d - WIN * l - MARGIN - OWN * j) % LANES
+                        shift = (OWN * d - WIN * l - MARGIN - OWN * xt) % LANES
                         acc = jnp.where(lane // OWN == d, pltpu.roll(sources[d], shift, 1), acc)
                     basis[
                         pl.ds((j * LV + l) * RX + 8 * xt, 8), pl.ds(h * LANES, LANES)
@@ -438,7 +465,7 @@
     return jax.ShapeDtypeStruct(dims, F32)
 
 
-def call(kernel, specs, outs, scratch=(), cost=None):
+def call(kernel, specs, outs, scratch=(), cost=None, grant=24 << 20):
     many = isinstance(outs, tuple)
     return pl.pallas_call(
         kernel,
@@ -447,7 +474,9 @@
         out_specs=(VM,) * len(outs) if many else VM,
         scratch_shapes=list(scratch),
         cost_estimate=cost,
-        compiler_params=pltpu.CompilerParams(vmem_limit_bytes=24 << 20),
+        compiler_params=pltpu.CompilerParams(
+            vmem_limit_bytes=grant
+        ),
     )
 
 
@@ -455,13 +484,21 @@
     tiles, groups = lax.axis_size("space"), lax.axis_size("obs")
     raw, patch, up, down = call(
         prepare_kernel,
-        [VM] * 4 + [SM],
+        [pl.BlockSpec(memory_space=pltpu.HBM)] * 4 + [SM],
         (
             shape(KINDS * LV * RX, NY),
             shape(NP * RX, LANES),
             shape(MSG, LANES),
             shape(MSG, LANES),
         ),
+        (
+            pltpu.VMEM((NP * LV * RX, NY), F32),
+            pltpu.VMEM((4 * LV * RX, NY), F32),
+            pltpu.VMEM(station_cell.shape, jnp.int32),
+            pltpu.VMEM(obs_weight.shape, F32),
+            pltpu.SemaphoreType.DMA((4,)),
+        ),
+        grant=60 * 1024 * 1024,
     )(
         probes.reshape(NP * LV * RX, NY),
         wind.reshape(4 * LV * RX, NY),
@@ -480,16 +517,16 @@
     msg = call(
         message_kernel,
         [VM] * 3,
-        shape(groups * KINDS * ROWS, LANES),
+        shape(groups * TALL, LANES),
         (pltpu.VMEM((KINDS * LV, 2, 8, LANES), F32),),
     )(own, low, high)
-    got = lax.all_to_all(msg.reshape(groups, KINDS * ROWS, LANES), "obs", 0, 0, tiled=True)
+    got = lax.all_to_all(msg.reshape(groups, TALL, LANES), "obs", 0, 0, tiled=True)
     field = pltpu.VMEM((NP * ROWS, LANES), F32)
     padded = pltpu.VMEM((NP * ROWS + 2 * PAD, LANES), F32)
     share, msg = call(
         patch_kernel,
         [VM] * 4,
-        (shape(RX * NP, LANES), shape(groups * 8, 128)),
+        (shape(8 * NP, LANES), shape(groups * 8, 128)),
         (
             padded,
             field,
@@ -501,10 +538,10 @@
             padded,
             padded,
             padded,
-            pltpu.VMEM((NP * RX, LANES), F32),
-            pltpu.VMEM((NP * RX, LANES), F32),
+            pltpu.VMEM((NP * 8, LANES), F32),
+            pltpu.VMEM((NP * 8, LANES), F32),
         ),
-    )(got.reshape(groups * KINDS * ROWS, LANES), patch, low, high)
+    )(got.reshape(groups * TALL, LANES), patch, low, high)
     got = lax.all_to_all(msg.reshape(groups, 8, 128), "obs", 0, 0, tiled=True)
     msg = call(sum_kernel, [VM], shape(tiles * 8, 128))(got.reshape(groups * 8, 128))
     got = lax.all_to_all(msg.reshape(tiles, 8, 128), "space", 0, 0, tiled=True)

time: 115 us -> 112 us (0.974)
  local copies, waits for them, and re-layouts: 3.89 us -> 0.97 us
  Pallas kernels: 23.2 us -> 25.6 us
  blocking collectives: 80 us -> 78.4 us
    unnamed x8 -> x4, local copies, waits for them, and re-layouts: 3.89 us -> 0.97 us
    pallas_call x3, Pallas kernels: 19.1 us -> 21.7 us  [the longest x1 17.8 us: on_device(): call(patch_kernel, [VM] * 4, (shape(8 * NP, LANES), shape(groups * 8, 128...]
    all_to_all x1, blocking collectives: 21.9 us -> 20 us  [on_device(): lax.all_to_all(msg.reshape(groups, TALL, LANES), 'obs', 0, 0, tiled=True)]
where the time goes in v5:
time: 112 us; the launch traced here: 111 us
  blocking collectives  78.4 us (70%)
  Pallas kernels  25.6 us (23%)
  starting transfers between devices  3.04 us (3%)
  waiting for transfers between devices  2.14 us (2%)
  between operations  1.34 us (1%)
    all_to_all x1, blocking collectives, on_device(): got = lax.all_to_all(msg.reshape(tiles, 8, 128), 'space', 0, 0, tiled=True)  36.4 us
    all_to_all x1, blocking collectives, on_device(): lax.all_to_all(msg.reshape(groups, TALL, LANES), 'obs', 0, 0, tiled=True)  20 us
    pallas_call x1, Pallas kernels, on_device(): call(patch_kernel, [VM] * 4, (shape(8 * NP, LANES), shape(groups * 8, 128...  17.8 us
    all_to_all x1, blocking collectives, on_device(): lax.all_to_all(msg.reshape(groups, 24, LANES), 'obs', 0, 0, tiled=True)  11.5 us
    all_to_all x1, blocking collectives, on_device(): got = lax.all_to_all(msg.reshape(groups, 8, 128), 'obs', 0, 0, tiled=True)  10.5 us
    pallas_call x1, Pallas kernels, on_device(): call(prepare_kernel, [pl.BlockSpec(memory_space=pltpu.HBM)] * 4 + [SM], (...  3.48 us
  transfers between devices with their start and end apart: 2, of which 1 were waited for; matrix products, arithmetic and copies ran while one was open for 0% of the time, Pallas kernels for 1%

profile of v5, /device:TPU:2, one launch (start us, length us, event | category | flops | bytes accessed | tf_op | source)
XLA Modules:
  0.0 111.5 jit_solution(14419040957451557239)
XLA Ops:
  1.3 3.5 %shard_map.68 = (f32[320,256]{1,0:T(8,128)}, f32[512,128]{1,0:T(8,128)}, f32[288,128]{1,0:T(8,128)}, f32[288,128]{1,0:T(8,128)}) custom-call(f32[2048,256]{1,0:T(8,128)} %bitcast.19, f32[256,256]{1,0:T(8,128)} %bitcast.20, s32[1,256]{1,0:T(1,128)} %cells_far.1, f32[1,256]{1,0:T(1,128)} %weight_far.1, s32[1,1]{1,0:T(1,128)S(6)} %copy.7.count), custom_call_target="tpu_custom_call" | custom-call | tf_op jit(solution)/shard_map/pallas_call | solution.py:485
  4.8 1.7 %collective-permute-start = (f32[288,128]{1,0:T(8,128)}, f32[288,128]{1,0:T(8,128)S(1)}, u32[]{:S(2)}, u32[]{:S(2)}) collective-permute-start(f32[288,128]{1,0:T(8,128)} %get-tuple-element.11), channel_id=1, source_target_pairs={{0,1},{1,2},{2,3},{3,4},{4,5},{5,6},{6,7},{7,8},{8,9},{9,10},{10,1... | collective-permute-start | bytes 442376 | tf_op jit(solution)/shard_map/ppermute | solution.py:509
  6.5 1.3 %collective-permute-start.1 = (f32[288,128]{1,0:T(8,128)}, f32[288,128]{1,0:T(8,128)S(1)}, u32[]{:S(2)}, u32[]{:S(2)}) collective-permute-start(f32[288,128]{1,0:T(8,128)} %get-tuple-element.12), channel_id=1, source_target_pairs={{1,0},{2,1},{3,2},{4,3},{5,4},{6,5},{7,6},{8,7},{9,8},{10,9},{11,1... | collective-permute-start | bytes 442376 | tf_op jit(solution)/shard_map/ppermute | solution.py:510
  7.8 0.0 copy-start
  7.8 1.0 copy-done
  8.8 0.0 copy-start.1
  8.8 0.7 shard_map.69.own
  9.5 0.0 collective-permute-done.low
  9.5 2.1 %collective-permute-done.1.high = f32[288,128]{1,0:T(8,128)S(1)} collective-permute-done((f32[288,128]{1,0:T(8,128)}, f32[288,128]{1,0:T(8,128)S(1)}, u32[]{:S(2)}, u32[]{:S(2)}) %collective-permute-start.1) | collective-permute-done | bytes 147488 | tf_op jit(solution)/shard_map/ppermute | solution.py:510
  11.7 0.4 shard_map.70
  12.1 20.0 %all_to_all.20 = f32[16,104,128]{2,1,0:T(8,128)S(1)} all-to-all(f32[16,104,128]{2,1,0:T(8,128)S(1)} %bitcast.11), channel_id=1, replica_groups=mesh['obs'=16,'space'=32] {'obs'}, dimensions={0} | all-to-all | bytes 1703936 | tf_op jit(solution)/shard_map/all_to_all | solution.py:523
  32.1 0.0 copy-done.1
  32.1 17.8 %shard_map.71 = (f32[256,128]{1,0:T(8,128)S(1)}, f32[128,128]{1,0:T(8,128)S(1)}) custom-call(f32[1664,128]{1,0:T(8,128)S(1)} %bitcast.12, f32[512,128]{1,0:T(8,128)S(1)} %copy-done.1, f32[288,128]{1,0:T(8,128)S(1)} %collective-permute-done.low, f32[288,128]{1,0:T(8,128)S(1)} %collective-permute-done.1.high), custom_call_target="tpu_custom_call" | custom-call | tf_op jit(solution)/shard_map/pallas_call | solution.py:526
  49.9 10.5 %all_to_all.21 = f32[16,8,128]{2,1,0:T(8,128)S(1)} all-to-all(f32[16,8,128]{2,1,0:T(8,128)S(1)} %bitcast.18), channel_id=1, replica_groups=mesh['obs'=16,'space'=32] {'obs'}, dimensions={0} | all-to-all | bytes 131072 | tf_op jit(solution)/shard_map/all_to_all | solution.py:545
  60.5 36.4 %all_to_all.22 = f32[32,8,128]{2,1,0:T(8,128)S(1)} all-to-all(f32[32,8,128]{2,1,0:T(8,128)S(1)} %bitcast.16), channel_id=1, replica_groups=mesh['obs'=16,'space'=32] {'space'}, dimensions={0} | all-to-all | bytes 262144 | tf_op jit(solution)/shard_map/all_to_all | solution.py:547
  96.8 2.2 %shard_map.73 = f32[384,128]{1,0:T(8,128)S(1)} custom-call(f32[256,128]{1,0:T(8,128)S(1)} %bitcast.15, f32[256,128]{1,0:T(8,128)S(1)} %get-tuple-element.15.refs_1_), custom_call_target="tpu_custom_call" | custom-call | tf_op jit(solution)/shard_map/pallas_call | solution.py:549
  99.0 11.5 %all_to_all.23 = f32[16,24,128]{2,1,0:T(8,128)S(1)} all-to-all(f32[16,24,128]{2,1,0:T(8,128)S(1)} %bitcast.13), channel_id=1, replica_groups=mesh['obs'=16,'space'=32] {'obs'}, dimensions={0} | all-to-all | bytes 393216 | tf_op jit(solution)/shard_map/all_to_all | solution.py:552
  110.5 1.0 shard_map.74
  (1 shorter events, 0.0 us)
Async XLA Ops:
  4.8 4.8 %collective-permute-start = (f32[288,128]{1,0:T(8,128)}, f32[288,128]{1,0:T(8,128)S(1)}, u32[]{:S(2)}, u32[]{:S(2)}) collective-permute-start(f32[288,128]{1,0:T(8,128)} %get-tuple-element.11), channel_id=1, source_target_pairs={{0,1},{1,2},{2,3},{3,4},{4,5},{5,6},{6,7},{7,8},{8,9},{9,10},{10,1... | collective-permute-start | bytes 442376 | tf_op jit(solution)/shard_map/ppermute | solution.py:509
  6.5 5.2 %collective-permute-start.1 = (f32[288,128]{1,0:T(8,128)}, f32[288,128]{1,0:T(8,128)S(1)}, u32[]{:S(2)}, u32[]{:S(2)}) collective-permute-start(f32[288,128]{1,0:T(8,128)} %get-tuple-element.12), channel_id=1, source_target_pairs={{1,0},{2,1},{3,2},{4,3},{5,4},{6,5},{7,6},{8,7},{9,8},{10,9},{11,1... | collective-permute-start | bytes 442376 | tf_op jit(solution)/shard_map/ppermute | solution.py:510
  7.8 1.0 copy-start
  8.8 23.3 %copy-start.1 = (f32[512,128]{1,0:T(8,128)S(1)}, f32[512,128]{1,0:T(8,128)}, u32[]{:S(2)}) copy-start(f32[512,128]{1,0:T(8,128)} %get-tuple-element.13.patch) | copy-start | bytes 786436

commit v6 on v5

--- a/solution.py
+++ b/solution.py
@@ -22,13 +22,14 @@
 LANES = 128
 GROUP = LANES // WIN
 PAD = 8
-UNROLL = 4
+UNROLL = 8
 SLOT = ROWS + 2 * PAD
 KINDS = 5
 FIRST = (1, 1, 2, 2, 2)
 COUNT = tuple(ROWS - 2 * f for f in FIRST)
 START = tuple(sum(COUNT[:k]) for k in range(KINDS))
 TALL = sum(COUNT)
+CHUNK = NP * LV * RX // 4
 SIDE = KINDS * LV * HALO
 MSG = 2 * SIDE + NP * HALO
 
@@ -92,7 +93,10 @@
                 (cells_far, cells),
                 (weight_far, weight),
                 (wind_far, wind),
-                (probes_far, probes),
+                *(
+                    (probes_far.at[pl.ds(c * CHUNK, CHUNK), :], probes.at[pl.ds(c * CHUNK, CHUNK), :])
+                    for c in range(4)
+                ),
             )
         )
     ]
@@ -107,8 +111,6 @@
     raw[pl.ds(4 * LV * RX, LV * RX), :] = weight_map(
         cells[...].astype(F32), live_weights(weight, count)
     )
-
-    copies[3].wait()
 
     def one(p, _):
         for l in range(LV):
@@ -126,7 +128,9 @@
                 patch[pl.ds(aligned((p * LV + l) * RX + 8 * xt), 8), :] = window(tiles, first)
         return 0
 
-    lax.fori_loop(0, NP // GROUP, one, 0)
+    for c in range(4):
+        copies[3 + c].wait()
+        lax.fori_loop(2 * c, 2 * c + 2, one, 0)
     for out, start in ((up, RX - HALO), (down, 0)):
         for h in range(2):
             for i in range(KINDS * LV):
@@ -262,10 +266,10 @@
 
     lax.fori_loop(0, NP // GROUP, shared, 0)
 
-    def coef(j, l, i, off=0):
-        return cf[pl.ds((j * LV + l) * SLOT + PAD + 8 * i + off, 8), :]
-
-    def one_window(g, _):
+    def place(turn, j, l):
+        return ((turn * 7 + j) * LV + l) * SLOT
+
+    def expand(g, turn):
         base = g * TALL
         for kind in range(KINDS):
             for off in (0, 8, COUNT[kind] - 8):
@@ -279,7 +283,11 @@
                     else:
                         pair = (({0: 4, 1: 5, 4: 6}[kind], 0.1 * m if kind == 4 else m),)
                     for j, value in pair:
-                        cf[pl.ds((j * LV + l) * SLOT + row, 8), :] = value
+                        cf[pl.ds(place(turn, j, l) + row, 8), :] = value
+
+    def steps(turn):
+        def coef(j, l, i, off=0):
+            return cf[pl.ds(place(turn, j, l) + PAD + 8 * i + off, 8), :]
 
         def some(step, _):
             slots = range(UNROLL)
@@ -322,10 +330,22 @@
                         qa[here, :] += b * r
             return 0
 
-        lax.fori_loop(0, NP // GROUP // UNROLL, some, 0)
+        if UNROLL == NP // GROUP:
+            some(0, 0)
+        else:
+            lax.fori_loop(0, NP // GROUP // UNROLL, some, 0)
+
+    windows = got.shape[0] // TALL
+    expand(0, 0)
+
+    def two_windows(h, _):
+        expand(2 * h + 1, 1)
+        steps(0)
+        expand(jnp.minimum(2 * h + 2, windows - 1), 0)
+        steps(1)
         return 0
 
-    lax.fori_loop(0, got.shape[0] // TALL, one_window, 0)
+    lax.fori_loop(0, windows // 2, two_windows, 0)
 
     def mask(f, _):
         for i in range(3):
@@ -496,7 +516,7 @@
             pltpu.VMEM((4 * LV * RX, NY), F32),
             pltpu.VMEM(station_cell.shape, jnp.int32),
             pltpu.VMEM(obs_weight.shape, F32),
-            pltpu.SemaphoreType.DMA((4,)),
+            pltpu.SemaphoreType.DMA((7,)),
         ),
         grant=60 * 1024 * 1024,
     )(
@@ -532,7 +552,7 @@
             field,
             field,
             field,
-            pltpu.VMEM((7 * LV * SLOT, LANES), F32),
+            pltpu.VMEM((2 * 7 * LV * SLOT, LANES), F32),
             pltpu.VMEM((UNROLL * LV * SLOT, LANES), F32),
             pltpu.VMEM((UNROLL * LV * SLOT, LANES), F32),
             padded,

time: 112 us -> 110 us (0.982)
  Pallas kernels: 25.6 us -> 23.3 us
    pallas_call x1, Pallas kernels: 17.8 us -> 16 us  [on_device(): call(patch_kernel, [VM] * 4, (shape(8 * NP, LANES), shape(groups * 8, 128...]
where the time goes in v6:
time: 110 us; the launch traced here: 109 us
  blocking collectives  78.4 us (71%)
  Pallas kernels  23.3 us (21%)
  starting transfers between devices  3.04 us (3%)
  waiting for transfers between devices  2.14 us (2%)
  between operations  1.34 us (1%)
    all_to_all x1, blocking collectives, on_device(): got = lax.all_to_all(msg.reshape(tiles, 8, 128), 'space', 0, 0, tiled=True)  36.4 us
    all_to_all x1, blocking collectives, on_device(): lax.all_to_all(msg.reshape(groups, TALL, LANES), 'obs', 0, 0, tiled=True)  20 us
    pallas_call x1, Pallas kernels, on_device(): call(patch_kernel, [VM] * 4, (shape(8 * NP, LANES), shape(groups * 8, 128...  16 us
    all_to_all x1, blocking collectives, on_device(): lax.all_to_all(msg.reshape(groups, 24, LANES), 'obs', 0, 0, tiled=True)  11.5 us
    all_to_all x1, blocking collectives, on_device(): got = lax.all_to_all(msg.reshape(groups, 8, 128), 'obs', 0, 0, tiled=True)  10.5 us
    pallas_call x1, Pallas kernels, on_device(): call(prepare_kernel, [pl.BlockSpec(memory_space=pltpu.HBM)] * 4 + [SM], (...  3.03 us
  transfers between devices with their start and end apart: 2, of which 1 were waited for; matrix products, arithmetic and copies ran while one was open for 0% of the time, Pallas kernels for 1%

profile of v6, /device:TPU:2, one launch (start us, length us, event | category | flops | bytes accessed | tf_op | source)
XLA Modules:
  0.0 109.2 jit_solution(5420394936422265188)
XLA Ops:
  1.3 3.0 %shard_map.68 = (f32[320,256]{1,0:T(8,128)}, f32[512,128]{1,0:T(8,128)}, f32[288,128]{1,0:T(8,128)}, f32[288,128]{1,0:T(8,128)}) custom-call(f32[2048,256]{1,0:T(8,128)} %bitcast.19, f32[256,256]{1,0:T(8,128)} %bitcast.20, s32[1,256]{1,0:T(1,128)} %cells_far.1, f32[1,256]{1,0:T(1,128)} %weight_far.1, s32[1,1]{1,0:T(1,128)S(6)} %copy.7.count), custom_call_target="tpu_custom_call" | custom-call | tf_op jit(solution)/shard_map/pallas_call | solution.py:505
  4.3 1.7 %collective-permute-start = (f32[288,128]{1,0:T(8,128)}, f32[288,128]{1,0:T(8,128)S(1)}, u32[]{:S(2)}, u32[]{:S(2)}) collective-permute-start(f32[288,128]{1,0:T(8,128)} %get-tuple-element.11), channel_id=1, source_target_pairs={{0,1},{1,2},{2,3},{3,4},{4,5},{5,6},{6,7},{7,8},{8,9},{9,10},{10,1... | collective-permute-start | bytes 442376 | tf_op jit(solution)/shard_map/ppermute | solution.py:529
  6.1 1.3 %collective-permute-start.1 = (f32[288,128]{1,0:T(8,128)}, f32[288,128]{1,0:T(8,128)S(1)}, u32[]{:S(2)}, u32[]{:S(2)}) collective-permute-start(f32[288,128]{1,0:T(8,128)} %get-tuple-element.12), channel_id=1, source_target_pairs={{1,0},{2,1},{3,2},{4,3},{5,4},{6,5},{7,6},{8,7},{9,8},{10,9},{11,1... | collective-permute-start | bytes 442376 | tf_op jit(solution)/shard_map/ppermute | solution.py:530
  7.4 0.0 copy-start
  7.4 1.0 copy-done
  8.3 0.0 copy-start.1
  8.3 0.7 shard_map.69.own
  9.1 0.0 collective-permute-done.low
  9.1 2.1 %collective-permute-done.1.high = f32[288,128]{1,0:T(8,128)S(1)} collective-permute-done((f32[288,128]{1,0:T(8,128)}, f32[288,128]{1,0:T(8,128)S(1)}, u32[]{:S(2)}, u32[]{:S(2)}) %collective-permute-start.1) | collective-permute-done | bytes 147488 | tf_op jit(solution)/shard_map/ppermute | solution.py:530
  11.2 0.4 shard_map.70
  11.7 20.0 %all_to_all.20 = f32[16,104,128]{2,1,0:T(8,128)S(1)} all-to-all(f32[16,104,128]{2,1,0:T(8,128)S(1)} %bitcast.11), channel_id=1, replica_groups=mesh['obs'=16,'space'=32] {'obs'}, dimensions={0} | all-to-all | bytes 1703936 | tf_op jit(solution)/shard_map/all_to_all | solution.py:543
  31.7 0.0 copy-done.1
  31.7 16.0 %shard_map.71 = (f32[256,128]{1,0:T(8,128)S(1)}, f32[128,128]{1,0:T(8,128)S(1)}) custom-call(f32[1664,128]{1,0:T(8,128)S(1)} %bitcast.12, f32[512,128]{1,0:T(8,128)S(1)} %copy-done.1, f32[288,128]{1,0:T(8,128)S(1)} %collective-permute-done.low, f32[288,128]{1,0:T(8,128)S(1)} %collective-permute-done.1.high), custom_call_target="tpu_custom_call" | custom-call | tf_op jit(solution)/shard_map/pallas_call | solution.py:546
  47.6 10.5 %all_to_all.21 = f32[16,8,128]{2,1,0:T(8,128)S(1)} all-to-all(f32[16,8,128]{2,1,0:T(8,128)S(1)} %bitcast.18), channel_id=1, replica_groups=mesh['obs'=16,'space'=32] {'obs'}, dimensions={0} | all-to-all | bytes 131072 | tf_op jit(solution)/shard_map/all_to_all | solution.py:565
  58.2 36.4 %all_to_all.22 = f32[32,8,128]{2,1,0:T(8,128)S(1)} all-to-all(f32[32,8,128]{2,1,0:T(8,128)S(1)} %bitcast.16), channel_id=1, replica_groups=mesh['obs'=16,'space'=32] {'space'}, dimensions={0} | all-to-all | bytes 262144 | tf_op jit(solution)/shard_map/all_to_all | solution.py:567
  94.6 2.2 %shard_map.73 = f32[384,128]{1,0:T(8,128)S(1)} custom-call(f32[256,128]{1,0:T(8,128)S(1)} %bitcast.15, f32[256,128]{1,0:T(8,128)S(1)} %get-tuple-element.15.refs_1_), custom_call_target="tpu_custom_call" | custom-call | tf_op jit(solution)/shard_map/pallas_call | solution.py:569
  96.8 11.5 %all_to_all.23 = f32[16,24,128]{2,1,0:T(8,128)S(1)} all-to-all(f32[16,24,128]{2,1,0:T(8,128)S(1)} %bitcast.13), channel_id=1, replica_groups=mesh['obs'=16,'space'=32] {'obs'}, dimensions={0} | all-to-all | bytes 393216 | tf_op jit(solution)/shard_map/all_to_all | solution.py:572
  108.2 1.0 shard_map.74
  (1 shorter events, 0.0 us)
Async XLA Ops:
  4.3 4.8 %collective-permute-start = (f32[288,128]{1,0:T(8,128)}, f32[288,128]{1,0:T(8,128)S(1)}, u32[]{:S(2)}, u32[]{:S(2)}) collective-permute-start(f32[288,128]{1,0:T(8,128)} %get-tuple-element.11), channel_id=1, source_target_pairs={{0,1},{1,2},{2,3},{3,4},{4,5},{5,6},{6,7},{7,8},{8,9},{9,10},{10,1... | collective-permute-start | bytes 442376 | tf_op jit(solution)/shard_map/ppermute | solution.py:529
  6.1 5.2 %collective-permute-start.1 = (f32[288,128]{1,0:T(8,128)}, f32[288,128]{1,0:T(8,128)S(1)}, u32[]{:S(2)}, u32[]{:S(2)}) collective-permute-start(f32[288,128]{1,0:T(8,128)} %get-tuple-element.12), channel_id=1, source_target_pairs={{1,0},{2,1},{3,2},{4,3},{5,4},{6,5},{7,6},{8,7},{9,8},{10,9},{11,1... | collective-permute-start | bytes 442376 | tf_op jit(solution)/shard_map/ppermute | solution.py:530
  7.4 1.0 copy-start
  8.3 23.3 %copy-start.1 = (f32[512,128]{1,0:T(8,128)S(1)}, f32[512,128]{1,0:T(8,128)}, u32[]{:S(2)}) copy-start(f32[512,128]{1,0:T(8,128)} %get-tuple-element.13.patch) | copy-start | bytes 786436

commit v7 on v6

--- a/solution.py
+++ b/solution.py
@@ -5,9 +5,11 @@
 from jax import lax
 from jax.experimental import pallas as pl
 from jax.experimental.pallas import tpu as pltpu
+from jax.sharding import Mesh
 from jax.sharding import PartitionSpec as P
 
 F32 = jnp.float32
+SPACE = ("z", "core")
 HIGH = lax.Precision.HIGHEST
 VM = pl.BlockSpec(memory_space=pltpu.VMEM)
 SM = pl.BlockSpec(memory_space=pltpu.SMEM)
@@ -212,8 +214,8 @@
 def patch_kernel(
     got, patch, low, high, share, msg, u, au, dx, dy, cf, t1, t2, va, pa, qa, s, om
 ):
-    t, o = lax.axis_index("space"), lax.axis_index("obs")
-    tiles = lax.axis_size("space")
+    t, o = lax.axis_index(SPACE), lax.axis_index("obs")
+    tiles = lax.axis_size(SPACE)
     lane = iota((8, LANES), 1)
     col = o * OWN - MARGIN + lane % WIN
     inside = []
@@ -264,7 +266,7 @@
                     ref[pl.ds(at[l] + PAD, 8), :] = edge
         return 0
 
-    lax.fori_loop(0, NP // GROUP, shared, 0)
+    lax.fori_loop(0, NP // GROUP, shared, 0, unroll=2)
 
     def place(turn, j, l):
         return ((turn * 7 + j) * LV + l) * SLOT
@@ -380,7 +382,7 @@
                 ref[pl.ds(aligned((p * GROUP + k) * 8), 8), :] = first + pltpu.roll(second, OWN, 1)
         return 0
 
-    lax.fori_loop(0, NP // GROUP, last, 0)
+    lax.fori_loop(0, NP // GROUP, last, 0, unroll=2)
 
     both = jnp.zeros((2 * NP, NP), F32)
     for x in range(8):
@@ -402,7 +404,8 @@
         piece = jnp.where(lane < 32, src[16 * rb : 16 * rb + 8], src[16 * rb + 8 : 16 * rb + 16])
         value = jnp.where(spare, piece, packed)
         for i in range(4):
-            msg[pl.ds((4 * i + kind) * 8, 8), :] = value
+            for core in range(2):
+                msg[pl.ds((2 * (4 * i + kind) + core) * 8, 8), :] = value
 
 
 def sum_kernel(parts, msg):
@@ -501,7 +504,8 @@
 
 
 def on_device(probes, wind, station_cell, obs_count, obs_weight):
-    tiles, groups = lax.axis_size("space"), lax.axis_size("obs")
+    tiles, groups = lax.axis_size(SPACE), lax.axis_size("obs")
+    layers, plane = lax.axis_size("z"), 2 * groups
     raw, patch, up, down = call(
         prepare_kernel,
         [pl.BlockSpec(memory_space=pltpu.HBM)] * 4 + [SM],
@@ -526,8 +530,8 @@
         obs_weight,
         obs_count,
     )
-    low = lax.ppermute(up, "space", [(i, i + 1) for i in range(tiles - 1)])
-    high = lax.ppermute(down, "space", [(i + 1, i) for i in range(tiles - 1)])
+    low = lax.ppermute(up, SPACE, [(i, i + 1) for i in range(tiles - 1)])
+    high = lax.ppermute(down, SPACE, [(i + 1, i) for i in range(tiles - 1)])
     own = call(
         own_kernel,
         [VM],
@@ -546,7 +550,7 @@
     share, msg = call(
         patch_kernel,
         [VM] * 4,
-        (shape(8 * NP, LANES), shape(groups * 8, 128)),
+        (shape(8 * NP, LANES), shape(plane * 8, 128)),
         (
             padded,
             field,
@@ -562,13 +566,13 @@
             pltpu.VMEM((NP * 8, LANES), F32),
         ),
     )(got.reshape(groups * TALL, LANES), patch, low, high)
-    got = lax.all_to_all(msg.reshape(groups, 8, 128), "obs", 0, 0, tiled=True)
-    msg = call(sum_kernel, [VM], shape(tiles * 8, 128))(got.reshape(groups * 8, 128))
-    got = lax.all_to_all(msg.reshape(tiles, 8, 128), "space", 0, 0, tiled=True)
+    got = lax.all_to_all(msg.reshape(plane, 8, 128), ("obs", "core"), 0, 0, tiled=True)
+    msg = call(sum_kernel, [VM], shape(layers * 8, 128))(got.reshape(plane * 8, 128))
+    got = lax.all_to_all(msg.reshape(layers, 8, 128), "z", 0, 0, tiled=True)
     scale = math.sqrt(LV * RX * tiles * NY)
     msg = call(
         lambda *refs: basis_kernel(*refs, scale=scale), [VM] * 2, shape(groups * 24, LANES)
-    )(got.reshape(tiles * 8, 128), share)
+    )(got.reshape(layers * 8, 128), share)
     got = lax.all_to_all(msg.reshape(groups, 24, LANES), "obs", 0, 0, tiled=True)
     factor = 1.0 / (groups * tiles * station_cell.shape[1])
     basis, core = call(
@@ -580,14 +584,16 @@
 
 
 def solution(mesh):
+    groups, tiles = mesh.shape["obs"], mesh.shape["space"]
+    split = Mesh(mesh.devices.reshape(groups, tiles // 2, 2), ("obs", *SPACE))
     in_specs = (
-        P(None, None, "space", None),
-        P("obs", None, None, None, "space", None),
-        P("obs", "space"),
-        P("obs", "space"),
-        P("obs", "space"),
+        P(None, None, SPACE, None),
+        P("obs", None, None, None, SPACE, None),
+        P("obs", SPACE),
+        P("obs", SPACE),
+        P("obs", SPACE),
     )
-    out_specs = (P("obs", None, "space", None), P())
+    out_specs = (P("obs", None, SPACE, None), P())
     return jax.shard_map(
-        on_device, mesh=mesh, in_specs=in_specs, out_specs=out_specs, check_vma=False
+        on_device, mesh=split, in_specs=in_specs, out_specs=out_specs, check_vma=False
     )

time: 110 us -> 104 us (0.945)
  blocking collectives: 78.4 us -> 74.3 us
  Pallas kernels: 23.3 us -> 22 us
    all_to_all x2, blocking collectives: 46.9 us -> 43 us  [the longest x1 30.2 us: on_device(): got = lax.all_to_all(msg.reshape(layers, 8, 128), 'z', 0, 0, tiled=True)]
    pallas_call x2, Pallas kernels: 16 us -> 14.7 us  [the longest x1 14.7 us: on_device(): call(patch_kernel, [VM] * 4, (shape(8 * NP, LANES), shape(plane * 8, 128)...]
where the time goes in v7:
time: 104 us
  blocking collectives  74.3 us (71%)
  Pallas kernels  22 us (21%)
  starting transfers between devices  3.04 us (3%)
  waiting for transfers between devices  2.14 us (2%)
  between operations  1.34 us (1%)
    all_to_all x1, blocking collectives, on_device(): got = lax.all_to_all(msg.reshape(layers, 8, 128), 'z', 0, 0, tiled=True)  30.2 us
    all_to_all x1, blocking collectives, on_device(): lax.all_to_all(msg.reshape(groups, TALL, LANES), 'obs', 0, 0, tiled=True)  20 us
    pallas_call x1, Pallas kernels, on_device(): call(patch_kernel, [VM] * 4, (shape(8 * NP, LANES), shape(plane * 8, 128)...  14.7 us
    all_to_all x1, blocking collectives, on_device(): lax.all_to_all(msg.reshape(plane, 8, 128), ('obs', 'core'), 0, 0, tiled=T...  12.8 us
    all_to_all x1, blocking collectives, on_device(): lax.all_to_all(msg.reshape(groups, 24, LANES), 'obs', 0, 0, tiled=True)  11.3 us
    pallas_call x1, Pallas kernels, on_device(): call(prepare_kernel, [pl.BlockSpec(memory_space=pltpu.HBM)] * 4 + [SM], (...  3.03 us
    pallas_call x1, Pallas kernels, on_device(): call(lambda *refs: basis_kernel(*refs, scale=scale), [VM] * 2, shape(grou...  2.15 us
    ppermute x1, waiting for transfers between devices, on_device(): high = lax.ppermute(down, SPACE, [(i + 1, i) for i in range(tiles - 1)])  2.14 us
  transfers between devices with their start and end apart: 2, of which 1 were waited for; matrix products, arithmetic and copies ran while one was open for 0% of the time, Pallas kernels for 1%

profile of v7, /device:TPU:2, one launch (start us, length us, event | category | flops | bytes accessed | tf_op | source)
XLA Modules:
  0.0 103.8 jit_solution(6786925650312456663)
XLA Ops:
  1.3 3.0 %shard_map.68 = (f32[320,256]{1,0:T(8,128)}, f32[512,128]{1,0:T(8,128)}, f32[288,128]{1,0:T(8,128)}, f32[288,128]{1,0:T(8,128)}) custom-call(f32[2048,256]{1,0:T(8,128)} %bitcast.19, f32[256,256]{1,0:T(8,128)} %bitcast.20, s32[1,256]{1,0:T(1,128)} %cells_far.1, f32[1,256]{1,0:T(1,128)} %weight_far.1, s32[1,1]{1,0:T(1,128)S(6)} %copy.7.count), custom_call_target="tpu_custom_call" | custom-call | tf_op jit(solution)/shard_map/pallas_call | solution.py:509
  4.3 1.7 %collective-permute-start = (f32[288,128]{1,0:T(8,128)}, f32[288,128]{1,0:T(8,128)S(1)}, u32[]{:S(2)}, u32[]{:S(2)}) collective-permute-start(f32[288,128]{1,0:T(8,128)} %get-tuple-element.11), channel_id=1, source_target_pairs={{0,1},{1,2},{2,3},{3,4},{4,5},{5,6},{6,7},{7,8},{8,9},{9,10},{10,1... | collective-permute-start | bytes 442376 | tf_op jit(solution)/shard_map/ppermute | solution.py:533
  6.1 1.3 %collective-permute-start.1 = (f32[288,128]{1,0:T(8,128)}, f32[288,128]{1,0:T(8,128)S(1)}, u32[]{:S(2)}, u32[]{:S(2)}) collective-permute-start(f32[288,128]{1,0:T(8,128)} %get-tuple-element.12), channel_id=1, source_target_pairs={{1,0},{2,1},{3,2},{4,3},{5,4},{6,5},{7,6},{8,7},{9,8},{10,9},{11,1... | collective-permute-start | bytes 442376 | tf_op jit(solution)/shard_map/ppermute | solution.py:534
  7.4 0.0 copy-start
  7.4 1.0 copy-done
  8.3 0.0 copy-start.1
  8.3 0.7 shard_map.69.own
  9.1 0.0 collective-permute-done.low
  9.1 2.1 %collective-permute-done.1.high = f32[288,128]{1,0:T(8,128)S(1)} collective-permute-done((f32[288,128]{1,0:T(8,128)}, f32[288,128]{1,0:T(8,128)S(1)}, u32[]{:S(2)}, u32[]{:S(2)}) %collective-permute-start.1) | collective-permute-done | bytes 147488 | tf_op jit(solution)/shard_map/ppermute | solution.py:534
  11.2 0.4 shard_map.70
  11.7 20.0 %all_to_all.20 = f32[16,104,128]{2,1,0:T(8,128)S(1)} all-to-all(f32[16,104,128]{2,1,0:T(8,128)S(1)} %bitcast.11), channel_id=1, replica_groups=mesh['obs'=16,'z'=16,'core'=2] {'obs'}, dimensions={0} | all-to-all | bytes 1703936 | tf_op jit(solution)/shard_map/all_to_all | solution.py:547
  31.7 0.0 copy-done.1
  31.7 14.7 %shard_map.71 = (f32[256,128]{1,0:T(8,128)S(1)}, f32[256,128]{1,0:T(8,128)S(1)}) custom-call(f32[1664,128]{1,0:T(8,128)S(1)} %bitcast.12, f32[512,128]{1,0:T(8,128)S(1)} %copy-done.1, f32[288,128]{1,0:T(8,128)S(1)} %collective-permute-done.low, f32[288,128]{1,0:T(8,128)S(1)} %collective-permute-done.1.high), custom_call_target="tpu_custom_call" | custom-call | tf_op jit(solution)/shard_map/pallas_call | solution.py:550
  46.3 12.8 %all_to_all.21 = f32[32,8,128]{2,1,0:T(8,128)S(1)} all-to-all(f32[32,8,128]{2,1,0:T(8,128)S(1)} %bitcast.18), channel_id=1, replica_groups=mesh['obs'=16,'z'=16,'core'=2] {'obs','core'}, dimensions={0} | all-to-all | bytes 262144 | tf_op jit(solution)/shard_map/all_to_all | solution.py:569
  59.2 30.2 %all_to_all.22 = f32[16,8,128]{2,1,0:T(8,128)S(1)} all-to-all(f32[16,8,128]{2,1,0:T(8,128)S(1)} %bitcast.16), channel_id=1, replica_groups=mesh['obs'=16,'z'=16,'core'=2] {'z'}, dimensions={0} | all-to-all | bytes 131072 | tf_op jit(solution)/shard_map/all_to_all | solution.py:571
  89.4 2.2 %shard_map.73 = f32[384,128]{1,0:T(8,128)S(1)} custom-call(f32[128,128]{1,0:T(8,128)S(1)} %bitcast.17, f32[256,128]{1,0:T(8,128)S(1)} %get-tuple-element.15.refs_1_), custom_call_target="tpu_custom_call" | custom-call | tf_op jit(solution)/shard_map/pallas_call | solution.py:573
  91.5 11.3 %all_to_all.23 = f32[16,24,128]{2,1,0:T(8,128)S(1)} all-to-all(f32[16,24,128]{2,1,0:T(8,128)S(1)} %bitcast.14), channel_id=1, replica_groups=mesh['obs'=16,'z'=16,'core'=2] {'obs'}, dimensions={0} | all-to-all | bytes 393216 | tf_op jit(solution)/shard_map/all_to_all | solution.py:576
  102.8 1.0 shard_map.74
  (1 shorter events, 0.0 us)
Async XLA Ops:
  4.3 4.8 %collective-permute-start = (f32[288,128]{1,0:T(8,128)}, f32[288,128]{1,0:T(8,128)S(1)}, u32[]{:S(2)}, u32[]{:S(2)}) collective-permute-start(f32[288,128]{1,0:T(8,128)} %get-tuple-element.11), channel_id=1, source_target_pairs={{0,1},{1,2},{2,3},{3,4},{4,5},{5,6},{6,7},{7,8},{8,9},{9,10},{10,1... | collective-permute-start | bytes 442376 | tf_op jit(solution)/shard_map/ppermute | solution.py:533
  6.1 5.2 %collective-permute-start.1 = (f32[288,128]{1,0:T(8,128)}, f32[288,128]{1,0:T(8,128)S(1)}, u32[]{:S(2)}, u32[]{:S(2)}) collective-permute-start(f32[288,128]{1,0:T(8,128)} %get-tuple-element.12), channel_id=1, source_target_pairs={{1,0},{2,1},{3,2},{4,3},{5,4},{6,5},{7,6},{8,7},{9,8},{10,9},{11,1... | collective-permute-start | bytes 442376 | tf_op jit(solution)/shard_map/ppermute | solution.py:534
  7.4 1.0 copy-start
  8.3 23.3 %copy-start.1 = (f32[512,128]{1,0:T(8,128)S(1)}, f32[512,128]{1,0:T(8,128)}, u32[]{:S(2)}) copy-start(f32[512,128]{1,0:T(8,128)} %get-tuple-element.13.patch) | copy-start | bytes 786436

commit v8 on v7

--- a/solution.py
+++ b/solution.py
@@ -85,7 +85,7 @@
 
 
 def prepare_kernel(
-    probes_far, wind_far, cells_far, weight_far, count, raw, patch, up, down,
+    probes_far, wind_far, cells_far, weight_far, count, raw, patch, inner, outer,
     probes, wind, cells, weight, sems,
 ):
     copies = [
@@ -133,14 +133,22 @@
     for c in range(4):
         copies[3 + c].wait()
         lax.fori_loop(2 * c, 2 * c + 2, one, 0)
-    for out, start in ((up, RX - HALO), (down, 0)):
+    low_core = lax.axis_index("core") == 0
+
+    def either(ref, row, cols, for_inner):
+        top, bottom = ref[pl.ds(row + RX - HALO, HALO), cols], ref[pl.ds(row, HALO), cols]
+        return jnp.where(low_core == for_inner, top, bottom)
+
+    for out, for_inner in ((inner, True), (outer, False)):
         for h in range(2):
             for i in range(KINDS * LV):
-                out[pl.ds(h * SIDE + i * HALO, HALO), :] = raw[
-                    pl.ds(i * RX + start, HALO), pl.ds(h * LANES, LANES)
-                ]
+                out[pl.ds(h * SIDE + i * HALO, HALO), :] = either(
+                    raw, i * RX, pl.ds(h * LANES, LANES), for_inner
+                )
         for p in range(NP):
-            out[pl.ds(2 * SIDE + p * HALO, HALO), :] = patch[pl.ds(p * RX + start, HALO), :]
+            out[pl.ds(2 * SIDE + p * HALO, HALO), :] = either(
+                patch, p * RX, slice(None), for_inner
+            )
 
 
 def own_kernel(raw, own):
@@ -159,12 +167,14 @@
                 )
 
 
-def message_kernel(own, low, high, msg, edge):
+def message_kernel(own, inner, outer, msg, edge):
+    low_core = lax.axis_index("core") == 0
     for h in range(2):
         for i in range(KINDS * LV):
             src = pl.ds(h * SIDE + i * HALO, HALO)
-            edge[i, h, pl.ds(0, HALO), :] = low[src, :]
-            edge[i, h, pl.ds(HALO, HALO), :] = high[src, :]
+            near, far = inner[src, :], outer[src, :]
+            edge[i, h, pl.ds(0, HALO), :] = jnp.where(low_core, far, near)
+            edge[i, h, pl.ds(HALO, HALO), :] = jnp.where(low_core, near, far)
     for kind in range(KINDS):
         tiles = [[edge[kind * LV + l, h] for h in range(2)] for l in range(LV)]
         for d in range(NY // OWN):
@@ -212,10 +222,11 @@
 
 
 def patch_kernel(
-    got, patch, low, high, share, msg, u, au, dx, dy, cf, t1, t2, va, pa, qa, s, om
+    got, patch, inner, outer, share, msg, u, au, dx, dy, cf, t1, t2, va, pa, qa, s, om
 ):
     t, o = lax.axis_index(SPACE), lax.axis_index("obs")
     tiles = lax.axis_size(SPACE)
+    low_core = lax.axis_index("core") == 0
     lane = iota((8, LANES), 1)
     col = o * OWN - MARGIN + lane % WIN
     inside = []
@@ -246,9 +257,11 @@
             ref[pl.ds(j * SLOT + PAD + ROWS, PAD), :] = edge
     for f in range(NP):
         base = PAD + f * ROWS
-        u[pl.ds(base, HALO), :] = low[pl.ds(2 * SIDE + f * HALO, HALO), :]
+        src = pl.ds(2 * SIDE + f * HALO, HALO)
+        near, far = inner[src, :], outer[src, :]
+        u[pl.ds(base, HALO), :] = jnp.where(low_core, far, near)
         u[pl.ds(base + HALO, RX), :] = patch[pl.ds(f * RX, RX), :]
-        u[pl.ds(base + HALO + RX, HALO), :] = high[pl.ds(2 * SIDE + f * HALO, HALO), :]
+        u[pl.ds(base + HALO + RX, HALO), :] = jnp.where(low_core, near, far)
 
     def shared(p, _):
         for i in range(3):
@@ -506,7 +519,7 @@
 def on_device(probes, wind, station_cell, obs_count, obs_weight):
     tiles, groups = lax.axis_size(SPACE), lax.axis_size("obs")
     layers, plane = lax.axis_size("z"), 2 * groups
-    raw, patch, up, down = call(
+    raw, patch, inner, outer = call(
         prepare_kernel,
         [pl.BlockSpec(memory_space=pltpu.HBM)] * 4 + [SM],
         (
@@ -530,8 +543,9 @@
         obs_weight,
         obs_count,
     )
-    low = lax.ppermute(up, SPACE, [(i, i + 1) for i in range(tiles - 1)])
-    high = lax.ppermute(down, SPACE, [(i + 1, i) for i in range(tiles - 1)])
+    inner = lax.ppermute(inner, SPACE, [(i, i ^ 1) for i in range(tiles)])
+    across = [(i, i + 1) for i in range(1, tiles - 1, 2)]
+    outer = lax.ppermute(outer, SPACE, across + [(b, a) for a, b in across])
     own = call(
         own_kernel,
         [VM],
@@ -543,7 +557,7 @@
         [VM] * 3,
         shape(groups * TALL, LANES),
         (pltpu.VMEM((KINDS * LV, 2, 8, LANES), F32),),
-    )(own, low, high)
+    )(own, inner, outer)
     got = lax.all_to_all(msg.reshape(groups, TALL, LANES), "obs", 0, 0, tiled=True)
     field = pltpu.VMEM((NP * ROWS, LANES), F32)
     padded = pltpu.VMEM((NP * ROWS + 2 * PAD, LANES), F32)
@@ -565,7 +579,7 @@
             pltpu.VMEM((NP * 8, LANES), F32),
             pltpu.VMEM((NP * 8, LANES), F32),
         ),
-    )(got.reshape(groups * TALL, LANES), patch, low, high)
+    )(got.reshape(groups * TALL, LANES), patch, inner, outer)
     got = lax.all_to_all(msg.reshape(plane, 8, 128), ("obs", "core"), 0, 0, tiled=True)
     msg = call(sum_kernel, [VM], shape(layers * 8, 128))(got.reshape(plane * 8, 128))
     got = lax.all_to_all(msg.reshape(layers, 8, 128), "z", 0, 0, tiled=True)

time: 104 us -> 104 us (level)
  blocking collectives: 74.3 us -> 76.5 us
  waiting for transfers between devices: 2.14 us -> 0.01 us
    ppermute x2, waiting for transfers between devices: 2.14 us -> 0.01 us  [the longest x1 0.01 us: on_device(): inner = lax.ppermute(inner, SPACE, [(i, i ^ 1) for i in range(tiles)])]
    all_to_all x1, blocking collectives: 30.2 us -> 31.3 us  [on_device(): got = lax.all_to_all(msg.reshape(layers, 8, 128), 'z', 0, 0, tiled=True)]
  transfers between devices with their start and end apart: 2 -> 2, of which waited for: 1 -> 0; matrix products, arithmetic and copies ran while one was open for 0% -> 0% of each run, Pallas kernels for 1% -> 1%
where the time goes in v8:
time: 104 us
  blocking collectives  76.5 us (74%)
  Pallas kernels  22.1 us (21%)
  starting transfers between devices  2.59 us (2%)
  between operations  1.35 us (1%)
    all_to_all x1, blocking collectives, on_device(): got = lax.all_to_all(msg.reshape(layers, 8, 128), 'z', 0, 0, tiled=True)  31.3 us
    all_to_all x1, blocking collectives, on_device(): lax.all_to_all(msg.reshape(groups, TALL, LANES), 'obs', 0, 0, tiled=True)  20.1 us
    pallas_call x1, Pallas kernels, on_device(): call(patch_kernel, [VM] * 4, (shape(8 * NP, LANES), shape(plane * 8, 128)...  14.7 us
    all_to_all x1, blocking collectives, on_device(): lax.all_to_all(msg.reshape(plane, 8, 128), ('obs', 'core'), 0, 0, tiled=T...  13.8 us
    all_to_all x1, blocking collectives, on_device(): lax.all_to_all(msg.reshape(groups, 24, LANES), 'obs', 0, 0, tiled=True)  11.3 us
    pallas_call x1, Pallas kernels, on_device(): call(prepare_kernel, [pl.BlockSpec(memory_space=pltpu.HBM)] * 4 + [SM], (...  3.1 us
    pallas_call x1, Pallas kernels, on_device(): call(lambda *refs: basis_kernel(*refs, scale=scale), [VM] * 2, shape(grou...  2.15 us
  transfers between devices with their start and end apart: 2, of which 0 were waited for; matrix products, arithmetic and copies ran while one was open for 0% of the time, Pallas kernels for 1%

profile of v8, /device:TPU:2, one launch (start us, length us, event | category | flops | bytes accessed | tf_op | source)
XLA Modules:
  0.0 103.6 jit_solution(13446295511091247269)
XLA Ops:
  1.3 3.1 %shard_map.68 = (f32[320,256]{1,0:T(8,128)}, f32[512,128]{1,0:T(8,128)}, f32[288,128]{1,0:T(8,128)}, f32[288,128]{1,0:T(8,128)}) custom-call(f32[2048,256]{1,0:T(8,128)} %bitcast.19, f32[256,256]{1,0:T(8,128)} %bitcast.20, s32[1,256]{1,0:T(1,128)} %cells_far.1, f32[1,256]{1,0:T(1,128)} %weight_far.1, s32[1,1]{1,0:T(1,128)S(6)} %copy.7.count), custom_call_target="tpu_custom_call" | custom-call | tf_op jit(solution)/shard_map/pallas_call | solution.py:522
  4.4 1.9 %collective-permute-start = (f32[288,128]{1,0:T(8,128)}, f32[288,128]{1,0:T(8,128)S(1)}, u32[]{:S(2)}, u32[]{:S(2)}) collective-permute-start(f32[288,128]{1,0:T(8,128)} %get-tuple-element.11), channel_id=1, source_target_pairs={{0,1},{1,0},{2,3},{3,2},{4,5},{5,4},{6,7},{7,6},{8,9},{9,8},{10,11... | collective-permute-start | bytes 442376 | tf_op jit(solution)/shard_map/ppermute | solution.py:546
  6.3 0.7 collective-permute-start.1
  7.0 0.0 copy-start
  7.0 1.0 copy-done
  8.0 0.0 copy-start.1
  8.0 0.7 shard_map.69.own
  8.7 0.0 collective-permute-done.inner
  8.7 0.0 collective-permute-done.1.outer
  8.7 0.4 shard_map.70
  9.2 20.1 %all_to_all.20 = f32[16,104,128]{2,1,0:T(8,128)S(1)} all-to-all(f32[16,104,128]{2,1,0:T(8,128)S(1)} %bitcast.11), channel_id=1, replica_groups=mesh['obs'=16,'z'=16,'core'=2] {'obs'}, dimensions={0} | all-to-all | bytes 1703936 | tf_op jit(solution)/shard_map/all_to_all | solution.py:561
  29.3 0.0 copy-done.1
  29.3 14.7 %shard_map.71 = (f32[256,128]{1,0:T(8,128)S(1)}, f32[256,128]{1,0:T(8,128)S(1)}) custom-call(f32[1664,128]{1,0:T(8,128)S(1)} %bitcast.12, f32[512,128]{1,0:T(8,128)S(1)} %copy-done.1, f32[288,128]{1,0:T(8,128)S(1)} %collective-permute-done.inner, f32[288,128]{1,0:T(8,128)S(1)} %collective-permute-done.1.outer), custom_call_target="tpu_custom_call" | custom-call | tf_op jit(solution)/shard_map/pallas_call | solution.py:564
  44.0 13.8 %all_to_all.21 = f32[32,8,128]{2,1,0:T(8,128)S(1)} all-to-all(f32[32,8,128]{2,1,0:T(8,128)S(1)} %bitcast.18), channel_id=1, replica_groups=mesh['obs'=16,'z'=16,'core'=2] {'obs','core'}, dimensions={0} | all-to-all | bytes 262144 | tf_op jit(solution)/shard_map/all_to_all | solution.py:583
  57.8 31.3 %all_to_all.22 = f32[16,8,128]{2,1,0:T(8,128)S(1)} all-to-all(f32[16,8,128]{2,1,0:T(8,128)S(1)} %bitcast.16), channel_id=1, replica_groups=mesh['obs'=16,'z'=16,'core'=2] {'z'}, dimensions={0} | all-to-all | bytes 131072 | tf_op jit(solution)/shard_map/all_to_all | solution.py:585
  89.1 2.1 %shard_map.73 = f32[384,128]{1,0:T(8,128)S(1)} custom-call(f32[128,128]{1,0:T(8,128)S(1)} %bitcast.17, f32[256,128]{1,0:T(8,128)S(1)} %get-tuple-element.15.refs_1_), custom_call_target="tpu_custom_call" | custom-call | tf_op jit(solution)/shard_map/pallas_call | solution.py:587
  91.2 11.3 %all_to_all.23 = f32[16,24,128]{2,1,0:T(8,128)S(1)} all-to-all(f32[16,24,128]{2,1,0:T(8,128)S(1)} %bitcast.14), channel_id=1, replica_groups=mesh['obs'=16,'z'=16,'core'=2] {'obs'}, dimensions={0} | all-to-all | bytes 393216 | tf_op jit(solution)/shard_map/all_to_all | solution.py:590
  102.6 1.0 shard_map.74
  (1 shorter events, 0.0 us)
Async XLA Ops:
  4.4 4.3 %collective-permute-start = (f32[288,128]{1,0:T(8,128)}, f32[288,128]{1,0:T(8,128)S(1)}, u32[]{:S(2)}, u32[]{:S(2)}) collective-permute-start(f32[288,128]{1,0:T(8,128)} %get-tuple-element.11), channel_id=1, source_target_pairs={{0,1},{1,0},{2,3},{3,2},{4,5},{5,4},{6,7},{7,6},{8,9},{9,8},{10,11... | collective-permute-start | bytes 442376 | tf_op jit(solution)/shard_map/ppermute | solution.py:546
  6.3 2.4 %collective-permute-start.1 = (f32[288,128]{1,0:T(8,128)}, f32[288,128]{1,0:T(8,128)S(1)}, u32[]{:S(2)}, u32[]{:S(2)}) collective-permute-start(f32[288,128]{1,0:T(8,128)} %get-tuple-element.12), channel_id=1, source_target_pairs={{1,2},{3,4},{5,6},{7,8},{9,10},{11,12},{13,14},{15,16},{17,18},{19... | collective-permute-start | bytes 442376 | tf_op jit(solution)/shard_map/ppermute | solution.py:548
  7.0 1.0 copy-start
  8.0 21.3 %copy-start.1 = (f32[512,128]{1,0:T(8,128)S(1)}, f32[512,128]{1,0:T(8,128)}, u32[]{:S(2)}) copy-start(f32[512,128]{1,0:T(8,128)} %get-tuple-element.13.patch) | copy-start | bytes 786436
